TPU v7x, 256 devices: a whole 4x4x8 slice. The times are simulated.
256 devices in a mesh: seq: 8 (over x, y_hi), dp: 32 (over y_lo, z, core).
Axes of the slice: x: 4, y: 4 (y_hi: 2, y_lo: 2; y = y_hi * 2 + y_lo), z: 8, core: 2. Of those that a mesh axis runs over, the one named last changes fastest.
Arguments:
- frames: bfloat16 [64, 1024, 3072], P('dp', 'seq'), may hold values from -6 to 6
- proj_weight: bfloat16 [3072, 4608], P('dp'), may hold values from -0.109375 to 0.109375
- rate_weight: bfloat16 [3072, 24], replicated, may hold values from -0.109375 to 0.109375
- rate_bias: float32 [24], replicated, may hold values from -2 to 1
- init_weights: float32 [2, 24, 64, 256], replicated, may hold values from -0.75 to 0.75
- init_bias_hidden: float32 [24, 256], replicated, may hold values from -3 to 3
- init_bias_out: float32 [24, 64], replicated, may hold values from -3 to 3
- out_gain: float32 [1536], replicated, may hold values from 0.5 to 1.5
Outputs:
- ttt_output: bfloat16 [64, 1024, 1536], P('dp', 'seq')
All inputs are finite; a program needn't handle non-finite values.
Results may differ from a plain program's by a relative error of at most 0.0091.
Values may be sent and summed in bfloat16 or wider, within the bound.
No kernel may reach another device: no remote copies, remote signals or barrier semaphores. Data moves between devices by JAX's collectives and lax.ppermute only.
A program may use at most 128 MiB of HBM per device.

v0:
```python
import math

import jax
import jax.numpy as jnp
from jax import lax
from jax.sharding import PartitionSpec as P

MB = 64


precise = lax.Precision.HIGHEST
coefficient = 0.044715
root_scale = math.sqrt(2.0 / math.pi)


def shortened(x):
    return jax.tree.map(lambda a: a.astype(jnp.bfloat16) if a.dtype == jnp.float32 else a, x)


def shifted(block, axis, distance):
    devices = range(lax.axis_size(axis))
    route = [(i - distance, i) for i in devices if i - distance in devices]
    return lax.ppermute(block, axis, route)


def gelu_pair(z_value):
    tanh_part = jnp.tanh(root_scale * (z_value + coefficient * z_value * z_value * z_value))
    result = 0.5 * z_value * (1.0 + tanh_part)
    derivative = 0.5 * (1.0 + tanh_part) + 0.5 * z_value * (
        1.0 - tanh_part * tanh_part
    ) * root_scale * (1.0 + 3.0 * coefficient * z_value * z_value)
    return (result, derivative)


def minibatch(carried, inputs):
    pair, bias_hidden, bias_out = carried
    queries, key_rows, values, step_rate = inputs
    w_first = pair[0]
    w_second = pair[1]
    block_len = queries.shape[1]
    causal = jnp.tril(jnp.ones((block_len, block_len), dtype=bool))
    z_first = (
        jnp.einsum("hbd,hdf->hbf", key_rows, w_first, precision=precise) + bias_hidden[:, None, :]
    )
    hidden, derivative = gelu_pair(z_first)
    z_second = (
        jnp.einsum("hbf,hdf->hbd", hidden, w_second, precision=precise) + bias_out[:, None, :]
    )
    grad_second = z_second - (values - key_rows)
    grad_first = jnp.einsum("hbd,hdf->hbf", grad_second, w_second, precision=precise) * derivative
    scores_first = jnp.einsum("htd,hsd->hts", queries, key_rows, precision=precise) + 1.0
    mix_first = jnp.where(causal[None], scores_first * step_rate[:, None, :], 0.0)
    zq_first = (
        jnp.einsum("htd,hdf->htf", queries, w_first, precision=precise) + bias_hidden[:, None, :]
    )
    zq_first = zq_first - jnp.einsum("hts,hsf->htf", mix_first, grad_first, precision=precise)
    hidden_query, unused = gelu_pair(zq_first)
    scores_second = jnp.einsum("htf,hsf->hts", hidden_query, hidden, precision=precise) + 1.0
    mix_second = jnp.where(causal[None], scores_second * step_rate[:, None, :], 0.0)
    zq_second = (
        jnp.einsum("htf,hdf->htd", hidden_query, w_second, precision=precise) + bias_out[:, None, :]
    )
    zq_second = zq_second - jnp.einsum("hts,hsd->htd", mix_second, grad_second, precision=precise)
    scaled_first = grad_first * step_rate[:, :, None]
    scaled_second = grad_second * step_rate[:, :, None]
    new_first = w_first - jnp.einsum("hbd,hbf->hdf", key_rows, scaled_first, precision=precise)
    new_second = w_second - jnp.einsum("hbd,hbf->hdf", scaled_second, hidden, precision=precise)
    new_pair = jnp.stack([new_first, new_second])
    new_hidden = bias_hidden - jnp.sum(scaled_first, axis=1)
    new_out = bias_out - jnp.sum(scaled_second, axis=1)
    return ((new_pair, new_hidden, new_out), queries + zq_second)


def run_slab(start_state, column_block, rate_block, gain_rows):
    slab_len = column_block.shape[0]
    group_heads = column_block.shape[2]
    head_size = column_block.shape[3]
    batches = slab_len // MB
    inputs = (
        column_block.astype(jnp.float32)
        .reshape(batches, MB, 3, group_heads, head_size)
        .transpose(2, 0, 3, 1, 4)
    )
    step_rate = rate_block.reshape(batches, MB, group_heads).transpose(0, 2, 1)
    final_state, results = lax.scan(
        minibatch, start_state, (inputs[0], inputs[1], inputs[2], step_rate)
    )
    results = results.transpose(0, 2, 1, 3).reshape(slab_len, group_heads, head_size)
    normed = (
        results * lax.rsqrt(jnp.mean(results * results, axis=-1, keepdims=True) + 1e-06) * gain_rows
    )
    return (final_state, normed.reshape(slab_len, group_heads * head_size).astype(jnp.bfloat16))


def on_device(
    frames,
    proj_weight,
    rate_weight,
    rate_bias,
    init_weights,
    init_bias_hidden,
    init_bias_out,
    out_gain,
):
    clip_count, slab_len, model_width = frames.shape
    head_count = rate_weight.shape[1]
    head_size = init_weights.shape[2]
    inner_width = init_weights.shape[3]
    token_rows = frames.reshape(clip_count * slab_len, model_width)
    full_weight = lax.all_gather(proj_weight, "dp", axis=0, tiled=True)
    projected = jnp.dot(token_rows, full_weight, preferred_element_type=jnp.float32)
    projected = projected.astype(jnp.bfloat16).reshape(
        clip_count, slab_len, 3, head_count, head_size
    )
    rates = jax.nn.sigmoid(
        jnp.dot(token_rows, rate_weight, preferred_element_type=jnp.float32) + rate_bias
    ) / (MB * (head_size + inner_width))
    rates = rates.reshape(clip_count, slab_len, head_count)
    gain_all = out_gain.reshape(head_count, head_size)
    length = lax.axis_size("seq")
    position = lax.axis_index("seq")
    turns = clip_count + length - 1
    received_start = (
        jnp.zeros((2, head_count, head_size, inner_width), jnp.bfloat16),
        jnp.zeros((head_count, inner_width), jnp.bfloat16),
        jnp.zeros((head_count, head_size), jnp.bfloat16),
    )
    outputs_start = jnp.zeros((clip_count, slab_len, head_count * head_size), jnp.bfloat16)
    own_state = (init_weights, init_bias_hidden, init_bias_out)

    def one_turn(turn_index, carry):
        received, outputs = carry
        unit_index = turn_index - position
        active = (unit_index >= 0) & (unit_index < clip_count)
        clip_index = jnp.clip(unit_index, 0, clip_count - 1)
        start_state = jax.tree.map(
            lambda member, other: jnp.where(position == 0, member, other.astype(jnp.float32)),
            own_state,
            received,
        )

        def run_unit(operands):
            entry_state, current = operands
            clip_block = lax.dynamic_index_in_dim(projected, clip_index, 0, keepdims=False)
            rate_block = lax.dynamic_index_in_dim(rates, clip_index, 0, keepdims=False)
            final_state, result = run_slab(entry_state, clip_block, rate_block, gain_all)
            current = lax.dynamic_update_slice(
                current, result[None], (clip_index, jnp.int32(0), jnp.int32(0))
            )
            return (jax.tree.map(lambda member: member.astype(jnp.bfloat16), final_state), current)

        def pass_through(operands):
            entry_state, current = operands
            return (jax.tree.map(lambda member: member.astype(jnp.bfloat16), entry_state), current)

        sent, outputs = lax.cond(active, run_unit, pass_through, (start_state, outputs))
        received = jax.tree.map(
            lambda part, own: part.astype(own.dtype), shifted(shortened(sent), "seq", 1), sent
        )
        return (received, outputs)

    unused, outputs = lax.fori_loop(0, turns, one_turn, (received_start, outputs_start))
    return outputs


def solution(mesh):
    return jax.shard_map(
        on_device,
        mesh=mesh,
        in_specs=(P("dp", "seq", None), P("dp", None), P(), P(), P(), P(), P(), P()),
        out_specs=P("dp", "seq", None),
        check_vma=False,
    )
```

profile of v0, /device:TPU:30, one launch (start us, length us, event | category | flops | bytes accessed | tf_op | source)
XLA Modules:
  0.0 1591.7 jit_solution(12472045964157043991)
XLA Ops:
  9.4 160.1 %all-gather.2.cloned.1.call-done = bf16[3072,4608]{1,0:T(8,128)(2,1)} async-done(((bf16[96,4608]{1,0:T(8,128)(2,1)}), bf16[3072,4608]{1,0:T(8,128)(2,1)}) %all-gather.2.cloned.1.call-update) | async-done | bytes 28311568 | tf_op jit(solution)/shard_map/all_gather | solution.py:110
  169.5 14.4 convolution_convert_fusion
  183.9 6.9 reshape.105
  190.9 6.4 copy.44
  199.6 1382.8 %while.36 = (s32[]{:T(128)}, bf16[2,24,64,256]{3,2,1,0:T(8,128)(2,1)}, bf16[24,256]{1,0:T(8,128)(2,1)S(1)}, bf16[24,64]{1,0:T(8,128)(2,1)S(1)}, bf16[2,128,1536]...) while((s32[]{:T(128)}, ...), condition=%wide.region_8.9_spmd, body=%wide.region_0.8_spmd.sunk | while | flops 2897933824 | bytes 141774256 | solution.py:162
  207.1 36.6 %collective-permute-done.2 = bf16[24,64]{1,0:T(8,128)(2,1)S(1)} collective-permute-done((bf16[24,64]{1,0:T(8,128)(2,1)S(1)}, bf16[24,64]{1,0:T(8,128)(2,1)S(1)}, u32[]{:S(2)}, u32[]{:S(2)}) %collective-permute-start.2) | collective-permute-done | bytes 3104 | tf_op jit(solution)/shard_map/while/body/eval_jaxpr/ppermute | solution.py:23
  252.2 35.8 %collective-permute-done.2 = bf16[24,64]{1,0:T(8,128)(2,1)S(1)} collective-permute-done((bf16[24,64]{1,0:T(8,128)(2,1)S(1)}, bf16[24,64]{1,0:T(8,128)(2,1)S(1)}, u32[]{:S(2)}, u32[]{:S(2)}) %collective-permute-start.2) | collective-permute-done | bytes 3104 | tf_op jit(solution)/shard_map/while/body/eval_jaxpr/ppermute | solution.py:23
  296.4 34.9 %collective-permute-done.2 = bf16[24,64]{1,0:T(8,128)(2,1)S(1)} collective-permute-done((bf16[24,64]{1,0:T(8,128)(2,1)S(1)}, bf16[24,64]{1,0:T(8,128)(2,1)S(1)}, u32[]{:S(2)}, u32[]{:S(2)}) %collective-permute-start.2) | collective-permute-done | bytes 3104 | tf_op jit(solution)/shard_map/while/body/eval_jaxpr/ppermute | solution.py:23
  339.7 34.8 %collective-permute-done.2 = bf16[24,64]{1,0:T(8,128)(2,1)S(1)} collective-permute-done((bf16[24,64]{1,0:T(8,128)(2,1)S(1)}, bf16[24,64]{1,0:T(8,128)(2,1)S(1)}, u32[]{:S(2)}, u32[]{:S(2)}) %collective-permute-start.2) | collective-permute-done | bytes 3104 | tf_op jit(solution)/shard_map/while/body/eval_jaxpr/ppermute | solution.py:23
  382.9 33.9 %collective-permute-done.2 = bf16[24,64]{1,0:T(8,128)(2,1)S(1)} collective-permute-done((bf16[24,64]{1,0:T(8,128)(2,1)S(1)}, bf16[24,64]{1,0:T(8,128)(2,1)S(1)}, u32[]{:S(2)}, u32[]{:S(2)}) %collective-permute-start.2) | collective-permute-done | bytes 3104 | tf_op jit(solution)/shard_map/while/body/eval_jaxpr/ppermute | solution.py:23
  425.3 33.0 %collective-permute-done.2 = bf16[24,64]{1,0:T(8,128)(2,1)S(1)} collective-permute-done((bf16[24,64]{1,0:T(8,128)(2,1)S(1)}, bf16[24,64]{1,0:T(8,128)(2,1)S(1)}, u32[]{:S(2)}, u32[]{:S(2)}) %collective-permute-start.2) | collective-permute-done | bytes 3104 | tf_op jit(solution)/shard_map/while/body/eval_jaxpr/ppermute | solution.py:23
  466.7 809.2 %collective-permute-done.2 = bf16[24,64]{1,0:T(8,128)(2,1)S(1)} collective-permute-done((bf16[24,64]{1,0:T(8,128)(2,1)S(1)}, bf16[24,64]{1,0:T(8,128)(2,1)S(1)}, u32[]{:S(2)}, u32[]{:S(2)}) %collective-permute-start.2) | collective-permute-done | bytes 3104 | tf_op jit(solution)/shard_map/while/body/eval_jaxpr/ppermute | solution.py:23
  1279.0 112.1 %conditional.2 = ((bf16[2,128,1536]{1,2,0:T(8,128)(2,1)}, f32[2,24,64,256]{3,2,1,0:T(8,128)S(1)}, f32[24,256]{1,0:T(8,128)S(1)}, f32[24,64]{1,0:T(8,128)S(1)})) conditional(s32[]{:T(128)} %convert_element_type.81, (bf16[2,128,1536]{1,2,0:T(8,128)(2,1)}, f32[2,24,64,256]{3,2,1,0:T(8,128)S(1)}, f32[24,256]{1,0:T(8,128)S(1)}, ...), branch_computations={%region_1.1_spmd, %region_2.7_spmd} | conditional | flops 2895551488 | bytes 116423672 | solution.py:156
  1282.1 5.8 reshape.104
  1287.9 3.8 slice_bitcast_fusion
  1291.8 88.4 %while.35 = (s32[]{:T(128)}, f32[2,24,64,256]{3,2,1,0:T(8,128)S(1)}, f32[24,256]{1,0:T(8,128)S(1)}, f32[24,64]{1,0:T(8,128)S(1)}, f32[2,24,64,64]{3,2,1,0:T(8,12...) while((s32[]{:T(128)}, ...), condition=%wide.region_6.5_spmd, body=%wide.region_3.4_spmd.sunk | while | flops 2893975552 | bytes 98181968 | solution.py:85
  1306.6 4.1 multiply_reduce_fusion.5
  1331.1 4.5 fusion.140
  1350.8 4.1 multiply_reduce_fusion.5
  1375.3 4.5 fusion.140
  1380.2 3.7 copy.41
  1396.4 33.0 %collective-permute-done.2 = bf16[24,64]{1,0:T(8,128)(2,1)S(1)} collective-permute-done((bf16[24,64]{1,0:T(8,128)(2,1)S(1)}, bf16[24,64]{1,0:T(8,128)(2,1)S(1)}, u32[]{:S(2)}, u32[]{:S(2)}) %collective-permute-start.2) | collective-permute-done | bytes 3104 | tf_op jit(solution)/shard_map/while/body/eval_jaxpr/ppermute | solution.py:23
  1432.5 112.1 %conditional.2 = ((bf16[2,128,1536]{1,2,0:T(8,128)(2,1)}, f32[2,24,64,256]{3,2,1,0:T(8,128)S(1)}, f32[24,256]{1,0:T(8,128)S(1)}, f32[24,64]{1,0:T(8,128)S(1)})) conditional(s32[]{:T(128)} %convert_element_type.81, (bf16[2,128,1536]{1,2,0:T(8,128)(2,1)}, f32[2,24,64,256]{3,2,1,0:T(8,128)S(1)}, f32[24,256]{1,0:T(8,128)S(1)}, ...), branch_computations={%region_1.1_spmd, %region_2.7_spmd} | conditional | flops 2895551488 | bytes 116423672 | solution.py:156
  1435.6 5.8 reshape.104
  1441.4 3.8 slice_bitcast_fusion
  1445.3 88.4 %while.35 = (s32[]{:T(128)}, f32[2,24,64,256]{3,2,1,0:T(8,128)S(1)}, f32[24,256]{1,0:T(8,128)S(1)}, f32[24,64]{1,0:T(8,128)S(1)}, f32[2,24,64,64]{3,2,1,0:T(8,12...) while((s32[]{:T(128)}, ...), condition=%wide.region_6.5_spmd, body=%wide.region_3.4_spmd.sunk | while | flops 2893975552 | bytes 98181968 | solution.py:85
  1460.0 4.1 multiply_reduce_fusion.5
  1484.6 4.5 fusion.140
  1504.2 4.1 multiply_reduce_fusion.5
  1528.8 4.5 fusion.140
  1533.7 3.7 copy.41
  1549.9 31.4 %collective-permute-done.2 = bf16[24,64]{1,0:T(8,128)(2,1)S(1)} collective-permute-done((bf16[24,64]{1,0:T(8,128)(2,1)S(1)}, bf16[24,64]{1,0:T(8,128)(2,1)S(1)}, u32[]{:S(2)}, u32[]{:S(2)}) %collective-permute-start.2) | collective-permute-done | bytes 3104 | tf_op jit(solution)/shard_map/while/body/eval_jaxpr/ppermute | solution.py:23
  (307 shorter events, 245.1 us)
Async XLA Ops:
  6.5 163.0 %all-gather.2.cloned.1.call-start = ((), (), s32[]{:S(2)}) async-start(), calls=%async_computation | async-start | bytes 29196288 | tf_op jit(solution)/shard_map/all_gather | solution.py:110
  203.2 40.5 %collective-permute-start = (bf16[2,24,64,256]{3,2,1,0:T(8,128)(2,1)}, bf16[2,24,64,256]{3,2,1,0:T(8,128)(2,1)S(1)}, u32[]{:S(2)}, u32[]{:S(2)}) collective-permute-start(bf16[2,24,64,256]{3,2,1,0:T(8,128)(2,1)} %convert_element_type.82), channel_id=1, source_target_pairs={{0,32},{32,64},{64,96},{96,128},{128,160},{160,192},{192,224},{1,3... | collective-permute-start | bytes 4718600 | tf_op jit(solution)/shard_map/while/body/eval_jaxpr/ppermute | solution.py:23
  204.5 39.2 %collective-permute-start.1 = (bf16[24,256]{1,0:T(8,128)(2,1)S(1)}, bf16[24,256]{1,0:T(8,128)(2,1)S(1)}, u32[]{:S(2)}, u32[]{:S(2)}) collective-permute-start(bf16[24,256]{1,0:T(8,128)(2,1)S(1)} %convert_element_type.83), channel_id=1, source_target_pairs={{0,32},{32,64},{64,96},{96,128},{128,160},{160,192},{192,224},{1,3... | collective-permute-start | bytes 36872 | tf_op jit(solution)/shard_map/while/body/eval_jaxpr/ppermute | solution.py:23
  205.8 37.9 %collective-permute-start.2 = (bf16[24,64]{1,0:T(8,128)(2,1)S(1)}, bf16[24,64]{1,0:T(8,128)(2,1)S(1)}, u32[]{:S(2)}, u32[]{:S(2)}) collective-permute-start(bf16[24,64]{1,0:T(8,128)(2,1)S(1)} %convert_element_type.84), channel_id=1, source_target_pairs={{0,32},{32,64},{64,96},{96,128},{128,160},{160,192},{192,224},{1,3... | collective-permute-start | bytes 9224 | tf_op jit(solution)/shard_map/while/body/eval_jaxpr/ppermute | solution.py:23
  248.2 39.7 %collective-permute-start = (bf16[2,24,64,256]{3,2,1,0:T(8,128)(2,1)}, bf16[2,24,64,256]{3,2,1,0:T(8,128)(2,1)S(1)}, u32[]{:S(2)}, u32[]{:S(2)}) collective-permute-start(bf16[2,24,64,256]{3,2,1,0:T(8,128)(2,1)} %convert_element_type.82), channel_id=1, source_target_pairs={{0,32},{32,64},{64,96},{96,128},{128,160},{160,192},{192,224},{1,3... | collective-permute-start | bytes 4718600 | tf_op jit(solution)/shard_map/while/body/eval_jaxpr/ppermute | solution.py:23
  249.5 38.4 %collective-permute-start.1 = (bf16[24,256]{1,0:T(8,128)(2,1)S(1)}, bf16[24,256]{1,0:T(8,128)(2,1)S(1)}, u32[]{:S(2)}, u32[]{:S(2)}) collective-permute-start(bf16[24,256]{1,0:T(8,128)(2,1)S(1)} %convert_element_type.83), channel_id=1, source_target_pairs={{0,32},{32,64},{64,96},{96,128},{128,160},{160,192},{192,224},{1,3... | collective-permute-start | bytes 36872 | tf_op jit(solution)/shard_map/while/body/eval_jaxpr/ppermute | solution.py:23
  250.8 37.1 %collective-permute-start.2 = (bf16[24,64]{1,0:T(8,128)(2,1)S(1)}, bf16[24,64]{1,0:T(8,128)(2,1)S(1)}, u32[]{:S(2)}, u32[]{:S(2)}) collective-permute-start(bf16[24,64]{1,0:T(8,128)(2,1)S(1)} %convert_element_type.84), channel_id=1, source_target_pairs={{0,32},{32,64},{64,96},{96,128},{128,160},{160,192},{192,224},{1,3... | collective-permute-start | bytes 9224 | tf_op jit(solution)/shard_map/while/body/eval_jaxpr/ppermute | solution.py:23
  292.5 38.8 %collective-permute-start = (bf16[2,24,64,256]{3,2,1,0:T(8,128)(2,1)}, bf16[2,24,64,256]{3,2,1,0:T(8,128)(2,1)S(1)}, u32[]{:S(2)}, u32[]{:S(2)}) collective-permute-start(bf16[2,24,64,256]{3,2,1,0:T(8,128)(2,1)} %convert_element_type.82), channel_id=1, source_target_pairs={{0,32},{32,64},{64,96},{96,128},{128,160},{160,192},{192,224},{1,3... | collective-permute-start | bytes 4718600 | tf_op jit(solution)/shard_map/while/body/eval_jaxpr/ppermute | solution.py:23
  293.8 37.5 %collective-permute-start.1 = (bf16[24,256]{1,0:T(8,128)(2,1)S(1)}, bf16[24,256]{1,0:T(8,128)(2,1)S(1)}, u32[]{:S(2)}, u32[]{:S(2)}) collective-permute-start(bf16[24,256]{1,0:T(8,128)(2,1)S(1)} %convert_element_type.83), channel_id=1, source_target_pairs={{0,32},{32,64},{64,96},{96,128},{128,160},{160,192},{192,224},{1,3... | collective-permute-start | bytes 36872 | tf_op jit(solution)/shard_map/while/body/eval_jaxpr/ppermute | solution.py:23
  295.1 36.2 %collective-permute-start.2 = (bf16[24,64]{1,0:T(8,128)(2,1)S(1)}, bf16[24,64]{1,0:T(8,128)(2,1)S(1)}, u32[]{:S(2)}, u32[]{:S(2)}) collective-permute-start(bf16[24,64]{1,0:T(8,128)(2,1)S(1)} %convert_element_type.84), channel_id=1, source_target_pairs={{0,32},{32,64},{64,96},{96,128},{128,160},{160,192},{192,224},{1,3... | collective-permute-start | bytes 9224 | tf_op jit(solution)/shard_map/while/body/eval_jaxpr/ppermute | solution.py:23
  335.8 38.8 %collective-permute-start = (bf16[2,24,64,256]{3,2,1,0:T(8,128)(2,1)}, bf16[2,24,64,256]{3,2,1,0:T(8,128)(2,1)S(1)}, u32[]{:S(2)}, u32[]{:S(2)}) collective-permute-start(bf16[2,24,64,256]{3,2,1,0:T(8,128)(2,1)} %convert_element_type.82), channel_id=1, source_target_pairs={{0,32},{32,64},{64,96},{96,128},{128,160},{160,192},{192,224},{1,3... | collective-permute-start | bytes 4718600 | tf_op jit(solution)/shard_map/while/body/eval_jaxpr/ppermute | solution.py:23
  337.1 37.4 %collective-permute-start.1 = (bf16[24,256]{1,0:T(8,128)(2,1)S(1)}, bf16[24,256]{1,0:T(8,128)(2,1)S(1)}, u32[]{:S(2)}, u32[]{:S(2)}) collective-permute-start(bf16[24,256]{1,0:T(8,128)(2,1)S(1)} %convert_element_type.83), channel_id=1, source_target_pairs={{0,32},{32,64},{64,96},{96,128},{128,160},{160,192},{192,224},{1,3... | collective-permute-start | bytes 36872 | tf_op jit(solution)/shard_map/while/body/eval_jaxpr/ppermute | solution.py:23
  338.4 36.1 %collective-permute-start.2 = (bf16[24,64]{1,0:T(8,128)(2,1)S(1)}, bf16[24,64]{1,0:T(8,128)(2,1)S(1)}, u32[]{:S(2)}, u32[]{:S(2)}) collective-permute-start(bf16[24,64]{1,0:T(8,128)(2,1)S(1)} %convert_element_type.84), channel_id=1, source_target_pairs={{0,32},{32,64},{64,96},{96,128},{128,160},{160,192},{192,224},{1,3... | collective-permute-start | bytes 9224 | tf_op jit(solution)/shard_map/while/body/eval_jaxpr/ppermute | solution.py:23
  379.0 37.9 %collective-permute-start = (bf16[2,24,64,256]{3,2,1,0:T(8,128)(2,1)}, bf16[2,24,64,256]{3,2,1,0:T(8,128)(2,1)S(1)}, u32[]{:S(2)}, u32[]{:S(2)}) collective-permute-start(bf16[2,24,64,256]{3,2,1,0:T(8,128)(2,1)} %convert_element_type.82), channel_id=1, source_target_pairs={{0,32},{32,64},{64,96},{96,128},{128,160},{160,192},{192,224},{1,3... | collective-permute-start | bytes 4718600 | tf_op jit(solution)/shard_map/while/body/eval_jaxpr/ppermute | solution.py:23
  380.3 36.6 %collective-permute-start.1 = (bf16[24,256]{1,0:T(8,128)(2,1)S(1)}, bf16[24,256]{1,0:T(8,128)(2,1)S(1)}, u32[]{:S(2)}, u32[]{:S(2)}) collective-permute-start(bf16[24,256]{1,0:T(8,128)(2,1)S(1)} %convert_element_type.83), channel_id=1, source_target_pairs={{0,32},{32,64},{64,96},{96,128},{128,160},{160,192},{192,224},{1,3... | collective-permute-start | bytes 36872 | tf_op jit(solution)/shard_map/while/body/eval_jaxpr/ppermute | solution.py:23
  381.6 35.2 %collective-permute-start.2 = (bf16[24,64]{1,0:T(8,128)(2,1)S(1)}, bf16[24,64]{1,0:T(8,128)(2,1)S(1)}, u32[]{:S(2)}, u32[]{:S(2)}) collective-permute-start(bf16[24,64]{1,0:T(8,128)(2,1)S(1)} %convert_element_type.84), channel_id=1, source_target_pairs={{0,32},{32,64},{64,96},{96,128},{128,160},{160,192},{192,224},{1,3... | collective-permute-start | bytes 9224 | tf_op jit(solution)/shard_map/while/body/eval_jaxpr/ppermute | solution.py:23
  421.4 36.9 %collective-permute-start = (bf16[2,24,64,256]{3,2,1,0:T(8,128)(2,1)}, bf16[2,24,64,256]{3,2,1,0:T(8,128)(2,1)S(1)}, u32[]{:S(2)}, u32[]{:S(2)}) collective-permute-start(bf16[2,24,64,256]{3,2,1,0:T(8,128)(2,1)} %convert_element_type.82), channel_id=1, source_target_pairs={{0,32},{32,64},{64,96},{96,128},{128,160},{160,192},{192,224},{1,3... | collective-permute-start | bytes 4718600 | tf_op jit(solution)/shard_map/while/body/eval_jaxpr/ppermute | solution.py:23
  422.7 35.6 %collective-permute-start.1 = (bf16[24,256]{1,0:T(8,128)(2,1)S(1)}, bf16[24,256]{1,0:T(8,128)(2,1)S(1)}, u32[]{:S(2)}, u32[]{:S(2)}) collective-permute-start(bf16[24,256]{1,0:T(8,128)(2,1)S(1)} %convert_element_type.83), channel_id=1, source_target_pairs={{0,32},{32,64},{64,96},{96,128},{128,160},{160,192},{192,224},{1,3... | collective-permute-start | bytes 36872 | tf_op jit(solution)/shard_map/while/body/eval_jaxpr/ppermute | solution.py:23
  424.0 34.3 %collective-permute-start.2 = (bf16[24,64]{1,0:T(8,128)(2,1)S(1)}, bf16[24,64]{1,0:T(8,128)(2,1)S(1)}, u32[]{:S(2)}, u32[]{:S(2)}) collective-permute-start(bf16[24,64]{1,0:T(8,128)(2,1)S(1)} %convert_element_type.84), channel_id=1, source_target_pairs={{0,32},{32,64},{64,96},{96,128},{128,160},{160,192},{192,224},{1,3... | collective-permute-start | bytes 9224 | tf_op jit(solution)/shard_map/while/body/eval_jaxpr/ppermute | solution.py:23
  462.8 813.1 %collective-permute-start = (bf16[2,24,64,256]{3,2,1,0:T(8,128)(2,1)}, bf16[2,24,64,256]{3,2,1,0:T(8,128)(2,1)S(1)}, u32[]{:S(2)}, u32[]{:S(2)}) collective-permute-start(bf16[2,24,64,256]{3,2,1,0:T(8,128)(2,1)} %convert_element_type.82), channel_id=1, source_target_pairs={{0,32},{32,64},{64,96},{96,128},{128,160},{160,192},{192,224},{1,3... | collective-permute-start | bytes 4718600 | tf_op jit(solution)/shard_map/while/body/eval_jaxpr/ppermute | solution.py:23
  464.1 811.8 %collective-permute-start.1 = (bf16[24,256]{1,0:T(8,128)(2,1)S(1)}, bf16[24,256]{1,0:T(8,128)(2,1)S(1)}, u32[]{:S(2)}, u32[]{:S(2)}) collective-permute-start(bf16[24,256]{1,0:T(8,128)(2,1)S(1)} %convert_element_type.83), channel_id=1, source_target_pairs={{0,32},{32,64},{64,96},{96,128},{128,160},{160,192},{192,224},{1,3... | collective-permute-start | bytes 36872 | tf_op jit(solution)/shard_map/while/body/eval_jaxpr/ppermute | solution.py:23
  465.4 810.5 %collective-permute-start.2 = (bf16[24,64]{1,0:T(8,128)(2,1)S(1)}, bf16[24,64]{1,0:T(8,128)(2,1)S(1)}, u32[]{:S(2)}, u32[]{:S(2)}) collective-permute-start(bf16[24,64]{1,0:T(8,128)(2,1)S(1)} %convert_element_type.84), channel_id=1, source_target_pairs={{0,32},{32,64},{64,96},{96,128},{128,160},{160,192},{192,224},{1,3... | collective-permute-start | bytes 9224 | tf_op jit(solution)/shard_map/while/body/eval_jaxpr/ppermute | solution.py:23
  1331.1 4.5 copy-start.5
  1375.3 4.5 copy-start.5
  1392.5 36.9 %collective-permute-start = (bf16[2,24,64,256]{3,2,1,0:T(8,128)(2,1)}, bf16[2,24,64,256]{3,2,1,0:T(8,128)(2,1)S(1)}, u32[]{:S(2)}, u32[]{:S(2)}) collective-permute-start(bf16[2,24,64,256]{3,2,1,0:T(8,128)(2,1)} %convert_element_type.82), channel_id=1, source_target_pairs={{0,32},{32,64},{64,96},{96,128},{128,160},{160,192},{192,224},{1,3... | collective-permute-start | bytes 4718600 | tf_op jit(solution)/shard_map/while/body/eval_jaxpr/ppermute | solution.py:23
  1393.8 35.6 %collective-permute-start.1 = (bf16[24,256]{1,0:T(8,128)(2,1)S(1)}, bf16[24,256]{1,0:T(8,128)(2,1)S(1)}, u32[]{:S(2)}, u32[]{:S(2)}) collective-permute-start(bf16[24,256]{1,0:T(8,128)(2,1)S(1)} %convert_element_type.83), channel_id=1, source_target_pairs={{0,32},{32,64},{64,96},{96,128},{128,160},{160,192},{192,224},{1,3... | collective-permute-start | bytes 36872 | tf_op jit(solution)/shard_map/while/body/eval_jaxpr/ppermute | solution.py:23
  1395.1 34.3 %collective-permute-start.2 = (bf16[24,64]{1,0:T(8,128)(2,1)S(1)}, bf16[24,64]{1,0:T(8,128)(2,1)S(1)}, u32[]{:S(2)}, u32[]{:S(2)}) collective-permute-start(bf16[24,64]{1,0:T(8,128)(2,1)S(1)} %convert_element_type.84), channel_id=1, source_target_pairs={{0,32},{32,64},{64,96},{96,128},{128,160},{160,192},{192,224},{1,3... | collective-permute-start | bytes 9224 | tf_op jit(solution)/shard_map/while/body/eval_jaxpr/ppermute | solution.py:23
  1484.6 4.5 copy-start.5
  1528.8 4.5 copy-start.5
  1546.0 35.3 %collective-permute-start = (bf16[2,24,64,256]{3,2,1,0:T(8,128)(2,1)}, bf16[2,24,64,256]{3,2,1,0:T(8,128)(2,1)S(1)}, u32[]{:S(2)}, u32[]{:S(2)}) collective-permute-start(bf16[2,24,64,256]{3,2,1,0:T(8,128)(2,1)} %convert_element_type.82), channel_id=1, source_target_pairs={{0,32},{32,64},{64,96},{96,128},{128,160},{160,192},{192,224},{1,3... | collective-permute-start | bytes 4718600 | tf_op jit(solution)/shard_map/while/body/eval_jaxpr/ppermute | solution.py:23
  1547.3 34.0 %collective-permute-start.1 = (bf16[24,256]{1,0:T(8,128)(2,1)S(1)}, bf16[24,256]{1,0:T(8,128)(2,1)S(1)}, u32[]{:S(2)}, u32[]{:S(2)}) collective-permute-start(bf16[24,256]{1,0:T(8,128)(2,1)S(1)} %convert_element_type.83), channel_id=1, source_target_pairs={{0,32},{32,64},{64,96},{96,128},{128,160},{160,192},{192,224},{1,3... | collective-permute-start | bytes 36872 | tf_op jit(solution)/shard_map/while/body/eval_jaxpr/ppermute | solution.py:23
  1548.6 32.7 %collective-permute-start.2 = (bf16[24,64]{1,0:T(8,128)(2,1)S(1)}, bf16[24,64]{1,0:T(8,128)(2,1)S(1)}, u32[]{:S(2)}, u32[]{:S(2)}) collective-permute-start(bf16[24,64]{1,0:T(8,128)(2,1)S(1)} %convert_element_type.84), channel_id=1, source_target_pairs={{0,32},{32,64},{64,96},{96,128},{128,160},{160,192},{192,224},{1,3... | collective-permute-start | bytes 9224 | tf_op jit(solution)/shard_map/while/body/eval_jaxpr/ppermute | solution.py:23
  (42 other events, 90.5 us)
Sparse Core Ops, SparseCore 0:
  9.2 160.2 all-gather.1
where the time goes:
time: 1590 us
  waiting for transfers between devices  1240 us (78%)
  local copies, waits for them, and re-layouts  124 us (8%)
  matrix products  122 us (8%)
  other arithmetic  52 us (3%)
  starting transfers between devices  34.8 us (2%)
    ppermute x27, waiting for transfers between devices, shifted(): return lax.ppermute(block, axis, route)  1080 us
    all_gather x1, waiting for transfers between devices, on_device(): full_weight = lax.all_gather(proj_weight, 'dp', axis=0, tiled=True)  160 us
    dynamic_slice x24, local copies, waits for them, and re-layouts, run_slab(): lax.scan(minibatch, start_state, (inputs[0], inputs[1], inputs[2], step_r...  56.4 us
    ppermute x27, starting transfers between devices, shifted(): return lax.ppermute(block, axis, route)  34.8 us
  transfers between devices with their start and end apart: 28, of which 10 were waited for; matrix products, arithmetic and copies ran while one was open for 0% of the time, Pallas kernels for 0%

commit v1 on v0

v1 whole, which is shorter than its diff:
```python
import math

import jax
import jax.numpy as jnp
from jax import lax
from jax.experimental import pallas as pl
from jax.experimental.pallas import tpu as pltpu
from jax.sharding import Mesh
from jax.sharding import PartitionSpec as P

MB = 64
PAIRS = 3
cubic = 0.044715
root_scale = math.sqrt(2.0 / math.pi)
bf16 = jnp.bfloat16
f32 = jnp.float32


def mm(a, b):
    return lax.dot_general(a, b, (((1,), (0,)), ((), ())), preferred_element_type=f32)


def mm_nt(a, b):
    return lax.dot_general(a, b, (((1,), (1,)), ((), ())), preferred_element_type=f32)


def mm_tn(a, b):
    return lax.dot_general(a, b, (((0,), (0,)), ((), ())), preferred_element_type=f32)


def gate(z):
    return 0.5 + 0.5 * jnp.tanh(z * (root_scale + (root_scale * cubic) * (z * z)))


def ttt_kernel(order_ref, proj_ref, rate_ref, w1i, w2i, b1i, b2i, gain_ref, out_ref,
               w1s, w2s, b1s, b2s):
    slab = pl.program_id(0)

    @pl.when(slab == 0)
    def _():
        w1s[...] = w1i[...]
        w2s[...] = w2i[...]
        b1s[...] = b1i[...]
        b2s[...] = b2i[...]

    row = lax.broadcasted_iota(jnp.int32, (128, 128), 0)
    col = lax.broadcasted_iota(jnp.int32, (128, 128), 1)
    same = (row // 64) == (col // 64)
    causal = same & (row >= col)
    low = lax.broadcasted_iota(jnp.int32, (64, 128), 1) < 64

    def two(x):
        zero = jnp.zeros_like(x)
        return jnp.concatenate([jnp.where(low, x, zero), jnp.where(low, zero, x)], axis=0)

    for m in range(2):
        rows = pl.ds(m * MB, MB)
        st = []
        for p in range(PAIRS):
            def part(c):
                cols = pl.ds(c * 384 + p * 128, 128)
                return proj_ref[rows, cols]
            q, k, v = part(0).astype(f32), part(1).astype(f32), part(2).astype(f32)
            qm = two(q)
            km = two(k)
            kmb = km.astype(bf16)
            qmb = qm.astype(bf16)
            target = b2s[p] - (v - k)
            rate = jnp.concatenate(
                [jnp.where(low, rate_ref[rows, 2 * p : 2 * p + 1], 0.0),
                 jnp.where(low, 0.0, rate_ref[rows, 2 * p + 1 : 2 * p + 2])], axis=0)
            w1 = w1s[p].astype(bf16)
            w2 = w2s[p].astype(bf16)
            b1 = b1s[p]
            bias = jnp.concatenate([jnp.broadcast_to(b1[0:1], (64, 256)), jnp.broadcast_to(b1[1:2], (64, 256))], axis=0)
            z1 = mm(kmb, w1) + bias
            zq = mm(qmb, w1) + bias
            st.append((qm, qmb, kmb, target, rate, w2, z1, zq))
        st2 = []
        for p in range(PAIRS):
            qm, qmb, kmb, target, rate, w2, z1, zq = st[p]
            s = gate(z1)
            x2 = (z1 * s).astype(bf16)
            slope = s + (z1 * (s - s * s)) * (2.0 * root_scale + (6.0 * root_scale * cubic) * (z1 * z1))
            z2 = mm_nt(x2, w2)
            h2 = (z2 + jnp.concatenate([target, target], axis=0)) * rate
            h2b = h2.astype(bf16)
            h1 = mm(h2b, w2) * slope
            h1b = h1.astype(bf16)
            st2.append((x2, h2, h2b, h1, h1b))
        for p in range(PAIRS):
            qm, qmb, kmb, target, rate, w2, z1, zq = st[p]
            x2, h2, h2b, h1, h1b = st2[p]
            w1n = w1s[p] - mm_tn(kmb, h1b)
            w2n = w2s[p] - mm_tn(h2b, x2)
            b1n = b1s[p] - jnp.concatenate(
                [jnp.sum(h1[:64], axis=0, keepdims=True), jnp.sum(h1[64:], axis=0, keepdims=True)], axis=0)
            b2o = b2s[p]
            b2n = b2o - jnp.sum(h2, axis=0, keepdims=True)
            if m == 1:
                w1n, w2n, b1n, b2n = [t.astype(bf16).astype(f32) for t in (w1n, w2n, b1n, b2n)]
            w1s[p] = w1n
            w2s[p] = w2n
            b1s[p] = b1n
            b2s[p] = b2n
            m1 = jnp.where(causal, mm_nt(qmb, kmb) + 1.0, 0.0).astype(bf16)
            zq = zq - mm(m1, h1b)
            xq = (zq * gate(zq)).astype(bf16)
            both = mm_nt(xq, jnp.concatenate([w2, x2], axis=0))
            m2 = jnp.where(causal, both[:, 128:] + 1.0, 0.0).astype(bf16)
            y = qm + jnp.where(same, both[:, :128] + b2o, 0.0) - mm(m2, h2b)
            y = y * lax.rsqrt(jnp.sum(y * y, axis=1, keepdims=True) * (1.0 / 64.0) + 1e-6)
            y = (y[:64] + y[64:]) * gain_ref[0:1, p * 128 : (p + 1) * 128]
            out_ref[0, rows, p * 128 : (p + 1) * 128] = y.astype(bf16)


def ttt(order, projected, rates, w1, w2, b1, b2, gain):
    def whole(shape):
        return pl.BlockSpec(shape, lambda i, order: (0,) * len(shape))

    return pl.pallas_call(
        ttt_kernel,
        out_shape=jax.ShapeDtypeStruct((8, 128, 384), bf16),
        grid_spec=pltpu.PrefetchScalarGridSpec(
            num_scalar_prefetch=1,
            grid=(8,),
            in_specs=[
                pl.BlockSpec((128, 1152), lambda i, order: (order[i], 0)),
                pl.BlockSpec((128, 6), lambda i, order: (order[i], 0)),
                whole((PAIRS, 128, 256)),
                whole((PAIRS, 128, 256)),
                whole((PAIRS, 2, 256)),
                whole((PAIRS, 1, 128)),
                whole((1, 384)),
            ],
            out_specs=pl.BlockSpec((1, 128, 384), lambda i, order: (i, 0, 0)),
            scratch_shapes=[
                pltpu.VMEM((PAIRS, 128, 256), f32),
                pltpu.VMEM((PAIRS, 128, 256), f32),
                pltpu.VMEM((PAIRS, 2, 256), f32),
                pltpu.VMEM((PAIRS, 1, 128), f32),
            ],
        ),
        compiler_params=pltpu.CompilerParams(dimension_semantics=("arbitrary",)),
        name="ttt",
    )(order, projected, rates, w1, w2, b1, b2, gain)


DP = ("yl", "z", "c")
SEQ = ("x", "yh")
swap = [(0, 1), (1, 0)]
x_up = [(i, (i + 1) % 4) for i in range(4)]
x_down = [(i, (i - 1) % 4) for i in range(4)]


def x_ring(block):
    half = block.shape[0] // 2
    below = lax.ppermute(block, "x", x_up)
    above = lax.ppermute(block, "x", x_down)
    first = lax.ppermute(below[:half], "x", x_up)
    second = lax.ppermute(above[half:], "x", x_down)
    return [block, below, above, first, second]


def on_device(
    frames,
    proj_weight,
    rate_weight,
    rate_bias,
    init_weights,
    init_bias_hidden,
    init_bias_out,
    out_gain,
):
    x = lax.axis_index("x")
    yh = lax.axis_index("yh")
    mine = lax.dynamic_index_in_dim(frames, yh, 0, keepdims=False)
    sent = lax.dynamic_index_in_dim(frames, 1 - yh, 0, keepdims=False)
    weight = lax.dynamic_slice(proj_weight.reshape(96, 3, 1536), (0, 0, x * 384), (96, 3, 384))
    weight = lax.all_gather(weight.reshape(96, 1152), DP, axis=0, tiled=True)
    theirs = lax.ppermute(sent, "yh", swap)
    tokens = jnp.concatenate(x_ring(mine) + x_ring(theirs), axis=0)
    rate_columns = lax.dynamic_slice(rate_weight, (0, x * 6), (3072, 6))
    rate_offset = lax.dynamic_slice(rate_bias, (x * 6,), (6,))
    rates = jax.nn.sigmoid(
        jnp.dot(tokens, rate_columns, preferred_element_type=f32) + rate_offset
    ) * (1.0 / 20480.0)
    projected = jnp.dot(tokens, weight, preferred_element_type=f32).astype(bf16)
    slabs = jnp.arange(8, dtype=jnp.int32)
    away = (slabs // 2 - x) % 4
    order = jnp.where(away == 0, 0, jnp.where(away == 3, 1, away + 1)) + 4 * (slabs % 2 != yh)
    pair_weights = lax.dynamic_slice(init_weights, (0, x * 6, 0, 0), (2, 6, 64, 256))
    pair_weights = pair_weights.reshape(2, PAIRS, 128, 256)
    hidden_bias = lax.dynamic_slice(init_bias_hidden, (x * 6, 0), (6, 256)).reshape(PAIRS, 2, 256)
    out_bias = lax.dynamic_slice(init_bias_out, (x * 6, 0), (6, 64)).reshape(PAIRS, 1, 128)
    gain = lax.dynamic_slice(out_gain, (x * 384,), (384,)).reshape(1, 384)
    result = ttt(
        order.astype(jnp.int32),
        projected,
        rates,
        pair_weights[0],
        pair_weights[1],
        hidden_bias,
        out_bias,
        gain,
    )
    result = lax.all_to_all(result, SEQ, 0, 0, tiled=True)
    return result.reshape(4, 2, 128, 384).transpose(1, 2, 0, 3).reshape(2, 128, 1536)


def solution(mesh):
    fine = Mesh(mesh.devices.reshape(4, 2, 2, 8, 2), ("x", "yh", "yl", "z", "c"))
    return jax.shard_map(
        on_device,
        mesh=fine,
        in_specs=(P(DP, SEQ, None), P(DP, None), P(), P(), P(), P(), P(), P()),
        out_specs=P(DP, SEQ, None),
        check_vma=False,
    )
```

time: 1590 us -> 161 us (0.10)
  the two profiles are of different devices: /device:TPU:30 before, /device:TPU:96 now
where the time goes in v1:
time: 161 us; the launch traced here: 158 us
  waiting for transfers between devices  36.1 us (22%)
  Pallas kernels  31.8 us (20%)
  local copies, waits for them, and re-layouts  22 us (14%)
  blocking collectives  19.1 us (12%)
  matrix products  18.9 us (12%)
  starting transfers between devices  16.6 us (10%)
  between operations  13.5 us (8%)
    pallas_call x1, Pallas kernels, ttt(): pl.pallas_call(ttt_kernel, out_shape=jax.ShapeDtypeStruct((8, 128, 384),...  31.8 us
    all_to_all x1, blocking collectives, on_device(): result = lax.all_to_all(result, SEQ, 0, 0, tiled=True)  19.1 us
    ppermute x2, waiting for transfers between devices, x_ring(): below = lax.ppermute(block, 'x', x_up)  18.9 us
    dot_general x1, matrix products, on_device(): projected = jnp.dot(tokens, weight, preferred_element_type=f32).astype(bf16)  13.5 us
    unnamed x16, local copies, waits for them, and re-layouts  10.4 us
    ppermute x2, waiting for transfers between devices, x_ring(): first = lax.ppermute(below[:half], 'x', x_up)  9.3 us
    all_gather x1, waiting for transfers between devices, on_device(): weight = lax.all_gather(weight.reshape(96, 1152), DP, axis=0, tiled=True)  7.35 us
    ppermute x2, starting transfers between devices, x_ring(): second = lax.ppermute(above[half:], 'x', x_down)  6.5 us
  transfers between devices with their start and end apart: 10, of which 6 were waited for; matrix products, arithmetic and copies ran while one was open for 15% of the time, Pallas kernels for 0%

profile of v1, /device:TPU:96, one launch (start us, length us, event | category | flops | bytes accessed | tf_op | source)
XLA Modules:
  0.0 158.5 jit_solution(1686395143222187625)
XLA Ops:
  6.6 2.5 %reshape.27 = bf16[96,3,1536]{2,1,0:T(4,128)(2,1)S(1)} reshape(bf16[96,4608]{1,0:T(8,128)(2,1)} %param.9) | data formatting | bytes 1769472 | tf_op jit(solution)/shard_map/reshape | solution.py:179
  9.1 0.7 copy.19
  9.9 2.5 %constant_dynamic-update-slice_fusion.9 = (bf16[1024,3072]{1,0:T(8,128)(2,1)}, bf16[128,3072]{1,0:T(8,128)(2,1)}) fusion(bf16[2,128,3072]{2,1,0:T(8,128)(2,1)} %param.8, s32[]{:T(128)S(6)} %select_n.46), kind=kLoop, calls=%fused_computation.19 | loop fusion | bytes 2359300
  12.4 1.5 collective-permute-start
  13.9 1.7 %collective-permute-start.1 = (bf16[128,3072]{1,0:T(8,128)(2,1)}, bf16[128,3072]{1,0:T(8,128)(2,1)S(1)}, u32[]{:S(2)}, u32[]{:S(2)}) collective-permute-start(bf16[128,3072]{1,0:T(8,128)(2,1)} %get-tuple-element.6), channel_id=1, source_target_pairs={{0,192},{64,0},{128,64},{192,128},{1,193},{65,1},{129,65},{193,129... | collective-permute-start | bytes 2359304 | tf_op jit(solution)/shard_map/ppermute | solution.py:159
  15.6 0.9 dynamic-slice_bitcast_fusion
  16.6 3.2 %collective-permute-start.4 = (bf16[128,3072]{1,0:T(8,128)(2,1)}, bf16[128,3072]{1,0:T(8,128)(2,1)S(1)}, u32[]{:S(2)}, u32[]{:S(2)}) collective-permute-start(bf16[128,3072]{1,0:T(8,128)(2,1)} %dynamic-slice_bitcast_fusion), channel_id=1, source_target_pairs={{0,32},{32,0},{1,33},{33,1},{2,34},{34,2},{3,35},{35,3},{4,36},{36... | collective-permute-start | bytes 2359304 | tf_op jit(solution)/shard_map/ppermute | solution.py:181
  19.8 0.7 constant_dynamic-slice_fusion.2
  22.5 0.8 dynamic_slice.36
  24.5 2.1 %constant_dynamic-slice_fusion.3 = (f32[1,6,64,256]{3,2,1,0:T(8,128)}, f32[1,6,64,256]{3,2,1,0:T(8,128)}) fusion(f32[2,24,64,256]{3,2,1,0:T(8,128)} %param.12, s32[]{:T(128)S(6)} %add.58, s32[]{:T(128)S(6)} %select_n.49), kind=kLoop, calls=%fused_computation.25 | loop fusion | bytes 1572872 | tf_op jit(solution)/shard_map/slice | solution.py:202
  26.5 6.5 %collective-permute-done = bf16[128,3072]{1,0:T(8,128)(2,1)S(1)} collective-permute-done((bf16[128,3072]{1,0:T(8,128)(2,1)}, bf16[128,3072]{1,0:T(8,128)(2,1)S(1)}, u32[]{:S(2)}, u32[]{:S(2)}) %collective-permute-start) | collective-permute-done | bytes 786464 | tf_op jit(solution)/shard_map/ppermute | solution.py:158
  33.5 3.0 %collective-permute-start.3 = (bf16[64,3072]{1,0:T(8,128)(2,1)S(1)}, bf16[64,3072]{1,0:T(8,128)(2,1)S(1)}, u32[]{:S(2)}, u32[]{:S(2)}) collective-permute-start(bf16[64,3072]{1,0:T(8,128)(2,1)S(1)} %slice.27), channel_id=1, source_target_pairs={{0,192},{64,0},{128,64},{192,128},{1,193},{65,1},{129,65},{193,129... | collective-permute-start | bytes 1179656 | tf_op jit(solution)/shard_map/ppermute | solution.py:161
  37.3 3.0 %collective-permute-start.6 = (bf16[128,3072]{1,0:T(8,128)(2,1)S(1)}, bf16[128,3072]{1,0:T(8,128)(2,1)S(1)}, u32[]{:S(2)}, u32[]{:S(2)}) collective-permute-start(bf16[128,3072]{1,0:T(8,128)(2,1)S(1)} %collective-permute-done.4), channel_id=1, source_target_pairs={{0,192},{64,0},{128,64},{192,128},{1,193},{65,1},{129,65},{193,129... | collective-permute-start | bytes 2359304 | tf_op jit(solution)/shard_map/ppermute | solution.py:159
  40.2 1.0 constant_dynamic-update-slice_fusion.8
  41.2 1.0 constant_dynamic-update-slice_fusion.7
  42.2 4.2 %collective-permute-done.2 = bf16[64,3072]{1,0:T(8,128)(2,1)S(1)} collective-permute-done((bf16[64,3072]{1,0:T(8,128)(2,1)S(1)}, bf16[64,3072]{1,0:T(8,128)(2,1)S(1)}, u32[]{:S(2)}, u32[]{:S(2)}) %collective-permute-start.2) | collective-permute-done | bytes 393248 | tf_op jit(solution)/shard_map/ppermute | solution.py:160
  46.5 0.8 constant_dynamic-update-slice_fusion.6
  47.2 0.8 constant_dynamic-update-slice_fusion.5
  48.0 0.9 constant_dynamic-update-slice_fusion.4
  49.0 12.4 %collective-permute-done.5 = bf16[128,3072]{1,0:T(8,128)(2,1)S(1)} collective-permute-done((bf16[128,3072]{1,0:T(8,128)(2,1)S(1)}, bf16[128,3072]{1,0:T(8,128)(2,1)S(1)}, u32[]{:S(2)}, u32[]{:S(2)}) %collective-permute-start.5) | collective-permute-done | bytes 786464 | tf_op jit(solution)/shard_map/ppermute | solution.py:158
  61.5 3.5 %collective-permute-start.8 = (bf16[64,3072]{1,0:T(8,128)(2,1)S(1)}, bf16[64,3072]{1,0:T(8,128)(2,1)S(1)}, u32[]{:S(2)}, u32[]{:S(2)}) collective-permute-start(bf16[64,3072]{1,0:T(8,128)(2,1)S(1)} %slice.29), channel_id=1, source_target_pairs={{0,192},{64,0},{128,64},{192,128},{1,193},{65,1},{129,65},{193,129... | collective-permute-start | bytes 1179656 | tf_op jit(solution)/shard_map/ppermute | solution.py:161
  65.0 0.9 constant_dynamic-update-slice_fusion.3
  65.9 0.9 constant_dynamic-update-slice_fusion.2
  66.8 5.1 %collective-permute-done.7 = bf16[64,3072]{1,0:T(8,128)(2,1)S(1)} collective-permute-done((bf16[64,3072]{1,0:T(8,128)(2,1)S(1)}, bf16[64,3072]{1,0:T(8,128)(2,1)S(1)}, u32[]{:S(2)}, u32[]{:S(2)}) %collective-permute-start.7) | collective-permute-done | bytes 393248 | tf_op jit(solution)/shard_map/ppermute | solution.py:160
  71.9 0.8 constant_dynamic-update-slice_fusion.1
  72.7 0.8 constant_dynamic-update-slice_fusion
  73.5 5.4 %fusion.4.rate_ref = f32[1024,6]{1,0:T(8,128)} fusion(bf16[1024,3072]{1,0:T(8,128)(2,1)} %constant_dynamic-update-slice_fusion, f32[6]{0:T(128)S(1)} %dynamic_slice.32, bf16[3072,24]{0,1:T(8,128)(2,1)S(1)} %copy-done, s32[]{:T(128)S(6)} %select_n.49), kind=kOutput, calls=%fused_computation.6 | convolution fusion | flops 37779456 | bytes 6365700 | tf_op jit(solution)/shard_map/dot_general | solution.py:186
  79.0 7.4 %all-gather.2.cloned.1.call-done = bf16[3072,1152]{1,0:T(8,128)(2,1)} async-done(((bf16[96,1152]{1,0:T(8,128)(2,1)}), bf16[3072,1152]{1,0:T(8,128)(2,1)}) %all-gather.2.cloned.1.call-update) | async-done | bytes 7077904 | tf_op jit(solution)/shard_map/all_gather | solution.py:180
  86.3 13.5 %convolution_convert_fusion.proj_ref = bf16[1024,1152]{1,0:T(8,128)(2,1)} fusion(bf16[1024,3072]{1,0:T(8,128)(2,1)} %constant_dynamic-update-slice_fusion, bf16[3072,1152]{1,0:T(8,128)(2,1)} %all-gather.2.cloned.1.call-done), kind=kOutput, calls=%fused_computation | convolution fusion | flops 7248936960 | bytes 15728640 | tf_op jit(solution)/shard_map/dot_general | solution.py:188
  99.8 31.8 %ttt.1 = bf16[8,128,384]{2,1,0:T(8,128)(2,1)} custom-call(s32[8]{0:T(128)} %fusion.7.order_ref, bf16[1024,1152]{1,0:T(8,128)(2,1)} %convolution_convert_fusion.proj_ref, f32[1024,6]{1,0:T(8,128)} %fusion.4.rate_ref, f32[3,128,256]{2,1,0:T(8,128)} %bitcast.19, f32[3,128,256]{2,1,0:T(8,128)} %bitcast.18, f32[3,2,256]{2,1,0:T(2,128)} %reshape.29.b1i, ...), custom_call_target="tpu_custom_call" | custom-call | tf_op jit(solution)/shard_map/ttt/pallas_call | solution.py:121
  131.5 19.1 %all_to_all.5 = bf16[8,128,384]{2,1,0:T(8,128)(2,1)S(1)} all-to-all(bf16[8,128,384]{2,1,0:T(8,128)(2,1)} %ttt.1), channel_id=1, replica_groups=mesh['x'=4,'yh'=2,'yl'=2,'z'=8,'c'=2] {'x','yh'}, dimensions={0} | all-to-all | bytes 1572864 | tf_op jit(solution)/shard_map/all_to_all | solution.py:207
  150.6 1.0 copy.18
  (27 shorter events, 4.7 us)
Async XLA Ops:
  6.5 67.0 %copy-start = (bf16[3072,24]{0,1:T(8,128)(2,1)S(1)}, bf16[3072,24]{0,1:T(8,128)(2,1)}, u32[]{:S(2)}) copy-start(bf16[3072,24]{0,1:T(8,128)(2,1)} %param.10) | copy-start | bytes 442372
  6.5 9.1 %copy-start.1 = (bf16[2,128,3072]{2,1,0:T(8,128)(2,1)S(1)}, bf16[2,128,3072]{2,1,0:T(8,128)(2,1)}, u32[]{:S(2)}) copy-start(bf16[2,128,3072]{2,1,0:T(8,128)(2,1)} %param.8) | copy-start | bytes 4718596
  6.5 13.2 %copy-start.2 = (f32[24]{0:T(128)S(1)}, f32[24]{0:T(128)}, u32[]{:S(2)}) copy-start(f32[24]{0:T(128)} %param.11) | copy-start | bytes 292
  6.5 79.8 %all-gather.2.cloned.1.call-start = ((), (), s32[]{:S(2)}) async-start(), calls=%async_computation.1 | async-start | bytes 7299072 | tf_op jit(solution)/shard_map/all_gather | solution.py:180
  12.4 20.7 %collective-permute-start = (bf16[128,3072]{1,0:T(8,128)(2,1)}, bf16[128,3072]{1,0:T(8,128)(2,1)S(1)}, u32[]{:S(2)}, u32[]{:S(2)}) collective-permute-start(bf16[128,3072]{1,0:T(8,128)(2,1)} %get-tuple-element.6), channel_id=1, source_target_pairs={{0,64},{64,128},{128,192},{192,0},{1,65},{65,129},{129,193},{193,1... | collective-permute-start | bytes 2359304 | tf_op jit(solution)/shard_map/ppermute | solution.py:158
  13.9 19.6 %collective-permute-start.1 = (bf16[128,3072]{1,0:T(8,128)(2,1)}, bf16[128,3072]{1,0:T(8,128)(2,1)S(1)}, u32[]{:S(2)}, u32[]{:S(2)}) collective-permute-start(bf16[128,3072]{1,0:T(8,128)(2,1)} %get-tuple-element.6), channel_id=1, source_target_pairs={{0,192},{64,0},{128,64},{192,128},{1,193},{65,1},{129,65},{193,129... | collective-permute-start | bytes 2359304 | tf_op jit(solution)/shard_map/ppermute | solution.py:159
  16.6 20.4 %collective-permute-start.4 = (bf16[128,3072]{1,0:T(8,128)(2,1)}, bf16[128,3072]{1,0:T(8,128)(2,1)S(1)}, u32[]{:S(2)}, u32[]{:S(2)}) collective-permute-start(bf16[128,3072]{1,0:T(8,128)(2,1)} %dynamic-slice_bitcast_fusion), channel_id=1, source_target_pairs={{0,32},{32,0},{1,33},{33,1},{2,34},{34,2},{3,35},{35,3},{4,36},{36... | collective-permute-start | bytes 2359304 | tf_op jit(solution)/shard_map/ppermute | solution.py:181
  33.1 13.3 %collective-permute-start.2 = (bf16[64,3072]{1,0:T(8,128)(2,1)S(1)}, bf16[64,3072]{1,0:T(8,128)(2,1)S(1)}, u32[]{:S(2)}, u32[]{:S(2)}) collective-permute-start(bf16[64,3072]{1,0:T(8,128)(2,1)S(1)} %slice.26), channel_id=1, source_target_pairs={{0,64},{64,128},{128,192},{192,0},{1,65},{65,129},{129,193},{193,1... | collective-permute-start | bytes 1179656 | tf_op jit(solution)/shard_map/ppermute | solution.py:160
  33.5 13.7 %collective-permute-start.3 = (bf16[64,3072]{1,0:T(8,128)(2,1)S(1)}, bf16[64,3072]{1,0:T(8,128)(2,1)S(1)}, u32[]{:S(2)}, u32[]{:S(2)}) collective-permute-start(bf16[64,3072]{1,0:T(8,128)(2,1)S(1)} %slice.27), channel_id=1, source_target_pairs={{0,192},{64,0},{128,64},{192,128},{1,193},{65,1},{129,65},{193,129... | collective-permute-start | bytes 1179656 | tf_op jit(solution)/shard_map/ppermute | solution.py:161
  37.0 24.4 %collective-permute-start.5 = (bf16[128,3072]{1,0:T(8,128)(2,1)S(1)}, bf16[128,3072]{1,0:T(8,128)(2,1)S(1)}, u32[]{:S(2)}, u32[]{:S(2)}) collective-permute-start(bf16[128,3072]{1,0:T(8,128)(2,1)S(1)} %collective-permute-done.4), channel_id=1, source_target_pairs={{0,64},{64,128},{128,192},{192,0},{1,65},{65,129},{129,193},{193,1... | collective-permute-start | bytes 2359304 | tf_op jit(solution)/shard_map/ppermute | solution.py:158
  37.3 24.2 %collective-permute-start.6 = (bf16[128,3072]{1,0:T(8,128)(2,1)S(1)}, bf16[128,3072]{1,0:T(8,128)(2,1)S(1)}, u32[]{:S(2)}, u32[]{:S(2)}) collective-permute-start(bf16[128,3072]{1,0:T(8,128)(2,1)S(1)} %collective-permute-done.4), channel_id=1, source_target_pairs={{0,192},{64,0},{128,64},{192,128},{1,193},{65,1},{129,65},{193,129... | collective-permute-start | bytes 2359304 | tf_op jit(solution)/shard_map/ppermute | solution.py:159
  61.4 10.6 %collective-permute-start.7 = (bf16[64,3072]{1,0:T(8,128)(2,1)S(1)}, bf16[64,3072]{1,0:T(8,128)(2,1)S(1)}, u32[]{:S(2)}, u32[]{:S(2)}) collective-permute-start(bf16[64,3072]{1,0:T(8,128)(2,1)S(1)} %slice.28), channel_id=1, source_target_pairs={{0,64},{64,128},{128,192},{192,0},{1,65},{65,129},{129,193},{193,1... | collective-permute-start | bytes 1179656 | tf_op jit(solution)/shard_map/ppermute | solution.py:160
  61.5 11.2 %collective-permute-start.8 = (bf16[64,3072]{1,0:T(8,128)(2,1)S(1)}, bf16[64,3072]{1,0:T(8,128)(2,1)S(1)}, u32[]{:S(2)}, u32[]{:S(2)}) collective-permute-start(bf16[64,3072]{1,0:T(8,128)(2,1)S(1)} %slice.29), channel_id=1, source_target_pairs={{0,192},{64,0},{128,64},{192,128},{1,193},{65,1},{129,65},{193,129... | collective-permute-start | bytes 1179656 | tf_op jit(solution)/shard_map/ppermute | solution.py:161
Sparse Core Ops, SparseCore 0:
  10.0 76.2 all-gather.1

commit v2 on v1

v2 whole, which is shorter than its diff:
```python
import math

import jax
import jax.numpy as jnp
import numpy as np
from jax import lax
from jax.experimental import pallas as pl
from jax.experimental.pallas import tpu as pltpu
from jax.sharding import Mesh
from jax.sharding import PartitionSpec as P

MB = 64
PAIRS = 3
cubic = 0.044715
root_scale = math.sqrt(2.0 / math.pi)
bf16 = jnp.bfloat16
f32 = jnp.float32


def mm(a, b):
    return lax.dot_general(a, b, (((1,), (0,)), ((), ())), preferred_element_type=f32)


def mm_nt(a, b):
    return lax.dot_general(a, b, (((1,), (1,)), ((), ())), preferred_element_type=f32)


def mm_tn(a, b):
    return lax.dot_general(a, b, (((0,), (0,)), ((), ())), preferred_element_type=f32)


def gate(z):
    return 0.5 + 0.5 * jnp.tanh(z * (root_scale + (root_scale * cubic) * (z * z)))


TOKEN_PIECES = [
    (0, 0, 128), (1, 0, 128), (2, 0, 128), (3, 0, 64), (4, 0, 64),
    (5, 0, 128), (3, 64, 128), (4, 64, 128), (6, 0, 64), (7, 0, 64),
]
NT = 8
WEIGHT_PIECES = [(h, i * 96, 96) for h in (0, 2) for i in range(14)] + [
    (h, i * 96, 96) for h in (1, 3) for i in range(2)
]


def layer_kernel(offset_ref, *refs):
    token_refs = refs[:NT]
    weight_refs = refs[NT : NT + 4]
    rwt_ref, rbias_ref, w1i, w2i, b1i, b2i, gain_ref, out_ref = refs[NT + 4 : NT + 12]
    (w1s, w2s, b1s, b2s, qm_s, wh_s, wx_s, h2_s, b1_s, b2_s, q_s,
     tokens_s, weight_s, proj_s, rate_s, sems) = refs[NT + 12 :]
    slab = pl.program_id(0)

    @pl.when(slab == 0)
    def _():
        copies = []
        for i, (ref, start, size) in enumerate(WEIGHT_PIECES):
            at = pl.multiple_of(offset_ref[len(TOKEN_PIECES) + i], 32)
            copies.append(
                pltpu.make_async_copy(
                    weight_refs[ref].at[pl.ds(start, size)], weight_s.at[pl.ds(at, size)], sems.at[i]
                )
            )
        for i, (ref, start, size) in enumerate(TOKEN_PIECES):
            at = pl.multiple_of(offset_ref[i], 64)
            copies.append(
                pltpu.make_async_copy(
                    token_refs[ref].at[pl.ds(start, size)],
                    tokens_s.at[pl.ds(at, size)],
                    sems.at[len(WEIGHT_PIECES) + i],
                )
            )
        for copy in copies:
            copy.start()
        w1s[...] = w1i[...]
        w2s[...] = w2i[...]
        b1s[...] = b1i[...]
        b2s[...] = b2i[...]
        for copy in copies:
            copy.wait()

        def project(i, carry):
            rows = pl.ds(pl.multiple_of(i * 256, 256), 256)
            for n in range(5):
                cols = pl.ds(n * 256, 256 if n < 4 else 128)
                proj_s[rows, cols] = mm(tokens_s[rows, :], weight_s[:, cols]).astype(bf16)
            logits = mm(tokens_s[rows, :], rwt_ref[...]) + rbias_ref[...]
            rate_s[rows] = (1.0 / 20480.0) / (1.0 + jnp.exp(-logits))
            return carry

        lax.fori_loop(0, 4, project, 0)

    low = lax.broadcasted_iota(jnp.int32, (64, 128), 1) < 64

    def two(x):
        zero = jnp.zeros_like(x)
        return jnp.concatenate([jnp.where(low, x, zero), jnp.where(low, zero, x)], axis=0)

    tri = lax.broadcasted_iota(jnp.int32, (64, 128), 0) >= lax.broadcasted_iota(jnp.int32, (64, 128), 1) % 64

    def one(x):
        return jnp.where(low, x[:64], x[64:])

    def train(m):
        rows = pl.ds(pl.multiple_of(slab * 128 + m * MB, MB), MB)
        D = []
        for p in range(PAIRS):
            def part(c):
                return proj_s[rows, pl.ds(c * 384 + p * 128, 128)]
            q, k, v = part(0), part(1), part(2)
            kf = k.astype(f32)
            kmb = two(k)
            w1 = w1s[p].astype(bf16); w2 = w2s[p].astype(bf16)
            b1 = b1s[p]
            bias = jnp.concatenate([jnp.broadcast_to(b1[0:1], (64, 256)), jnp.broadcast_to(b1[1:2], (64, 256))], axis=0)
            z1 = mm(kmb, w1) + bias
            D.append(dict(w1=w1, w2=w2, kmb=kmb, q=q, vk=v.astype(f32) - kf, z1=z1, b1=b1, b2=b2s[p]))
        yield
        for p in range(PAIRS):
            d = D[p]
            z1 = d["z1"]
            s = gate(z1)
            d["x2"] = (z1 * s).astype(bf16)
            d["z2"] = mm_nt(d["x2"], d["w2"])
            d["slope"] = s + (z1 * (s - s * s)) * (2.0 * root_scale + (6.0 * root_scale * cubic) * (z1 * z1))
        yield
        for p in range(PAIRS):
            d = D[p]
            rate = jnp.where(low, rate_s[rows, 2 * p : 2 * p + 1], rate_s[rows, 2 * p + 1 : 2 * p + 2])
            h2 = (one(d["z2"]) + (d["b2"] - d["vk"])) * rate
            d["h2b"] = two(h2.astype(bf16))
            d["g1"] = mm(d["h2b"], d["w2"])
            b2n = d["b2"] - jnp.sum(h2, axis=0, keepdims=True)
            if m == 1:
                b2n = b2n.astype(bf16).astype(f32)
            b2s[p] = b2n
        for p in range(PAIRS):
            d = D[p]
            d["m1"] = two(jnp.where(tri, -1.0 - mm_nt(d["q"], d["kmb"]), 0.0).astype(bf16))
            w2n = w2s[p] - mm_tn(d["h2b"], d["x2"])
            if m == 1:
                w2n = w2n.astype(bf16).astype(f32)
            w2s[p] = w2n
        yield
        for p in range(PAIRS):
            d = D[p]
            h1 = d["g1"] * d["slope"]
            h1b = h1.astype(bf16)
            w1n = w1s[p] - mm_tn(d["kmb"], h1b)
            db = jnp.concatenate([jnp.sum(h1[:64], axis=0, keepdims=True), jnp.sum(h1[64:], axis=0, keepdims=True)], axis=0)
            b1n = d["b1"] - db
            if m == 1:
                w1n = w1n.astype(bf16).astype(f32); b1n = b1n.astype(bf16).astype(f32)
            w1s[p] = w1n; b1s[p] = b1n
            d["h1b"] = h1b
        yield
        for p in range(PAIRS):
            d = D[p]
            qm_s[m, p, :, :128] = two(d["q"])
            qm_s[m, p, :, 128:] = d["m1"]
            wh_s[m, p, :128] = d["w1"]
            wh_s[m, p, 128:] = d["h1b"]
            wx_s[m, p, :128] = d["w2"]
            wx_s[m, p, 128:] = d["x2"]
            h2_s[m, p] = d["h2b"]
            b1_s[m, p] = d["b1"]
            b2_s[m, p] = d["b2"]
            q_s[m, p] = d["q"]
        yield

    def query(m, start):
        D = [dict() for _ in range(PAIRS)]
        for p in range(PAIRS):
            b1 = b1_s[m, p]
            bias = jnp.concatenate([jnp.broadcast_to(b1[0:1], (64, 256)), jnp.broadcast_to(b1[1:2], (64, 256))], axis=0)
            D[p]["zq"] = mm(qm_s[m, p], wh_s[m, p]) + bias
        yield
        for p in range(PAIRS):
            d = D[p]
            zq = d["zq"]
            xq = (zq * gate(zq)).astype(bf16)
            both = mm_nt(xq, wx_s[m, p])
            d["bw"] = both[:, :128]
            d["bx"] = both[:, 128:]
        yield
        for p in range(PAIRS):
            d = D[p]
            m2 = jnp.where(tri, one(d["bx"]) + 1.0, 0.0).astype(bf16)
            d["mh"] = mm(m2, h2_s[m, p])
        yield
        for p in range(PAIRS):
            d = D[p]
            y = q_s[m, p].astype(f32) + (one(d["bw"]) + b2_s[m, p]) - d["mh"]
            yy = y * y
            lo = jnp.sum(jnp.where(low, yy, 0.0), axis=1, keepdims=True)
            hi = jnp.sum(jnp.where(low, 0.0, yy), axis=1, keepdims=True)
            y = y * lax.rsqrt(jnp.where(low, lo, hi) * (1.0 / 64.0) + 1e-6)
            y = y * gain_ref[0:1, p * 128 : (p + 1) * 128]
            out_ref[pl.ds(start, MB), p * 128 : (p + 1) * 128] = y.astype(bf16)
        yield

    def weave(*gens):
        gens = list(gens)
        while gens:
            for g in list(gens):
                if next(g, "end") == "end":
                    gens.remove(g)

    before = pl.multiple_of(jnp.maximum(slab * 128 - MB, 0), MB)
    weave(train(0), query(1, before))
    weave(train(1), query(0, pl.multiple_of(slab * 128, MB)))

    @pl.when(slab == 7)
    def _():
        weave(query(1, pl.multiple_of(slab * 128 + MB, MB)))


def layer(offsets, tokens, weights, rwt, rbias, w1, w2, b1, b2, gain):
    def whole(shape):
        return pl.BlockSpec(shape, lambda i, offsets: (0,) * len(shape))

    anywhere = pl.BlockSpec(memory_space=pl.ANY)
    pieces = len(TOKEN_PIECES) + len(WEIGHT_PIECES)
    return pl.pallas_call(
        layer_kernel,
        out_shape=jax.ShapeDtypeStruct((1024, 384), bf16),
        grid_spec=pltpu.PrefetchScalarGridSpec(
            num_scalar_prefetch=1,
            grid=(8,),
            in_specs=[anywhere] * (NT + 4)
            + [
                whole((3072, 128)),
                whole((1, 128)),
                whole((PAIRS, 128, 256)),
                whole((PAIRS, 128, 256)),
                whole((PAIRS, 2, 256)),
                whole((PAIRS, 1, 128)),
                whole((1, 384)),
            ],
            out_specs=whole((1024, 384)),
            scratch_shapes=[
                pltpu.VMEM((PAIRS, 128, 256), f32),
                pltpu.VMEM((PAIRS, 128, 256), f32),
                pltpu.VMEM((PAIRS, 2, 256), f32),
                pltpu.VMEM((PAIRS, 1, 128), f32),
                pltpu.VMEM((2, PAIRS, 128, 256), bf16),
                pltpu.VMEM((2, PAIRS, 256, 256), bf16),
                pltpu.VMEM((2, PAIRS, 256, 256), bf16),
                pltpu.VMEM((2, PAIRS, 128, 128), bf16),
                pltpu.VMEM((2, PAIRS, 2, 256), f32),
                pltpu.VMEM((2, PAIRS, 1, 128), f32),
                pltpu.VMEM((2, PAIRS, 64, 128), bf16),
                pltpu.VMEM((1024, 3072), bf16),
                pltpu.VMEM((3072, 1152), bf16),
                pltpu.VMEM((1024, 1152), bf16),
                pltpu.VMEM((1024, 128), f32),
                pltpu.SemaphoreType.DMA((pieces,)),
            ],
        ),
        compiler_params=pltpu.CompilerParams(
            dimension_semantics=("arbitrary",), vmem_limit_bytes=32 << 20
        ),
        name="layer",
    )(offsets, *tokens, *weights, rwt, rbias, w1, w2, b1, b2, gain)


DP = ("yl", "z", "c")
SEQ = ("x", "yh")
swap = [(0, 1), (1, 0)]


def ring(size, step):
    return [(i, (i + step) % size) for i in range(size)]


def after(value, others):
    return lax.optimization_barrier((value, others))[0]


def on_device(
    frames,
    proj_weight,
    rate_weight,
    rate_bias,
    init_weights,
    init_bias_hidden,
    init_bias_out,
    out_gain,
):
    x, yh, yl, z, c = (lax.axis_index(name) for name in ("x", "yh", "yl", "z", "c"))

    mine = lax.dynamic_index_in_dim(frames, yh, 0, keepdims=False)
    sent = lax.dynamic_index_in_dim(frames, 1 - yh, 0, keepdims=False)
    theirs = lax.ppermute(sent, "yh", swap)
    below = lax.ppermute(mine, "x", ring(4, 1))
    above = lax.ppermute(mine, "x", ring(4, -1))
    below2 = lax.ppermute(jnp.concatenate([below[:64], theirs]), "x", ring(4, 1))
    above2 = lax.ppermute(jnp.concatenate([above[64:], theirs]), "x", ring(4, -1))
    below3 = lax.ppermute(below2[64:128], "x", ring(4, 1))
    above3 = lax.ppermute(above2[128:], "x", ring(4, -1))
    tokens = [mine, below, above, below2, above2, theirs, below3, above3]

    part = jnp.concatenate(
        [lax.dynamic_slice(proj_weight, (0, i * 1536 + x * 384), (96, 384)) for i in range(3)], axis=1
    )
    up = down = jnp.concatenate([part, lax.ppermute(part, "yl", swap)])
    blocks = [up]
    for step in range(3):
        if step == 1:
            up, down = after((up, down), (below, above, theirs))
        up = lax.ppermute(up, "z", ring(8, 1))
        down = lax.ppermute(down, "z", ring(8, -1))
        blocks += [up, down]
    near = jnp.concatenate(blocks)
    up, down, near = after((up, down, near), (below2, above2))
    up = lax.ppermute(up[:96], "z", ring(8, 1))
    down = lax.ppermute(down[96:], "z", ring(8, -1))
    far = jnp.concatenate([up, down])
    weights = [near, far, lax.ppermute(near, "c", swap), lax.ppermute(far, "c", swap)]

    dx = np.tile(np.array([0, -1, 1, 2, 2]), 2)
    other_slab = np.repeat([0, 1], 5)
    late_half = np.tile(np.array([0, 0, 0, 0, 64]), 2)
    slab = (x + dx) % 4 * 2 + (yh + other_slab) % 2
    dz = np.concatenate([np.tile(np.repeat([0, -1, 1, -2, 2, -3, 3], 2), 2), np.full(4, 4)])
    other_row = np.tile(np.array([0, 1]), 16)
    other_core = np.concatenate([np.repeat([0, 1], 14), np.repeat([0, 1], 2)])
    block = ((yl + other_row) % 2 * 8 + (z + dz) % 8) * 2 + (c + other_core) % 2
    offsets = jnp.concatenate([slab * 128 + late_half, block * 96]).astype(jnp.int32)

    rate_columns = jnp.pad(lax.dynamic_slice(rate_weight, (0, x * 6), (3072, 6)), ((0, 0), (0, 122)))
    rate_offset = jnp.pad(lax.dynamic_slice(rate_bias, (x * 6,), (6,)), (0, 122)).reshape(1, 128)
    pair_weights = lax.dynamic_slice(init_weights, (0, x * 6, 0, 0), (2, 6, 64, 256))
    pair_weights = pair_weights.reshape(2, PAIRS, 128, 256)
    hidden_bias = lax.dynamic_slice(init_bias_hidden, (x * 6, 0), (6, 256)).reshape(PAIRS, 2, 256)
    out_bias = lax.dynamic_slice(init_bias_out, (x * 6, 0), (6, 64)).reshape(PAIRS, 1, 128)
    gain = lax.dynamic_slice(out_gain, (x * 384,), (384,)).reshape(1, 384)
    result = layer(
        offsets, tokens, weights, rate_columns, rate_offset,
        pair_weights[0], pair_weights[1], hidden_bias, out_bias, gain,
    )
    result = lax.all_to_all(result.reshape(8, 128, 384), SEQ, 0, 0, tiled=True)
    return result.reshape(4, 2, 128, 384).transpose(1, 2, 0, 3).reshape(2, 128, 1536)


def solution(mesh):
    fine = Mesh(mesh.devices.reshape(4, 2, 2, 8, 2), ("x", "yh", "yl", "z", "c"))
    return jax.shard_map(
        on_device,
        mesh=fine,
        in_specs=(P(DP, SEQ, None), P(DP, None), P(), P(), P(), P(), P(), P()),
        out_specs=P(DP, SEQ, None),
        check_vma=False,
    )
```

time: 161 us -> 150 us (0.932); the launches traced: 158 us -> 149 us
  matrix products: 18.9 us -> 0 us
  between operations: 13.5 us -> 0.36 us
  starting transfers between devices: 16.6 us -> 25.4 us
  waiting for transfers between devices: 36.1 us -> 43.9 us
  local copies, waits for them, and re-layouts: 22 us -> 25.3 us
    dot_general x2 -> x0, matrix products: 18.9 us -> none  [the longest x1 13.5 us: on_device(): projected = jnp.dot(tokens, weight, preferred_element_type=f32).astype(bf16)]
    ppermute x8 -> x17, waiting for transfers between devices: 28.2 us -> 41.3 us  [the longest x3 19.4 us: on_device(): up = lax.ppermute(up, 'z', ring(8, 1))]
    ppermute x8 -> x17, starting transfers between devices: 13.4 us -> 22.5 us  [the longest x3 10.1 us: on_device(): up = lax.ppermute(up, 'z', ring(8, 1))]
    all_gather x1 -> x0, waiting for transfers between devices: 7.35 us -> none  [on_device(): weight = lax.all_gather(weight.reshape(96, 1152), DP, axis=0, tiled=True)]
    slice x4 -> x6, local copies, waits for them, and re-layouts: 0.11 us -> 5.5 us  [the longest x1 1.79 us: on_device(): above3 = lax.ppermute(above2[128:], 'x', ring(4, -1))]
    reshape x1, local copies, waits for them, and re-layouts: 2.46 us -> 0.01 us  [on_device(): jnp.pad(lax.dynamic_slice(rate_bias, (x * 6,), (6,)), (0, 122))]
    ppermute x1, waiting for transfers between devices: 0.45 us -> 2.57 us  [on_device(): theirs = lax.ppermute(sent, 'yh', swap)]
    unnamed x16 -> x60, local copies, waits for them, and re-layouts: 10.4 us -> 9.69 us
  transfers between devices with their start and end apart: 10 -> 18, of which waited for: 6 -> 9; matrix products, arithmetic and copies ran while one was open for 15% -> 10% of each run, Pallas kernels for 0% -> 0%
where the time goes in v2:
time: 150 us; the launch traced here: 149 us
  waiting for transfers between devices  43.9 us (29%)
  Pallas kernels  33.1 us (22%)
  starting transfers between devices  25.4 us (17%)
  local copies, waits for them, and re-layouts  25.3 us (17%)
  blocking collectives  20 us (13%)
    pallas_call x1, Pallas kernels, layer(): pl.pallas_call(layer_kernel, out_shape=jax.ShapeDtypeStruct((1024, 384),...  33.1 us
    all_to_all x1, blocking collectives, on_device(): result = lax.all_to_all(result.reshape(8, 128, 384), SEQ, 0, 0, tiled=True)  20 us
    ppermute x3, waiting for transfers between devices, on_device(): up = lax.ppermute(up, 'z', ring(8, 1))  19.4 us
    ppermute x3, starting transfers between devices, on_device(): up = lax.ppermute(up, 'z', ring(8, 1))  10.1 us
    unnamed x60, local copies, waits for them, and re-layouts  9.69 us
    ppermute x1, waiting for transfers between devices, on_device(): down = lax.ppermute(down[96:], 'z', ring(8, -1))  7.49 us
    ppermute x3, waiting for transfers between devices, on_device(): down = lax.ppermute(down, 'z', ring(8, -1))  6.72 us
    ppermute x1, waiting for transfers between devices, on_device(): lax.ppermute(jnp.concatenate([above[64:], theirs]), 'x', ring(4, -1))  5.55 us
  transfers between devices with their start and end apart: 18, of which 9 were waited for; matrix products, arithmetic and copies ran while one was open for 10% of the time, Pallas kernels for 0%

profile of v2, /device:TPU:96, one launch (start us, length us, event | category | flops | bytes accessed | tf_op | source)
XLA Modules:
  0.0 149.1 jit_solution(8759135651677084763)
XLA Ops:
  1.8 1.6 %collective-permute-start.7 = (bf16[96,1152]{1,0:T(8,128)(2,1)}, bf16[96,1152]{1,0:T(8,128)(2,1)S(1)}, u32[]{:S(2)}, u32[]{:S(2)}) collective-permute-start(bf16[96,1152]{1,0:T(8,128)(2,1)} %get-tuple-element.25), channel_id=1, source_target_pairs={{0,16},{16,0},{1,17},{17,1},{2,18},{18,2},{3,19},{19,3},{4,20},{20... | collective-permute-start | bytes 663560 | tf_op jit(solution)/shard_map/ppermute | solution.py:306
  3.4 1.5 %dynamic-slice_bitcast_fusion = (bf16[128,3072]{1,0:T(8,128)(2,1)S(1)}, bf16[128,3072]{1,0:T(8,128)(2,1)S(1)}) fusion(bf16[2,128,3072]{2,1,0:T(8,128)(2,1)} %param.14, s32[]{:T(128)S(6)} %select_n.57, s32[]{:T(128)S(6)} %select_n.56), kind=kLoop, calls=%fused_computation.3 | loop fusion | bytes 3145736 | tf_op jit(solution)/shard_map/jit(dynamic_index_in_dim)/squeeze | solution.py:293
  4.9 2.8 %collective-permute-start.1 = (bf16[128,3072]{1,0:T(8,128)(2,1)S(1)}, bf16[128,3072]{1,0:T(8,128)(2,1)S(1)}, u32[]{:S(2)}, u32[]{:S(2)}) collective-permute-start(bf16[128,3072]{1,0:T(8,128)(2,1)S(1)} %get-tuple-element.18.refs_0_), channel_id=1, source_target_pairs={{0,192},{64,0},{128,64},{192,128},{1,193},{65,1},{129,65},{193,129... | collective-permute-start | bytes 2359304 | tf_op jit(solution)/shard_map/ppermute | solution.py:296
  7.7 2.9 %collective-permute-start.2 = (bf16[128,3072]{1,0:T(8,128)(2,1)S(1)}, bf16[128,3072]{1,0:T(8,128)(2,1)S(1)}, u32[]{:S(2)}, u32[]{:S(2)}) collective-permute-start(bf16[128,3072]{1,0:T(8,128)(2,1)S(1)} %get-tuple-element.17), channel_id=1, source_target_pairs={{0,32},{32,0},{1,33},{33,1},{2,34},{34,2},{3,35},{35,3},{4,36},{36... | collective-permute-start | bytes 2359304 | tf_op jit(solution)/shard_map/ppermute | solution.py:294
  10.7 3.2 %collective-permute-start.8 = (bf16[192,1152]{1,0:T(8,128)(2,1)S(1)}, bf16[192,1152]{1,0:T(8,128)(2,1)S(1)}, u32[]{:S(2)}, u32[]{:S(2)}) collective-permute-start(bf16[192,1152]{1,0:T(8,128)(2,1)S(1)} %pad_maximum_fusion.2), channel_id=1, source_target_pairs={{0,2},{2,4},{4,6},{6,8},{8,10},{10,12},{12,14},{14,0},{1,3},{3,5},... | collective-permute-start | bytes 1327112 | tf_op jit(solution)/shard_map/ppermute | solution.py:311
  13.9 8.6 %collective-permute-done.8 = bf16[192,1152]{1,0:T(8,128)(2,1)S(1)} collective-permute-done((bf16[192,1152]{1,0:T(8,128)(2,1)S(1)}, bf16[192,1152]{1,0:T(8,128)(2,1)S(1)}, u32[]{:S(2)}, u32[]{:S(2)}) %collective-permute-start.8) | collective-permute-done | bytes 442400 | tf_op jit(solution)/shard_map/ppermute | solution.py:311
  22.5 3.4 %collective-permute-done.9 = bf16[192,1152]{1,0:T(8,128)(2,1)S(1)} collective-permute-done((bf16[192,1152]{1,0:T(8,128)(2,1)S(1)}, bf16[192,1152]{1,0:T(8,128)(2,1)S(1)}, u32[]{:S(2)}, u32[]{:S(2)}) %collective-permute-start.9) | collective-permute-done | bytes 442400 | tf_op jit(solution)/shard_map/ppermute | solution.py:312
  25.9 2.6 %collective-permute-done.2.refs_5_ = bf16[128,3072]{1,0:T(8,128)(2,1)S(1)} collective-permute-done((bf16[128,3072]{1,0:T(8,128)(2,1)S(1)}, bf16[128,3072]{1,0:T(8,128)(2,1)S(1)}, u32[]{:S(2)}, u32[]{:S(2)}) %collective-permute-start.2) | collective-permute-done | bytes 786464 | tf_op jit(solution)/shard_map/ppermute | solution.py:294
  28.5 3.2 %collective-permute-start.10 = (bf16[192,1152]{1,0:T(8,128)(2,1)S(1)}, bf16[192,1152]{1,0:T(8,128)(2,1)S(1)}, u32[]{:S(2)}, u32[]{:S(2)}) collective-permute-start(bf16[192,1152]{1,0:T(8,128)(2,1)S(1)} %collective-permute-done.8), channel_id=1, source_target_pairs={{0,2},{2,4},{4,6},{6,8},{8,10},{10,12},{12,14},{14,0},{1,3},{3,5},... | collective-permute-start | bytes 1327112 | tf_op jit(solution)/shard_map/ppermute | solution.py:311
  33.8 2.8 %collective-permute-start.4 = (bf16[192,3072]{1,0:T(8,128)(2,1)S(1)}, bf16[192,3072]{1,0:T(8,128)(2,1)S(1)}, u32[]{:S(2)}, u32[]{:S(2)}) collective-permute-start(bf16[192,3072]{1,0:T(8,128)(2,1)S(1)} %get-tuple-element.22), channel_id=1, source_target_pairs={{0,192},{64,0},{128,64},{192,128},{1,193},{65,1},{129,65},{193,129... | collective-permute-start | bytes 3538952 | tf_op jit(solution)/shard_map/ppermute | solution.py:298
  36.7 3.4 %collective-permute-done.10 = bf16[192,1152]{1,0:T(8,128)(2,1)S(1)} collective-permute-done((bf16[192,1152]{1,0:T(8,128)(2,1)S(1)}, bf16[192,1152]{1,0:T(8,128)(2,1)S(1)}, u32[]{:S(2)}, u32[]{:S(2)}) %collective-permute-start.10) | collective-permute-done | bytes 442400 | tf_op jit(solution)/shard_map/ppermute | solution.py:311
  40.1 3.7 %collective-permute-start.11 = (bf16[192,1152]{1,0:T(8,128)(2,1)S(1)}, bf16[192,1152]{1,0:T(8,128)(2,1)S(1)}, u32[]{:S(2)}, u32[]{:S(2)}) collective-permute-start(bf16[192,1152]{1,0:T(8,128)(2,1)S(1)} %collective-permute-done.10), channel_id=1, source_target_pairs={{0,2},{2,4},{4,6},{6,8},{8,10},{10,12},{12,14},{14,0},{1,3},{3,5},... | collective-permute-start | bytes 1327112 | tf_op jit(solution)/shard_map/ppermute | solution.py:311
  43.9 7.4 %collective-permute-done.11 = bf16[192,1152]{1,0:T(8,128)(2,1)S(1)} collective-permute-done((bf16[192,1152]{1,0:T(8,128)(2,1)S(1)}, bf16[192,1152]{1,0:T(8,128)(2,1)S(1)}, u32[]{:S(2)}, u32[]{:S(2)}) %collective-permute-start.11) | collective-permute-done | bytes 442400 | tf_op jit(solution)/shard_map/ppermute | solution.py:311
  51.4 3.4 %collective-permute-done.13 = bf16[192,1152]{1,0:T(8,128)(2,1)S(1)} collective-permute-done((bf16[192,1152]{1,0:T(8,128)(2,1)S(1)}, bf16[192,1152]{1,0:T(8,128)(2,1)S(1)}, u32[]{:S(2)}, u32[]{:S(2)}) %collective-permute-start.13) | collective-permute-done | bytes 442400 | tf_op jit(solution)/shard_map/ppermute | solution.py:312
  54.8 5.6 %collective-permute-done.4.refs_4_ = bf16[192,3072]{1,0:T(8,128)(2,1)S(1)} collective-permute-done((bf16[192,3072]{1,0:T(8,128)(2,1)S(1)}, bf16[192,3072]{1,0:T(8,128)(2,1)S(1)}, u32[]{:S(2)}, u32[]{:S(2)}) %collective-permute-start.4) | collective-permute-done | bytes 1179680 | tf_op jit(solution)/shard_map/ppermute | solution.py:298
  60.4 1.0 copy-done.5
  61.4 2.2 %collective-permute-done.3.refs_3_ = bf16[192,3072]{1,0:T(8,128)(2,1)S(1)} collective-permute-done((bf16[192,3072]{1,0:T(8,128)(2,1)S(1)}, bf16[192,3072]{1,0:T(8,128)(2,1)S(1)}, u32[]{:S(2)}, u32[]{:S(2)}) %collective-permute-start.3) | collective-permute-done | bytes 1179680 | tf_op jit(solution)/shard_map/ppermute | solution.py:297
  63.6 1.0 copy-done.7
  66.4 3.0 %collective-permute-start.14 = (bf16[96,1152]{1,0:T(8,128)(2,1)S(1)}, bf16[96,1152]{1,0:T(8,128)(2,1)S(1)}, u32[]{:S(2)}, u32[]{:S(2)}) collective-permute-start(bf16[96,1152]{1,0:T(8,128)(2,1)S(1)} %slice.30), channel_id=1, source_target_pairs={{0,2},{2,4},{4,6},{6,8},{8,10},{10,12},{12,14},{14,0},{1,3},{3,5},... | collective-permute-start | bytes 663560 | tf_op jit(solution)/shard_map/ppermute | solution.py:316
  69.5 1.8 %slice.37 = bf16[64,3072]{1,0:T(8,128)(2,1)} slice(bf16[192,3072]{1,0:T(8,128)(2,1)} %copy-done.5), slice={[128:192], [0:3072]} | slice | bytes 786432 | tf_op jit(solution)/shard_map/slice | solution.py:300
  71.2 1.3 collective-permute-start.6
  72.6 1.8 %slice.36 = bf16[64,3072]{1,0:T(8,128)(2,1)} slice(bf16[192,3072]{1,0:T(8,128)(2,1)} %copy-done.7), slice={[64:128], [0:3072]} | slice | bytes 786432 | tf_op jit(solution)/shard_map/slice | solution.py:299
  76.8 7.5 %collective-permute-done.15 = bf16[96,1152]{1,0:T(8,128)(2,1)S(1)} collective-permute-done((bf16[96,1152]{1,0:T(8,128)(2,1)S(1)}, bf16[96,1152]{1,0:T(8,128)(2,1)S(1)}, u32[]{:S(2)}, u32[]{:S(2)}) %collective-permute-start.15) | collective-permute-done | bytes 221216 | tf_op jit(solution)/shard_map/ppermute | solution.py:317
  86.6 1.3 copy.17
  87.9 1.4 pad.8.refs_12_
  89.5 1.2 constant_dynamic-slice_fusion.3
  90.7 1.3 copy-done.8
  92.0 1.1 copy-done.10
  93.1 1.1 copy-done.12
  94.3 33.1 %layer.1 = bf16[1024,384]{1,0:T(8,128)(2,1)S(1)} custom-call(s32[42]{0:T(128)S(1)} %pad_add_fusion.offset_ref, bf16[128,3072]{1,0:T(8,128)(2,1)S(1)} %copy-done.2, bf16[128,3072]{1,0:T(8,128)(2,1)S(1)} %copy-done.12, bf16[128,3072]{1,0:T(8,128)(2,1)S(1)} %copy-done.10, bf16[192,3072]{1,0:T(8,128)(2,1)S(1)} %copy-done.8, bf16[192,3072]{1,0:T(8,128)(2,1)S(1)} %copy-done.6, ...), custom_call_target="tpu_custom_call" | custom-call | tf_op jit(solution)/shard_map/layer/pallas_call | solution.py:224
  127.3 20.0 %all_to_all.5 = bf16[8,128,384]{2,1,0:T(8,128)(2,1)S(1)} all-to-all(bf16[8,128,384]{2,1,0:T(8,128)(2,1)S(1)} %bitcast.13), channel_id=1, replica_groups=mesh['x'=4,'yh'=2,'yl'=2,'z'=8,'c'=2] {'x','yh'}, dimensions={0} | all-to-all | bytes 1572864 | tf_op jit(solution)/shard_map/all_to_all | solution.py:342
  147.9 1.2 reshape.32
  (95 shorter events, 11.5 us)
Async XLA Ops:
  0.0 65.4 %copy-start = (bf16[3072,24]{0,1:T(8,128)(2,1)S(1)}, bf16[3072,24]{0,1:T(8,128)(2,1)}, u32[]{:S(2)}) copy-start(bf16[3072,24]{0,1:T(8,128)(2,1)} %param.16) | copy-start | bytes 442372
  1.8 8.8 %collective-permute-start.7 = (bf16[96,1152]{1,0:T(8,128)(2,1)}, bf16[96,1152]{1,0:T(8,128)(2,1)S(1)}, u32[]{:S(2)}, u32[]{:S(2)}) collective-permute-start(bf16[96,1152]{1,0:T(8,128)(2,1)} %get-tuple-element.25), channel_id=1, source_target_pairs={{0,16},{16,0},{1,17},{17,1},{2,18},{18,2},{3,19},{19,3},{4,20},{20... | collective-permute-start | bytes 663560 | tf_op jit(solution)/shard_map/ppermute | solution.py:306
  3.3 7.3 %copy-start.16 = (bf16[96,384]{1,0:T(8,128)(2,1)S(1)}, bf16[96,384]{1,0:T(8,128)(2,1)}, u32[]{:S(2)}) copy-start(bf16[96,384]{1,0:T(8,128)(2,1)} %copy-done.15) | copy-start | bytes 221188
  3.4 7.3 %copy-start.18 = (bf16[96,384]{1,0:T(8,128)(2,1)S(1)}, bf16[96,384]{1,0:T(8,128)(2,1)}, u32[]{:S(2)}) copy-start(bf16[96,384]{1,0:T(8,128)(2,1)} %copy-done.17) | copy-start | bytes 221188
  4.9 17.7 %copy-start.1 = (bf16[128,3072]{1,0:T(8,128)(2,1)}, bf16[128,3072]{1,0:T(8,128)(2,1)S(1)}, u32[]{:S(2)}) copy-start(bf16[128,3072]{1,0:T(8,128)(2,1)S(1)} %get-tuple-element.18.refs_0_) | copy-start | bytes 2359300
  4.9 23.6 %collective-permute-start.1 = (bf16[128,3072]{1,0:T(8,128)(2,1)S(1)}, bf16[128,3072]{1,0:T(8,128)(2,1)S(1)}, u32[]{:S(2)}, u32[]{:S(2)}) collective-permute-start(bf16[128,3072]{1,0:T(8,128)(2,1)S(1)} %get-tuple-element.18.refs_0_), channel_id=1, source_target_pairs={{0,192},{64,0},{128,64},{192,128},{1,193},{65,1},{129,65},{193,129... | collective-permute-start | bytes 2359304 | tf_op jit(solution)/shard_map/ppermute | solution.py:296
  7.7 20.8 %collective-permute-start = (bf16[128,3072]{1,0:T(8,128)(2,1)S(1)}, bf16[128,3072]{1,0:T(8,128)(2,1)S(1)}, u32[]{:S(2)}, u32[]{:S(2)}) collective-permute-start(bf16[128,3072]{1,0:T(8,128)(2,1)S(1)} %get-tuple-element.18.refs_0_), channel_id=1, source_target_pairs={{0,64},{64,128},{128,192},{192,0},{1,65},{65,129},{129,193},{193,1... | collective-permute-start | bytes 2359304 | tf_op jit(solution)/shard_map/ppermute | solution.py:295
  7.7 20.7 %collective-permute-start.2 = (bf16[128,3072]{1,0:T(8,128)(2,1)S(1)}, bf16[128,3072]{1,0:T(8,128)(2,1)S(1)}, u32[]{:S(2)}, u32[]{:S(2)}) collective-permute-start(bf16[128,3072]{1,0:T(8,128)(2,1)S(1)} %get-tuple-element.17), channel_id=1, source_target_pairs={{0,32},{32,0},{1,33},{33,1},{2,34},{34,2},{3,35},{35,3},{4,36},{36... | collective-permute-start | bytes 2359304 | tf_op jit(solution)/shard_map/ppermute | solution.py:294
  10.7 11.8 %collective-permute-start.8 = (bf16[192,1152]{1,0:T(8,128)(2,1)S(1)}, bf16[192,1152]{1,0:T(8,128)(2,1)S(1)}, u32[]{:S(2)}, u32[]{:S(2)}) collective-permute-start(bf16[192,1152]{1,0:T(8,128)(2,1)S(1)} %pad_maximum_fusion.2), channel_id=1, source_target_pairs={{0,2},{2,4},{4,6},{6,8},{8,10},{10,12},{12,14},{14,0},{1,3},{3,5},... | collective-permute-start | bytes 1327112 | tf_op jit(solution)/shard_map/ppermute | solution.py:311
  13.9 12.0 %collective-permute-start.9 = (bf16[192,1152]{1,0:T(8,128)(2,1)S(1)}, bf16[192,1152]{1,0:T(8,128)(2,1)S(1)}, u32[]{:S(2)}, u32[]{:S(2)}) collective-permute-start(bf16[192,1152]{1,0:T(8,128)(2,1)S(1)} %pad_maximum_fusion.2), channel_id=1, source_target_pairs={{0,14},{2,0},{4,2},{6,4},{8,6},{10,8},{12,10},{14,12},{1,15},{3,1}... | collective-permute-start | bytes 1327112 | tf_op jit(solution)/shard_map/ppermute | solution.py:312
  28.5 8.3 %copy-start.3 = (bf16[128,3072]{1,0:T(8,128)(2,1)}, bf16[128,3072]{1,0:T(8,128)(2,1)S(1)}, u32[]{:S(2)}) copy-start(bf16[128,3072]{1,0:T(8,128)(2,1)S(1)} %collective-permute-done.2.refs_5_) | copy-start | bytes 2359300
  28.5 11.7 %collective-permute-start.10 = (bf16[192,1152]{1,0:T(8,128)(2,1)S(1)}, bf16[192,1152]{1,0:T(8,128)(2,1)S(1)}, u32[]{:S(2)}, u32[]{:S(2)}) collective-permute-start(bf16[192,1152]{1,0:T(8,128)(2,1)S(1)} %collective-permute-done.8), channel_id=1, source_target_pairs={{0,2},{2,4},{4,6},{6,8},{8,10},{10,12},{12,14},{14,0},{1,3},{3,5},... | collective-permute-start | bytes 1327112 | tf_op jit(solution)/shard_map/ppermute | solution.py:311
  31.7 12.2 %collective-permute-start.12 = (bf16[192,1152]{1,0:T(8,128)(2,1)S(1)}, bf16[192,1152]{1,0:T(8,128)(2,1)S(1)}, u32[]{:S(2)}, u32[]{:S(2)}) collective-permute-start(bf16[192,1152]{1,0:T(8,128)(2,1)S(1)} %collective-permute-done.9), channel_id=1, source_target_pairs={{0,14},{2,0},{4,2},{6,4},{8,6},{10,8},{12,10},{14,12},{1,15},{3,1}... | collective-permute-start | bytes 1327112 | tf_op jit(solution)/shard_map/ppermute | solution.py:312
  33.8 31.6 %copy-start.22 = (s32[10]{0:T(128)S(1)}, s32[10]{0:T(128)}, u32[]{:S(2)}) copy-start(s32[10]{0:T(128)} %constant.125.clone) | copy-start | bytes 124
  33.8 31.6 %copy-start.23 = (s32[10]{0:T(128)S(1)}, s32[10]{0:T(128)}, u32[]{:S(2)}) copy-start(s32[10]{0:T(128)} %constant.121.clone) | copy-start | bytes 124
  33.8 31.6 %copy-start.24 = (s32[10]{0:T(128)S(1)}, s32[10]{0:T(128)}, u32[]{:S(2)}) copy-start(s32[10]{0:T(128)} %constant.120.clone) | copy-start | bytes 124
  33.8 35.6 %copy-start.19 = (s32[32]{0:T(128)S(1)}, s32[32]{0:T(128)}, u32[]{:S(2)}) copy-start(s32[32]{0:T(128)} %constant.124.clone) | copy-start | bytes 388
  33.8 35.6 %copy-start.20 = (s32[32]{0:T(128)S(1)}, s32[32]{0:T(128)}, u32[]{:S(2)}) copy-start(s32[32]{0:T(128)} %constant.123.clone) | copy-start | bytes 388
  33.8 35.6 %copy-start.21 = (s32[32]{0:T(128)S(1)}, s32[32]{0:T(128)}, u32[]{:S(2)}) copy-start(s32[32]{0:T(128)} %constant.122.clone) | copy-start | bytes 388
  33.8 26.5 %collective-permute-start.4 = (bf16[192,3072]{1,0:T(8,128)(2,1)S(1)}, bf16[192,3072]{1,0:T(8,128)(2,1)S(1)}, u32[]{:S(2)}, u32[]{:S(2)}) collective-permute-start(bf16[192,3072]{1,0:T(8,128)(2,1)S(1)} %get-tuple-element.22), channel_id=1, source_target_pairs={{0,192},{64,0},{128,64},{192,128},{1,193},{65,1},{129,65},{193,129... | collective-permute-start | bytes 3538952 | tf_op jit(solution)/shard_map/ppermute | solution.py:298
  36.7 26.9 %collective-permute-start.3 = (bf16[192,3072]{1,0:T(8,128)(2,1)S(1)}, bf16[192,3072]{1,0:T(8,128)(2,1)S(1)}, u32[]{:S(2)}, u32[]{:S(2)}) collective-permute-start(bf16[192,3072]{1,0:T(8,128)(2,1)S(1)} %get-tuple-element.23), channel_id=1, source_target_pairs={{0,64},{64,128},{128,192},{192,0},{1,65},{65,129},{129,193},{193,1... | collective-permute-start | bytes 3538952 | tf_op jit(solution)/shard_map/ppermute | solution.py:297
  40.1 11.2 %collective-permute-start.11 = (bf16[192,1152]{1,0:T(8,128)(2,1)S(1)}, bf16[192,1152]{1,0:T(8,128)(2,1)S(1)}, u32[]{:S(2)}, u32[]{:S(2)}) collective-permute-start(bf16[192,1152]{1,0:T(8,128)(2,1)S(1)} %collective-permute-done.10), channel_id=1, source_target_pairs={{0,2},{2,4},{4,6},{6,8},{8,10},{10,12},{12,14},{14,0},{1,3},{3,5},... | collective-permute-start | bytes 1327112 | tf_op jit(solution)/shard_map/ppermute | solution.py:311
  43.8 10.9 %collective-permute-start.13 = (bf16[192,1152]{1,0:T(8,128)(2,1)S(1)}, bf16[192,1152]{1,0:T(8,128)(2,1)S(1)}, u32[]{:S(2)}, u32[]{:S(2)}) collective-permute-start(bf16[192,1152]{1,0:T(8,128)(2,1)S(1)} %collective-permute-done.12), channel_id=1, source_target_pairs={{0,14},{2,0},{4,2},{6,4},{8,6},{10,8},{12,10},{14,12},{1,15},{3,1}... | collective-permute-start | bytes 1327112 | tf_op jit(solution)/shard_map/ppermute | solution.py:312
  43.9 41.8 %copy-start.25 = (f32[24]{0:T(128)S(1)}, f32[24]{0:T(128)}, u32[]{:S(2)}) copy-start(f32[24]{0:T(128)} %param.17) | copy-start | bytes 292
  51.4 12.2 %copy-start.14 = (bf16[192,1152]{1,0:T(8,128)(2,1)}, bf16[192,1152]{1,0:T(8,128)(2,1)S(1)}, u32[]{:S(2)}) copy-start(bf16[192,1152]{1,0:T(8,128)(2,1)S(1)} %collective-permute-done.11) | copy-start | bytes 1327108
  54.8 8.8 %copy-start.13 = (bf16[192,1152]{1,0:T(8,128)(2,1)}, bf16[192,1152]{1,0:T(8,128)(2,1)S(1)}, u32[]{:S(2)}) copy-start(bf16[192,1152]{1,0:T(8,128)(2,1)S(1)} %collective-permute-done.13) | copy-start | bytes 1327108
  64.6 26.1 %collective-permute-start.16 = (bf16[1344,1152]{1,0:T(8,128)(2,1)S(1)}, bf16[1344,1152]{1,0:T(8,128)(2,1)}, u32[]{:S(2)}, u32[]{:S(2)}) collective-permute-start(bf16[1344,1152]{1,0:T(8,128)(2,1)S(1)} %constant_dynamic-update-slice_fusion.refs_8_), channel_id=1, source_target_pairs={{0,1},{1,0},{2,3},{3,2},{4,5},{5,4},{6,7},{7,6},{8,9},{9,8},{10,11... | collective-permute-start | bytes 9289736 | tf_op jit(solution)/shard_map/ppermute | solution.py:319
  66.4 9.7 %collective-permute-start.14 = (bf16[96,1152]{1,0:T(8,128)(2,1)S(1)}, bf16[96,1152]{1,0:T(8,128)(2,1)S(1)}, u32[]{:S(2)}, u32[]{:S(2)}) collective-permute-start(bf16[96,1152]{1,0:T(8,128)(2,1)S(1)} %slice.30), channel_id=1, source_target_pairs={{0,2},{2,4},{4,6},{6,8},{8,10},{10,12},{12,14},{14,0},{1,3},{3,5},... | collective-permute-start | bytes 663560 | tf_op jit(solution)/shard_map/ppermute | solution.py:316
  71.2 19.4 %collective-permute-start.6 = (bf16[64,3072]{1,0:T(8,128)(2,1)}, bf16[64,3072]{1,0:T(8,128)(2,1)}, u32[]{:S(2)}, u32[]{:S(2)}) collective-permute-start(bf16[64,3072]{1,0:T(8,128)(2,1)} %slice.37), channel_id=1, source_target_pairs={{0,192},{64,0},{128,64},{192,128},{1,193},{65,1},{129,65},{193,129... | collective-permute-start | bytes 1179656 | tf_op jit(solution)/shard_map/ppermute | solution.py:300
  74.3 16.3 %collective-permute-start.5 = (bf16[64,3072]{1,0:T(8,128)(2,1)}, bf16[64,3072]{1,0:T(8,128)(2,1)}, u32[]{:S(2)}, u32[]{:S(2)}) collective-permute-start(bf16[64,3072]{1,0:T(8,128)(2,1)} %slice.36), channel_id=1, source_target_pairs={{0,64},{64,128},{128,192},{192,0},{1,65},{65,129},{129,193},{193,1... | collective-permute-start | bytes 1179656 | tf_op jit(solution)/shard_map/ppermute | solution.py:299
  76.0 8.3 %collective-permute-start.15 = (bf16[96,1152]{1,0:T(8,128)(2,1)S(1)}, bf16[96,1152]{1,0:T(8,128)(2,1)S(1)}, u32[]{:S(2)}, u32[]{:S(2)}) collective-permute-start(bf16[96,1152]{1,0:T(8,128)(2,1)S(1)} %slice.31), channel_id=1, source_target_pairs={{0,14},{2,0},{4,2},{6,4},{8,6},{10,8},{12,10},{14,12},{1,15},{3,1}... | collective-permute-start | bytes 663560 | tf_op jit(solution)/shard_map/ppermute | solution.py:317
  85.0 5.7 %collective-permute-start.17 = (bf16[192,1152]{1,0:T(8,128)(2,1)}, bf16[192,1152]{1,0:T(8,128)(2,1)}, u32[]{:S(2)}, u32[]{:S(2)}) collective-permute-start(bf16[192,1152]{1,0:T(8,128)(2,1)} %constant_dynamic-update-slice_fusion.8.refs_9_), channel_id=1, source_target_pairs={{0,1},{1,0},{2,3},{3,2},{4,5},{5,4},{6,7},{7,6},{8,9},{9,8},{10,11... | collective-permute-start | bytes 1327112 | tf_op jit(solution)/shard_map/ppermute | solution.py:319
  (12 other events, 17.2 us)

commit v3 on v2

--- a/solution.py
+++ b/solution.py
@@ -2,7 +2,6 @@
 
 import jax
 import jax.numpy as jnp
-import numpy as np
 from jax import lax
 from jax.experimental import pallas as pl
 from jax.experimental.pallas import tpu as pltpu
@@ -33,62 +32,85 @@
     return 0.5 + 0.5 * jnp.tanh(z * (root_scale + (root_scale * cubic) * (z * z)))
 
 
+NT = 10
+NW = 2
 TOKEN_PIECES = [
-    (0, 0, 128), (1, 0, 128), (2, 0, 128), (3, 0, 64), (4, 0, 64),
-    (5, 0, 128), (3, 64, 128), (4, 64, 128), (6, 0, 64), (7, 0, 64),
+    (i, j * 64, 64) for i, count in enumerate((2, 2, 2, 2, 2, 2, 1, 1, 1, 1)) for j in range(count)
 ]
-NT = 8
-WEIGHT_PIECES = [(h, i * 96, 96) for h in (0, 2) for i in range(14)] + [
-    (h, i * 96, 96) for h in (1, 3) for i in range(2)
-]
-
-
-def layer_kernel(offset_ref, *refs):
+WEIGHT_PIECES = [(h, i * 96, 96) for h in range(NW) for i in range(16)]
+
+
+def layer_kernel(place_ref, *refs):
     token_refs = refs[:NT]
-    weight_refs = refs[NT : NT + 4]
-    rwt_ref, rbias_ref, w1i, w2i, b1i, b2i, gain_ref, out_ref = refs[NT + 4 : NT + 12]
+    weight_refs = refs[NT : NT + NW]
+    rate_t_ref, rate_bias_ref, init_ref, hidden_ref, outer_ref, gain_ref, out_ref = refs[NT + NW : NT + NW + 7]
     (w1s, w2s, b1s, b2s, qm_s, wh_s, wx_s, h2_s, b1_s, b2_s, q_s,
-     tokens_s, weight_s, proj_s, rate_s, sems) = refs[NT + 12 :]
+     tokens_s, weight_s, proj_s, rate_s, sems) = refs[NT + NW + 7 :]
     slab = pl.program_id(0)
+    x, yh, yl, z, c = (place_ref[i] for i in range(5))
 
     @pl.when(slab == 0)
     def _():
         copies = []
         for i, (ref, start, size) in enumerate(WEIGHT_PIECES):
-            at = pl.multiple_of(offset_ref[len(TOKEN_PIECES) + i], 32)
+            block = ((yl + i % 2) % 2 * 8 + i % 16 // 2) * 2 + (c + ref) % 2
+            at = pl.multiple_of(block * 96, 96)
             copies.append(
                 pltpu.make_async_copy(
-                    weight_refs[ref].at[pl.ds(start, size)], weight_s.at[pl.ds(at, size)], sems.at[i]
+                    weight_refs[ref].at[pl.ds(start, size)],
+                    weight_s.at[pl.ds(at, size), pl.ds(0, 1152)],
+                    sems.at[i],
                 )
             )
         for i, (ref, start, size) in enumerate(TOKEN_PIECES):
-            at = pl.multiple_of(offset_ref[i], 64)
             copies.append(
                 pltpu.make_async_copy(
                     token_refs[ref].at[pl.ds(start, size)],
-                    tokens_s.at[pl.ds(at, size)],
+                    tokens_s.at[pl.ds(i * 64, size)],
                     sems.at[len(WEIGHT_PIECES) + i],
                 )
             )
         for copy in copies:
             copy.start()
-        w1s[...] = w1i[...]
-        w2s[...] = w2i[...]
-        b1s[...] = b1i[...]
-        b2s[...] = b2i[...]
-        for copy in copies:
+        first = x * 6
+        for p in range(PAIRS):
+            for j in range(2):
+                head = 2 * p + j
+                w1s[p, 64 * j : 64 * j + 64] = init_ref[0, head]
+                w2s[p, 64 * j : 64 * j + 64] = init_ref[1, head]
+                b1s[p, j : j + 1] = hidden_ref[pl.ds(first + head, 1), :]
+            b2s[p] = jnp.concatenate(
+                [outer_ref[pl.ds(first + 2 * p, 1), :], outer_ref[pl.ds(first + 2 * p + 1, 1), :]], axis=1
+            )
+        pick = lax.broadcasted_iota(jnp.int32, (24, 128), 0) == (
+            first + lax.broadcasted_iota(jnp.int32, (24, 128), 1)
+        )
+        pick = pick & (lax.broadcasted_iota(jnp.int32, (24, 128), 1) < 6)
+        weight_s[:, 1152:] = mm_tn(rate_t_ref[...], jnp.where(pick, 1.0, 0.0).astype(bf16)).astype(bf16)
+        lane = lax.broadcasted_iota(jnp.int32, (1, 128), 1)
+        rate_bias = jnp.zeros((1, 128), f32)
+        for j in range(6):
+            rate_bias = jnp.where(lane == j, rate_bias_ref[first + j], rate_bias)
+        for copy in copies[: len(WEIGHT_PIECES)]:
             copy.wait()
-
-        def project(i, carry):
-            rows = pl.ds(pl.multiple_of(i * 256, 256), 256)
-            for n in range(5):
-                cols = pl.ds(n * 256, 256 if n < 4 else 128)
+        for i in range(4):
+            for copy in copies[len(WEIGHT_PIECES) + 4 * i : len(WEIGHT_PIECES) + 4 * i + 4]:
+                copy.wait()
+            rows = pl.ds(i * 256, 256)
+            for n in range(4):
+                cols = pl.ds(n * 256, 256)
                 proj_s[rows, cols] = mm(tokens_s[rows, :], weight_s[:, cols]).astype(bf16)
-            logits = mm(tokens_s[rows, :], rwt_ref[...]) + rbias_ref[...]
-            rate_s[rows] = (1.0 / 20480.0) / (1.0 + jnp.exp(-logits))
-            return carry
-
-        lax.fori_loop(0, 4, project, 0)
+            rest = mm(tokens_s[rows, :], weight_s[:, 1024:])
+            proj_s[rows, 1024:] = rest[:, :128].astype(bf16)
+            rate_s[rows] = (1.0 / 20480.0) / (1.0 + jnp.exp(-(rest[:, 128:] + rate_bias)))
+
+    def first_row(half):
+        away = (slab // 2 - x + 4) % 4
+        near = jnp.where(away == 0, 0, jnp.where(away == 3, 2, 4)) + half
+        own = jnp.where(away == 2, 6 + 2 * half, near)
+        below, above = (7, 13) if half else (12, 9)
+        far = jnp.where(away == 3, below, jnp.where(away == 1, above, jnp.where(away == 0, 10, 14) + half))
+        return jnp.where(slab % 2 == yh, own, far) * MB
 
     low = lax.broadcasted_iota(jnp.int32, (64, 128), 1) < 64
 
@@ -102,7 +124,7 @@
         return jnp.where(low, x[:64], x[64:])
 
     def train(m):
-        rows = pl.ds(pl.multiple_of(slab * 128 + m * MB, MB), MB)
+        rows = pl.ds(pl.multiple_of(first_row(m), MB), MB)
         D = []
         for p in range(PAIRS):
             def part(c):
@@ -215,10 +237,11 @@
         weave(query(1, pl.multiple_of(slab * 128 + MB, MB)))
 
 
-def layer(offsets, tokens, weights, rwt, rbias, w1, w2, b1, b2, gain):
+def layer(place, tokens, weights, rate_t, rate_bias, init_weights, hidden, outer, gain):
     def whole(shape):
-        return pl.BlockSpec(shape, lambda i, offsets: (0,) * len(shape))
-
+        return pl.BlockSpec(shape, lambda i, place: (0,) * len(shape))
+
+    far = pl.BlockSpec(memory_space=pltpu.HBM)
     anywhere = pl.BlockSpec(memory_space=pl.ANY)
     pieces = len(TOKEN_PIECES) + len(WEIGHT_PIECES)
     return pl.pallas_call(
@@ -227,15 +250,15 @@
         grid_spec=pltpu.PrefetchScalarGridSpec(
             num_scalar_prefetch=1,
             grid=(8,),
-            in_specs=[anywhere] * (NT + 4)
+            in_specs=[far] * (NT + 1)
+            + [anywhere]
             + [
-                whole((3072, 128)),
-                whole((1, 128)),
-                whole((PAIRS, 128, 256)),
-                whole((PAIRS, 128, 256)),
-                whole((PAIRS, 2, 256)),
-                whole((PAIRS, 1, 128)),
-                whole((1, 384)),
+                whole((24, 3072)),
+                pl.BlockSpec(memory_space=pltpu.SMEM),
+                pl.BlockSpec((2, 6, 64, 256), lambda i, place: (0, place[0], 0, 0)),
+                whole((24, 256)),
+                whole((24, 64)),
+                pl.BlockSpec((1, 384), lambda i, place: (0, place[0])),
             ],
             out_specs=whole((1024, 384)),
             scratch_shapes=[
@@ -251,7 +274,7 @@
                 pltpu.VMEM((2, PAIRS, 1, 128), f32),
                 pltpu.VMEM((2, PAIRS, 64, 128), bf16),
                 pltpu.VMEM((1024, 3072), bf16),
-                pltpu.VMEM((3072, 1152), bf16),
+                pltpu.VMEM((3072, 1280), bf16),
                 pltpu.VMEM((1024, 1152), bf16),
                 pltpu.VMEM((1024, 128), f32),
                 pltpu.SemaphoreType.DMA((pieces,)),
@@ -261,7 +284,7 @@
             dimension_semantics=("arbitrary",), vmem_limit_bytes=32 << 20
         ),
         name="layer",
-    )(offsets, *tokens, *weights, rwt, rbias, w1, w2, b1, b2, gain)
+    )(place, *tokens, *weights, rate_t, rate_bias, init_weights, hidden, outer, gain)
 
 
 DP = ("yl", "z", "c")
@@ -289,55 +312,29 @@
 ):
     x, yh, yl, z, c = (lax.axis_index(name) for name in ("x", "yh", "yl", "z", "c"))
 
+    up, down = ring(4, 1), ring(4, -1)
+
+    part = jnp.concatenate(
+        [lax.dynamic_slice(proj_weight, (0, i * 1536 + x * 384), (96, 384)) for i in range(3)], axis=1
+    )
     mine = lax.dynamic_index_in_dim(frames, yh, 0, keepdims=False)
     sent = lax.dynamic_index_in_dim(frames, 1 - yh, 0, keepdims=False)
     theirs = lax.ppermute(sent, "yh", swap)
-    below = lax.ppermute(mine, "x", ring(4, 1))
-    above = lax.ppermute(mine, "x", ring(4, -1))
-    below2 = lax.ppermute(jnp.concatenate([below[:64], theirs]), "x", ring(4, 1))
-    above2 = lax.ppermute(jnp.concatenate([above[64:], theirs]), "x", ring(4, -1))
-    below3 = lax.ppermute(below2[64:128], "x", ring(4, 1))
-    above3 = lax.ppermute(above2[128:], "x", ring(4, -1))
-    tokens = [mine, below, above, below2, above2, theirs, below3, above3]
-
-    part = jnp.concatenate(
-        [lax.dynamic_slice(proj_weight, (0, i * 1536 + x * 384), (96, 384)) for i in range(3)], axis=1
-    )
-    up = down = jnp.concatenate([part, lax.ppermute(part, "yl", swap)])
-    blocks = [up]
-    for step in range(3):
-        if step == 1:
-            up, down = after((up, down), (below, above, theirs))
-        up = lax.ppermute(up, "z", ring(8, 1))
-        down = lax.ppermute(down, "z", ring(8, -1))
-        blocks += [up, down]
-    near = jnp.concatenate(blocks)
-    up, down, near = after((up, down, near), (below2, above2))
-    up = lax.ppermute(up[:96], "z", ring(8, 1))
-    down = lax.ppermute(down[96:], "z", ring(8, -1))
-    far = jnp.concatenate([up, down])
-    weights = [near, far, lax.ppermute(near, "c", swap), lax.ppermute(far, "c", swap)]
-
-    dx = np.tile(np.array([0, -1, 1, 2, 2]), 2)
-    other_slab = np.repeat([0, 1], 5)
-    late_half = np.tile(np.array([0, 0, 0, 0, 64]), 2)
-    slab = (x + dx) % 4 * 2 + (yh + other_slab) % 2
-    dz = np.concatenate([np.tile(np.repeat([0, -1, 1, -2, 2, -3, 3], 2), 2), np.full(4, 4)])
-    other_row = np.tile(np.array([0, 1]), 16)
-    other_core = np.concatenate([np.repeat([0, 1], 14), np.repeat([0, 1], 2)])
-    block = ((yl + other_row) % 2 * 8 + (z + dz) % 8) * 2 + (c + other_core) % 2
-    offsets = jnp.concatenate([slab * 128 + late_half, block * 96]).astype(jnp.int32)
-
-    rate_columns = jnp.pad(lax.dynamic_slice(rate_weight, (0, x * 6), (3072, 6)), ((0, 0), (0, 122)))
-    rate_offset = jnp.pad(lax.dynamic_slice(rate_bias, (x * 6,), (6,)), (0, 122)).reshape(1, 128)
-    pair_weights = lax.dynamic_slice(init_weights, (0, x * 6, 0, 0), (2, 6, 64, 256))
-    pair_weights = pair_weights.reshape(2, PAIRS, 128, 256)
-    hidden_bias = lax.dynamic_slice(init_bias_hidden, (x * 6, 0), (6, 256)).reshape(PAIRS, 2, 256)
-    out_bias = lax.dynamic_slice(init_bias_out, (x * 6, 0), (6, 64)).reshape(PAIRS, 1, 128)
-    gain = lax.dynamic_slice(out_gain, (x * 384,), (384,)).reshape(1, 384)
+    a1, b1 = lax.ppermute(mine, "x", up), lax.ppermute(mine, "x", down)
+    t0, t1, a1, b1 = lax.optimization_barrier((theirs[:64], theirs[64:], a1, b1))
+    a2, b2 = lax.ppermute(t0, "x", up), lax.ppermute(t1, "x", down)
+    a3 = lax.ppermute(jnp.concatenate([a1[:64], t1]), "x", up)
+    b3 = lax.ppermute(jnp.concatenate([b1[64:], t0]), "x", down)
+    a4, b4 = lax.ppermute(a2, "x", up), lax.ppermute(b2, "x", down)
+    tokens = [mine, a1, b1, a3, b3, theirs, a2, b2, a4, b4]
+    pair = jnp.concatenate([part, lax.ppermute(part, "yl", swap)])
+    gathered = lax.all_gather(pair, "z", axis=0, tiled=True)
+    gathered = after(gathered, (a3, b3, a4, b4))
+    weights = [gathered, lax.ppermute(gathered, "c", swap)]
+
     result = layer(
-        offsets, tokens, weights, rate_columns, rate_offset,
-        pair_weights[0], pair_weights[1], hidden_bias, out_bias, gain,
+        jnp.stack([x, yh, yl, z, c]).astype(jnp.int32), tokens, weights, rate_weight.T, rate_bias,
+        init_weights, init_bias_hidden, init_bias_out, out_gain.reshape(1, 1536),
     )
     result = lax.all_to_all(result.reshape(8, 128, 384), SEQ, 0, 0, tiled=True)
     return result.reshape(4, 2, 128, 384).transpose(1, 2, 0, 3).reshape(2, 128, 1536)

time: 150 us -> 161 us (1.073)
  waiting for transfers between devices: 43.9 us -> 57.4 us
  between operations: 0.36 us -> 13.5 us
  starting transfers between devices: 25.4 us -> 13.5 us
  blocking collectives: 20 us -> 17.1 us
    unnamed x60 -> x54, local copies, waits for them, and re-layouts: 9.69 us -> 22.3 us
    ppermute x17 -> x10, starting transfers between devices: 22.5 us -> 10.2 us  [the longest x2 2.76 us: on_device(): a1, b1 = (lax.ppermute(mine, 'x', up), lax.ppermute(mine, 'x', down))]
    ppermute x1, waiting for transfers between devices: 2.57 us -> 14 us  [on_device(): theirs = lax.ppermute(sent, 'yh', swap)]
    slice x7 -> x3, local copies, waits for them, and re-layouts: 6.69 us -> 0.11 us  [the longest x1 0.05 us: on_device(): theirs[64:]]
    all_to_all x1, blocking collectives: 20 us -> 17.1 us  [on_device(): result = lax.all_to_all(result.reshape(8, 128, 384), SEQ, 0, 0, tiled=True)]
    dynamic_slice x5 -> x0, local copies, waits for them, and re-layouts: 2.3 us -> none  [the longest x1 0.77 us: on_device(): gain = lax.dynamic_slice(out_gain, (x * 384,), (384,)).reshape(1, 384)]
    ppermute x17 -> x10, waiting for transfers between devices: 41.3 us -> 43.5 us  [the longest x2 19.4 us: on_device(): a4, b4 = (lax.ppermute(a2, 'x', up), lax.ppermute(b2, 'x', down))]
  transfers between devices with their start and end apart: 18 -> 12, of which waited for: 9 -> 8; matrix products, arithmetic and copies ran while one was open for 10% -> 1% of each run, Pallas kernels for 0% -> 0%
where the time goes in v3:
time: 161 us
  waiting for transfers between devices  57.4 us (36%)
  Pallas kernels  31.9 us (20%)
  local copies, waits for them, and re-layouts  26.2 us (16%)
  blocking collectives  17.1 us (11%)
  starting transfers between devices  13.5 us (8%)
  between operations  13.5 us (8%)
    pallas_call x1, Pallas kernels, layer(): pl.pallas_call(layer_kernel, out_shape=jax.ShapeDtypeStruct((1024, 384),...  31.9 us
    unnamed x54, local copies, waits for them, and re-layouts  22.3 us
    ppermute x2, waiting for transfers between devices, on_device(): a4, b4 = (lax.ppermute(a2, 'x', up), lax.ppermute(b2, 'x', down))  19.4 us
    all_to_all x1, blocking collectives, on_device(): result = lax.all_to_all(result.reshape(8, 128, 384), SEQ, 0, 0, tiled=True)  17.1 us
    ppermute x1, waiting for transfers between devices, on_device(): theirs = lax.ppermute(sent, 'yh', swap)  14 us
    ppermute x2, waiting for transfers between devices, on_device(): a2, b2 = (lax.ppermute(t0, 'x', up), lax.ppermute(t1, 'x', down))  7.8 us
    ppermute x1, waiting for transfers between devices, on_device(): weights = [gathered, lax.ppermute(gathered, 'c', swap)]  5.64 us
    ppermute x1, waiting for transfers between devices, on_device(): pair = jnp.concatenate([part, lax.ppermute(part, 'yl', swap)])  5.59 us
  transfers between devices with their start and end apart: 12, of which 8 were waited for; matrix products, arithmetic and copies ran while one was open for 1% of the time, Pallas kernels for 0%

profile of v3, /device:TPU:96, one launch (start us, length us, event | category | flops | bytes accessed | tf_op | source)
XLA Modules:
  0.0 160.6 jit_solution(9775633881947175728)
XLA Ops:
  6.5 1.1 constant_dynamic-slice_fusion.2
  7.7 1.7 %collective-permute-start.9 = (bf16[96,1152]{1,0:T(8,128)(2,1)S(1)}, bf16[96,1152]{1,0:T(8,128)(2,1)S(1)}, u32[]{:S(2)}, u32[]{:S(2)}) collective-permute-start(bf16[96,1152]{1,0:T(8,128)(2,1)S(1)} %pad_maximum_fusion.3), channel_id=1, source_target_pairs={{0,16},{16,0},{1,17},{17,1},{2,18},{18,2},{3,19},{19,3},{4,20},{20... | collective-permute-start | bytes 663560 | tf_op jit(solution)/shard_map/ppermute | solution.py:330
  9.3 5.6 %collective-permute-done.9 = bf16[96,1152]{1,0:T(8,128)(2,1)S(1)} collective-permute-done((bf16[96,1152]{1,0:T(8,128)(2,1)S(1)}, bf16[96,1152]{1,0:T(8,128)(2,1)S(1)}, u32[]{:S(2)}, u32[]{:S(2)}) %collective-permute-start.9) | collective-permute-done | bytes 221216 | tf_op jit(solution)/shard_map/ppermute | solution.py:330
  15.9 3.3 %collective-permute-start = (bf16[128,3072]{1,0:T(8,128)(2,1)S(1)}, bf16[128,3072]{1,0:T(8,128)(2,1)S(1)}, u32[]{:S(2)}, u32[]{:S(2)}) collective-permute-start(bf16[128,3072]{1,0:T(8,128)(2,1)S(1)} %get-tuple-element.15), channel_id=1, source_target_pairs={{0,32},{32,0},{1,33},{33,1},{2,34},{34,2},{3,35},{35,3},{4,36},{36... | collective-permute-start | bytes 2359304 | tf_op jit(solution)/shard_map/ppermute | solution.py:322
  19.2 2.8 %collective-permute-start.2 = (bf16[128,3072]{1,0:T(8,128)(2,1)S(1)}, bf16[128,3072]{1,0:T(8,128)(2,1)S(1)}, u32[]{:S(2)}, u32[]{:S(2)}) collective-permute-start(bf16[128,3072]{1,0:T(8,128)(2,1)S(1)} %get-tuple-element.16.refs_0_), channel_id=1, source_target_pairs={{0,192},{64,0},{128,64},{192,128},{1,193},{65,1},{129,65},{193,129... | collective-permute-start | bytes 2359304 | tf_op jit(solution)/shard_map/ppermute | solution.py:323
  22.0 14.0 %collective-permute-done.refs_5_ = bf16[128,3072]{1,0:T(8,128)(2,1)S(1)} collective-permute-done((bf16[128,3072]{1,0:T(8,128)(2,1)S(1)}, bf16[128,3072]{1,0:T(8,128)(2,1)S(1)}, u32[]{:S(2)}, u32[]{:S(2)}) %collective-permute-start) | collective-permute-done | bytes 786464 | tf_op jit(solution)/shard_map/ppermute | solution.py:322
  36.0 1.6 %collective-permute-done.2.refs_2_ = bf16[128,3072]{1,0:T(8,128)(2,1)S(1)} collective-permute-done((bf16[128,3072]{1,0:T(8,128)(2,1)S(1)}, bf16[128,3072]{1,0:T(8,128)(2,1)S(1)}, u32[]{:S(2)}, u32[]{:S(2)}) %collective-permute-start.2) | collective-permute-done | bytes 786464 | tf_op jit(solution)/shard_map/ppermute | solution.py:323
  37.6 3.4 %collective-permute-done.1.refs_1_ = bf16[128,3072]{1,0:T(8,128)(2,1)S(1)} collective-permute-done((bf16[128,3072]{1,0:T(8,128)(2,1)S(1)}, bf16[128,3072]{1,0:T(8,128)(2,1)S(1)}, u32[]{:S(2)}, u32[]{:S(2)}) %collective-permute-start.1) | collective-permute-done | bytes 786464 | tf_op jit(solution)/shard_map/ppermute | solution.py:323
  41.9 1.3 collective-permute-start.5
  43.4 2.0 %collective-permute-start.4 = (bf16[128,3072]{1,0:T(8,128)(2,1)S(1)}, bf16[128,3072]{1,0:T(8,128)(2,1)S(1)}, u32[]{:S(2)}, u32[]{:S(2)}) collective-permute-start(bf16[128,3072]{1,0:T(8,128)(2,1)S(1)} %pad_maximum_fusion.1), channel_id=1, source_target_pairs={{0,192},{64,0},{128,64},{192,128},{1,193},{65,1},{129,65},{193,129... | collective-permute-start | bytes 2359304 | tf_op jit(solution)/shard_map/ppermute | solution.py:327
  45.5 7.8 %collective-permute-done.6.refs_7_ = bf16[64,3072]{1,0:T(8,128)(2,1)S(1)} collective-permute-done((bf16[64,3072]{1,0:T(8,128)(2,1)S(1)}, bf16[64,3072]{1,0:T(8,128)(2,1)S(1)}, u32[]{:S(2)}, u32[]{:S(2)}) %collective-permute-start.6) | collective-permute-done | bytes 393248 | tf_op jit(solution)/shard_map/ppermute | solution.py:325
  53.3 1.5 collective-permute-start.8
  56.9 18.2 %collective-permute-done.8.refs_9_ = bf16[64,3072]{1,0:T(8,128)(2,1)S(1)} collective-permute-done((bf16[64,3072]{1,0:T(8,128)(2,1)S(1)}, bf16[64,3072]{1,0:T(8,128)(2,1)S(1)}, u32[]{:S(2)}, u32[]{:S(2)}) %collective-permute-start.8) | collective-permute-done | bytes 393248 | tf_op jit(solution)/shard_map/ppermute | solution.py:328
  75.8 1.2 collective-permute-done.7.refs_8_
  78.6 0.9 copy-done.12
  80.4 5.6 %collective-permute-done.10.refs_11_ = bf16[1536,1152]{1,0:T(8,128)(2,1)S(1)} collective-permute-done((bf16[1536,1152]{1,0:T(8,128)(2,1)}, bf16[1536,1152]{1,0:T(8,128)(2,1)S(1)}, u32[]{:S(2)}, u32[]{:S(2)}) %collective-permute-start.10) | collective-permute-done | bytes 3538976 | tf_op jit(solution)/shard_map/ppermute | solution.py:333
  86.0 2.0 %copy-done = bf16[1536,1152]{1,0:T(8,128)(2,1)S(1)} copy-done((bf16[1536,1152]{1,0:T(8,128)(2,1)S(1)}, bf16[1536,1152]{1,0:T(8,128)(2,1)}, u32[]{:S(2)}) %copy-start) | copy-done | bytes 3538968
  88.0 1.1 copy-done.2
  89.1 1.1 copy-done.4
  90.3 1.9 %copy-done.5 = f32[2,24,64,256]{3,2,1,0:T(8,128)S(1)} copy-done((f32[2,24,64,256]{3,2,1,0:T(8,128)S(1)}, f32[2,24,64,256]{3,2,1,0:T(8,128)}, u32[]{:S(2)}) %copy-start.5) | copy-done | bytes 3145752
  92.2 1.1 copy-done.7
  93.3 1.1 copy-done.9
  94.4 1.1 copy-done.11
  95.6 1.1 copy-done.13
  96.7 1.0 copy-done.15
  97.7 1.0 copy-done.17
  98.7 1.0 copy-done.19
  99.7 1.0 copy-done.21
  100.7 0.9 copy-done.22
  103.0 31.9 %layer.1 = bf16[1024,384]{1,0:T(8,128)(2,1)S(1)} custom-call(s32[5]{0:T(128)S(1)} %stack.23.place_ref, bf16[128,3072]{1,0:T(8,128)(2,1)S(1)} %copy-done.4, bf16[128,3072]{1,0:T(8,128)(2,1)S(1)} %copy-done.9, bf16[128,3072]{1,0:T(8,128)(2,1)S(1)} %copy-done.7, bf16[128,3072]{1,0:T(8,128)(2,1)S(1)} %copy-done.13, bf16[128,3072]{1,0:T(8,128)(2,1)S(1)} %copy-done.11, ...), custom_call_target="tpu_custom_call" | custom-call | tf_op jit(solution)/shard_map/layer/pallas_call | solution.py:247
  134.9 17.1 %all_to_all.5 = bf16[8,128,384]{2,1,0:T(8,128)(2,1)S(1)} all-to-all(bf16[8,128,384]{2,1,0:T(8,128)(2,1)S(1)} %bitcast.15), channel_id=1, replica_groups=mesh['x'=4,'yh'=2,'yl'=2,'z'=8,'c'=2] {'x','yh'}, dimensions={0} | all-to-all | bytes 1572864 | tf_op jit(solution)/shard_map/all_to_all | solution.py:339
  152.6 1.2 reshape.15
  (62 shorter events, 9.5 us)
Async XLA Ops:
  6.5 9.3 %copy-start.26 = (bf16[2,128,3072]{2,1,0:T(8,128)(2,1)S(1)}, bf16[2,128,3072]{2,1,0:T(8,128)(2,1)}, u32[]{:S(2)}) copy-start(bf16[2,128,3072]{2,1,0:T(8,128)(2,1)} %param.8) | copy-start | bytes 4718596
  6.5 73.0 %all-gather.2.cloned.1.call-start = ((), (), s32[]{:S(2)}) async-start(), calls=%async_computation.1 | async-start | bytes 3981312 | tf_op jit(solution)/shard_map/all_gather | solution.py:331
  7.7 7.3 %collective-permute-start.9 = (bf16[96,1152]{1,0:T(8,128)(2,1)S(1)}, bf16[96,1152]{1,0:T(8,128)(2,1)S(1)}, u32[]{:S(2)}, u32[]{:S(2)}) collective-permute-start(bf16[96,1152]{1,0:T(8,128)(2,1)S(1)} %pad_maximum_fusion.3), channel_id=1, source_target_pairs={{0,16},{16,0},{1,17},{17,1},{2,18},{18,2},{3,19},{19,3},{4,20},{20... | collective-permute-start | bytes 663560 | tf_op jit(solution)/shard_map/ppermute | solution.py:330
  15.9 25.2 %copy-start.3 = (bf16[128,3072]{1,0:T(8,128)(2,1)}, bf16[128,3072]{1,0:T(8,128)(2,1)S(1)}, u32[]{:S(2)}) copy-start(bf16[128,3072]{1,0:T(8,128)(2,1)S(1)} %get-tuple-element.16.refs_0_) | copy-start | bytes 2359300
  15.9 20.0 %collective-permute-start = (bf16[128,3072]{1,0:T(8,128)(2,1)S(1)}, bf16[128,3072]{1,0:T(8,128)(2,1)S(1)}, u32[]{:S(2)}, u32[]{:S(2)}) collective-permute-start(bf16[128,3072]{1,0:T(8,128)(2,1)S(1)} %get-tuple-element.15), channel_id=1, source_target_pairs={{0,32},{32,0},{1,33},{33,1},{2,34},{34,2},{3,35},{35,3},{4,36},{36... | collective-permute-start | bytes 2359304 | tf_op jit(solution)/shard_map/ppermute | solution.py:322
  19.2 18.4 %collective-permute-start.2 = (bf16[128,3072]{1,0:T(8,128)(2,1)S(1)}, bf16[128,3072]{1,0:T(8,128)(2,1)S(1)}, u32[]{:S(2)}, u32[]{:S(2)}) collective-permute-start(bf16[128,3072]{1,0:T(8,128)(2,1)S(1)} %get-tuple-element.16.refs_0_), channel_id=1, source_target_pairs={{0,192},{64,0},{128,64},{192,128},{1,193},{65,1},{129,65},{193,129... | collective-permute-start | bytes 2359304 | tf_op jit(solution)/shard_map/ppermute | solution.py:323
  22.0 19.1 %collective-permute-start.1 = (bf16[128,3072]{1,0:T(8,128)(2,1)S(1)}, bf16[128,3072]{1,0:T(8,128)(2,1)S(1)}, u32[]{:S(2)}, u32[]{:S(2)}) collective-permute-start(bf16[128,3072]{1,0:T(8,128)(2,1)S(1)} %get-tuple-element.16.refs_0_), channel_id=1, source_target_pairs={{0,64},{64,128},{128,192},{192,0},{1,65},{65,129},{129,193},{193,1... | collective-permute-start | bytes 2359304 | tf_op jit(solution)/shard_map/ppermute | solution.py:323
  35.9 5.2 %copy-start.1 = (bf16[128,3072]{1,0:T(8,128)(2,1)}, bf16[128,3072]{1,0:T(8,128)(2,1)S(1)}, u32[]{:S(2)}) copy-start(bf16[128,3072]{1,0:T(8,128)(2,1)S(1)} %collective-permute-done.refs_5_) | copy-start | bytes 2359300
  37.6 3.9 %copy-start.6 = (bf16[128,3072]{1,0:T(8,128)(2,1)}, bf16[128,3072]{1,0:T(8,128)(2,1)S(1)}, u32[]{:S(2)}) copy-start(bf16[128,3072]{1,0:T(8,128)(2,1)S(1)} %collective-permute-done.2.refs_2_) | copy-start | bytes 2359300
  41.1 44.9 %copy-start.25 = (f32[24]{0:T(128)S(1)}, f32[24]{0:T(128)}, u32[]{:S(2)}) copy-start(f32[24]{0:T(128)} %refs_13_.1) | copy-start | bytes 292
  41.1 12.1 %collective-permute-start.6 = (bf16[64,3072]{1,0:T(8,128)(2,1)S(1)}, bf16[64,3072]{1,0:T(8,128)(2,1)S(1)}, u32[]{:S(2)}, u32[]{:S(2)}) collective-permute-start(bf16[64,3072]{1,0:T(8,128)(2,1)S(1)} %get-tuple-element.12), channel_id=1, source_target_pairs={{0,192},{64,0},{128,64},{192,128},{1,193},{65,1},{129,65},{193,129... | collective-permute-start | bytes 1179656 | tf_op jit(solution)/shard_map/ppermute | solution.py:325
  41.9 13.7 %collective-permute-start.5 = (bf16[64,3072]{1,0:T(8,128)(2,1)S(1)}, bf16[64,3072]{1,0:T(8,128)(2,1)S(1)}, u32[]{:S(2)}, u32[]{:S(2)}) collective-permute-start(bf16[64,3072]{1,0:T(8,128)(2,1)S(1)} %get-tuple-element.13), channel_id=1, source_target_pairs={{0,64},{64,128},{128,192},{192,0},{1,65},{65,129},{129,193},{193,1... | collective-permute-start | bytes 1179656 | tf_op jit(solution)/shard_map/ppermute | solution.py:325
  43.4 34.4 %collective-permute-start.4 = (bf16[128,3072]{1,0:T(8,128)(2,1)S(1)}, bf16[128,3072]{1,0:T(8,128)(2,1)S(1)}, u32[]{:S(2)}, u32[]{:S(2)}) collective-permute-start(bf16[128,3072]{1,0:T(8,128)(2,1)S(1)} %pad_maximum_fusion.1), channel_id=1, source_target_pairs={{0,192},{64,0},{128,64},{192,128},{1,193},{65,1},{129,65},{193,129... | collective-permute-start | bytes 2359304 | tf_op jit(solution)/shard_map/ppermute | solution.py:327
  45.3 33.3 %collective-permute-start.3 = (bf16[128,3072]{1,0:T(8,128)(2,1)S(1)}, bf16[128,3072]{1,0:T(8,128)(2,1)S(1)}, u32[]{:S(2)}, u32[]{:S(2)}) collective-permute-start(bf16[128,3072]{1,0:T(8,128)(2,1)S(1)} %pad_maximum_fusion), channel_id=1, source_target_pairs={{0,64},{64,128},{128,192},{192,0},{1,65},{65,129},{129,193},{193,1... | collective-permute-start | bytes 2359304 | tf_op jit(solution)/shard_map/ppermute | solution.py:326
  53.3 21.8 %collective-permute-start.8 = (bf16[64,3072]{1,0:T(8,128)(2,1)S(1)}, bf16[64,3072]{1,0:T(8,128)(2,1)S(1)}, u32[]{:S(2)}, u32[]{:S(2)}) collective-permute-start(bf16[64,3072]{1,0:T(8,128)(2,1)S(1)} %collective-permute-done.6.refs_7_), channel_id=1, source_target_pairs={{0,192},{64,0},{128,64},{192,128},{1,193},{65,1},{129,65},{193,129... | collective-permute-start | bytes 1179656 | tf_op jit(solution)/shard_map/ppermute | solution.py:328
  55.6 21.4 %collective-permute-start.7 = (bf16[64,3072]{1,0:T(8,128)(2,1)S(1)}, bf16[64,3072]{1,0:T(8,128)(2,1)S(1)}, u32[]{:S(2)}, u32[]{:S(2)}) collective-permute-start(bf16[64,3072]{1,0:T(8,128)(2,1)S(1)} %collective-permute-done.5.refs_6_), channel_id=1, source_target_pairs={{0,64},{64,128},{128,192},{192,0},{1,65},{65,129},{129,193},{193,1... | collective-permute-start | bytes 1179656 | tf_op jit(solution)/shard_map/ppermute | solution.py:328
  77.8 0.9 copy-start.10
  78.6 0.9 copy-start.12
  79.6 6.4 %collective-permute-start.10 = (bf16[1536,1152]{1,0:T(8,128)(2,1)}, bf16[1536,1152]{1,0:T(8,128)(2,1)S(1)}, u32[]{:S(2)}, u32[]{:S(2)}) collective-permute-start(bf16[1536,1152]{1,0:T(8,128)(2,1)} %all-gather.2.cloned.1.call-done.refs_10_), channel_id=1, source_target_pairs={{0,1},{1,0},{2,3},{3,2},{4,5},{5,4},{6,7},{7,6},{8,9},{9,8},{10,11... | collective-permute-start | bytes 10616840 | tf_op jit(solution)/shard_map/ppermute | solution.py:333
  86.0 2.0 %copy-start = (bf16[1536,1152]{1,0:T(8,128)(2,1)S(1)}, bf16[1536,1152]{1,0:T(8,128)(2,1)}, u32[]{:S(2)}) copy-start(bf16[1536,1152]{1,0:T(8,128)(2,1)} %all-gather.2.cloned.1.call-done.refs_10_) | copy-start | bytes 10616836
  88.0 1.1 copy-start.2
  89.1 1.1 copy-start.4
  90.3 1.9 %copy-start.5 = (f32[2,24,64,256]{3,2,1,0:T(8,128)S(1)}, f32[2,24,64,256]{3,2,1,0:T(8,128)}, u32[]{:S(2)}) copy-start(f32[2,24,64,256]{3,2,1,0:T(8,128)} %refs_14_.1) | copy-start | bytes 9437188
  92.2 1.1 copy-start.7
  93.3 1.1 copy-start.9
  94.4 1.1 copy-start.11
  95.6 1.1 copy-start.13
  96.7 1.0 copy-start.15
  97.7 1.0 copy-start.17
  98.7 1.0 copy-start.19
  99.7 1.0 copy-start.21
  100.7 0.9 copy-start.22
  (7 other events, 5.4 us)
Sparse Core Ops, SparseCore 0:
  15.9 49.9 all-gather.1

commit v4 on v3

--- a/solution.py
+++ b/solution.py
@@ -281,7 +281,7 @@
             ],
         ),
         compiler_params=pltpu.CompilerParams(
-            dimension_semantics=("arbitrary",), vmem_limit_bytes=32 << 20
+            dimension_semantics=("arbitrary",), vmem_limit_bytes=60 << 20
         ),
         name="layer",
     )(place, *tokens, *weights, rate_t, rate_bias, init_weights, hidden, outer, gain)
@@ -329,7 +329,7 @@
     tokens = [mine, a1, b1, a3, b3, theirs, a2, b2, a4, b4]
     pair = jnp.concatenate([part, lax.ppermute(part, "yl", swap)])
     gathered = lax.all_gather(pair, "z", axis=0, tiled=True)
-    gathered = after(gathered, (a3, b3, a4, b4))
+    gathered = after(gathered, (a2, b2, a3, b3))
     weights = [gathered, lax.ppermute(gathered, "c", swap)]
 
     result = layer(
@@ -337,7 +337,8 @@
         init_weights, init_bias_hidden, init_bias_out, out_gain.reshape(1, 1536),
     )
     result = lax.all_to_all(result.reshape(8, 128, 384), SEQ, 0, 0, tiled=True)
-    return result.reshape(4, 2, 128, 384).transpose(1, 2, 0, 3).reshape(2, 128, 1536)
+    result = result.reshape(4, 2, 128, 384)
+    return jnp.concatenate([result[i] for i in range(4)], axis=2)
 
 
 def solution(mesh):

time: 161 us -> 143 us (0.89)
  local copies, waits for them, and re-layouts: 26.2 us -> 6.92 us
    unnamed x54 -> x18, local copies, waits for them, and re-layouts: 22.3 us -> 4.34 us
    ppermute x2, waiting for transfers between devices: 7.8 us -> 23.2 us  [on_device(): a2, b2 = (lax.ppermute(t0, 'x', up), lax.ppermute(t1, 'x', down))]
    ppermute x2, waiting for transfers between devices: 19.4 us -> 9.77 us  [on_device(): a4, b4 = (lax.ppermute(a2, 'x', up), lax.ppermute(b2, 'x', down))]
    ppermute x1, waiting for transfers between devices: 5.64 us -> 0.01 us  [on_device(): weights = [gathered, lax.ppermute(gathered, 'c', swap)]]
    reshape x2 -> x0, local copies, waits for them, and re-layouts: 1.79 us -> none  [on_device(): result.reshape(4, 2, 128, 384).transpose(1, 2, 0, 3).reshape(2, 128, 1536)]
where the time goes in v4:
time: 143 us
  waiting for transfers between devices  56.7 us (40%)
  Pallas kernels  32.3 us (23%)
  blocking collectives  17.3 us (12%)
  starting transfers between devices  14 us (10%)
  between operations  13.5 us (9%)
  local copies, waits for them, and re-layouts  6.92 us (5%)
  other arithmetic  1.87 us (1%)
    pallas_call x1, Pallas kernels, layer(): pl.pallas_call(layer_kernel, out_shape=jax.ShapeDtypeStruct((1024, 384),...  32.3 us
    ppermute x2, waiting for transfers between devices, on_device(): a2, b2 = (lax.ppermute(t0, 'x', up), lax.ppermute(t1, 'x', down))  23.2 us
    all_to_all x1, blocking collectives, on_device(): result = lax.all_to_all(result.reshape(8, 128, 384), SEQ, 0, 0, tiled=True)  17.3 us
    ppermute x1, waiting for transfers between devices, on_device(): theirs = lax.ppermute(sent, 'yh', swap)  14 us
    ppermute x2, waiting for transfers between devices, on_device(): a4, b4 = (lax.ppermute(a2, 'x', up), lax.ppermute(b2, 'x', down))  9.77 us
    ppermute x1, waiting for transfers between devices, on_device(): pair = jnp.concatenate([part, lax.ppermute(part, 'yl', swap)])  5.59 us
    unnamed x18, local copies, waits for them, and re-layouts  4.34 us
    ppermute x2, waiting for transfers between devices, on_device(): a1, b1 = (lax.ppermute(mine, 'x', up), lax.ppermute(mine, 'x', down))  4.13 us
  transfers between devices with their start and end apart: 12, of which 8 were waited for; matrix products, arithmetic and copies ran while one was open for 1% of the time, Pallas kernels for 0%

profile of v4, /device:TPU:96, one launch (start us, length us, event | category | flops | bytes accessed | tf_op | source)
XLA Modules:
  0.0 142.6 jit_solution(14151019088539546332)
XLA Ops:
  6.5 1.1 constant_dynamic-slice_fusion.2
  7.7 1.7 %collective-permute-start.9 = (bf16[96,1152]{1,0:T(8,128)(2,1)S(1)}, bf16[96,1152]{1,0:T(8,128)(2,1)S(1)}, u32[]{:S(2)}, u32[]{:S(2)}) collective-permute-start(bf16[96,1152]{1,0:T(8,128)(2,1)S(1)} %pad_maximum_fusion.4), channel_id=1, source_target_pairs={{0,16},{16,0},{1,17},{17,1},{2,18},{18,2},{3,19},{19,3},{4,20},{20... | collective-permute-start | bytes 663560 | tf_op jit(solution)/shard_map/ppermute | solution.py:330
  9.3 5.6 %collective-permute-done.9 = bf16[96,1152]{1,0:T(8,128)(2,1)S(1)} collective-permute-done((bf16[96,1152]{1,0:T(8,128)(2,1)S(1)}, bf16[96,1152]{1,0:T(8,128)(2,1)S(1)}, u32[]{:S(2)}, u32[]{:S(2)}) %collective-permute-start.9) | collective-permute-done | bytes 221216 | tf_op jit(solution)/shard_map/ppermute | solution.py:330
  14.9 0.8 pad_maximum_fusion.3
  15.8 0.1 dynamic-slice_bitcast_fusion
  15.9 3.3 %collective-permute-start = (bf16[128,3072]{1,0:T(8,128)(2,1)S(1)}, bf16[128,3072]{1,0:T(8,128)(2,1)S(1)}, u32[]{:S(2)}, u32[]{:S(2)}) collective-permute-start(bf16[128,3072]{1,0:T(8,128)(2,1)S(1)} %get-tuple-element.15), channel_id=1, source_target_pairs={{0,32},{32,0},{1,33},{33,1},{2,34},{34,2},{3,35},{35,3},{4,36},{36... | collective-permute-start | bytes 2359304 | tf_op jit(solution)/shard_map/ppermute | solution.py:322
  19.2 2.8 %collective-permute-start.2 = (bf16[128,3072]{1,0:T(8,128)(2,1)S(1)}, bf16[128,3072]{1,0:T(8,128)(2,1)S(1)}, u32[]{:S(2)}, u32[]{:S(2)}) collective-permute-start(bf16[128,3072]{1,0:T(8,128)(2,1)S(1)} %get-tuple-element.16.refs_0_), channel_id=1, source_target_pairs={{0,192},{64,0},{128,64},{192,128},{1,193},{65,1},{129,65},{193,129... | collective-permute-start | bytes 2359304 | tf_op jit(solution)/shard_map/ppermute | solution.py:323
  21.9 14.0 %collective-permute-done.refs_5_ = bf16[128,3072]{1,0:T(8,128)(2,1)S(1)} collective-permute-done((bf16[128,3072]{1,0:T(8,128)(2,1)S(1)}, bf16[128,3072]{1,0:T(8,128)(2,1)S(1)}, u32[]{:S(2)}, u32[]{:S(2)}) %collective-permute-start) | collective-permute-done | bytes 786464 | tf_op jit(solution)/shard_map/ppermute | solution.py:322
  35.9 0.9 copy-done.1
  36.8 0.1 fusion.1
  36.9 0.7 collective-permute-done.2.refs_2_
  37.6 3.4 %collective-permute-done.1.refs_1_ = bf16[128,3072]{1,0:T(8,128)(2,1)S(1)} collective-permute-done((bf16[128,3072]{1,0:T(8,128)(2,1)S(1)}, bf16[128,3072]{1,0:T(8,128)(2,1)S(1)}, u32[]{:S(2)}, u32[]{:S(2)}) %collective-permute-start.1) | collective-permute-done | bytes 786464 | tf_op jit(solution)/shard_map/ppermute | solution.py:323
  41.0 0.9 copy-done.4
  42.0 0.1 pad_maximum_fusion.1
  42.0 0.6 collective-permute-start.4
  42.7 1.5 %collective-permute-start.3 = (bf16[128,3072]{1,0:T(8,128)(2,1)S(1)}, bf16[128,3072]{1,0:T(8,128)(2,1)}, u32[]{:S(2)}, u32[]{:S(2)}) collective-permute-start(bf16[128,3072]{1,0:T(8,128)(2,1)S(1)} %pad_maximum_fusion), channel_id=1, source_target_pairs={{0,64},{64,128},{128,192},{192,0},{1,65},{65,129},{129,193},{193,1... | collective-permute-start | bytes 2359304 | tf_op jit(solution)/shard_map/ppermute | solution.py:326
  44.3 1.8 %collective-permute-start.6 = (bf16[64,3072]{1,0:T(8,128)(2,1)S(1)}, bf16[64,3072]{1,0:T(8,128)(2,1)S(1)}, u32[]{:S(2)}, u32[]{:S(2)}) collective-permute-start(bf16[64,3072]{1,0:T(8,128)(2,1)S(1)} %get-tuple-element.12), channel_id=1, source_target_pairs={{0,192},{64,0},{128,64},{192,128},{1,193},{65,1},{129,65},{193,129... | collective-permute-start | bytes 1179656 | tf_op jit(solution)/shard_map/ppermute | solution.py:325
  46.1 0.2 collective-permute-start.5
  46.3 21.3 %collective-permute-done.6.refs_7_ = bf16[64,3072]{1,0:T(8,128)(2,1)S(1)} collective-permute-done((bf16[64,3072]{1,0:T(8,128)(2,1)S(1)}, bf16[64,3072]{1,0:T(8,128)(2,1)S(1)}, u32[]{:S(2)}, u32[]{:S(2)}) %collective-permute-start.6) | collective-permute-done | bytes 393248 | tf_op jit(solution)/shard_map/ppermute | solution.py:325
  67.6 1.9 %collective-permute-done.5.refs_6_ = bf16[64,3072]{1,0:T(8,128)(2,1)S(1)} collective-permute-done((bf16[64,3072]{1,0:T(8,128)(2,1)S(1)}, bf16[64,3072]{1,0:T(8,128)(2,1)S(1)}, u32[]{:S(2)}, u32[]{:S(2)}) %collective-permute-start.5) | collective-permute-done | bytes 393248 | tf_op jit(solution)/shard_map/ppermute | solution.py:325
  69.5 0.7 copy-done.7
  70.3 0.4 collective-permute-start.8
  70.6 1.7 %collective-permute-start.7 = (bf16[64,3072]{1,0:T(8,128)(2,1)}, bf16[64,3072]{1,0:T(8,128)(2,1)}, u32[]{:S(2)}, u32[]{:S(2)}) collective-permute-start(bf16[64,3072]{1,0:T(8,128)(2,1)} %copy-done.7), channel_id=1, source_target_pairs={{0,64},{64,128},{128,192},{192,0},{1,65},{65,129},{129,193},{193,1... | collective-permute-start | bytes 1179656 | tf_op jit(solution)/shard_map/ppermute | solution.py:328
  72.4 0.6 reshape.15.refs_17_
  73.0 0.6 stack.23.place_ref
  73.6 8.6 %collective-permute-done.8.refs_9_ = bf16[64,3072]{1,0:T(8,128)(2,1)} collective-permute-done((bf16[64,3072]{1,0:T(8,128)(2,1)}, bf16[64,3072]{1,0:T(8,128)(2,1)}, u32[]{:S(2)}, u32[]{:S(2)}) %collective-permute-start.8) | collective-permute-done | bytes 393248 | tf_op jit(solution)/shard_map/ppermute | solution.py:328
  82.1 1.2 collective-permute-done.7.refs_8_
  83.3 1.8 %copy-done = bf16[1536,1152]{1,0:T(8,128)(2,1)} copy-done((bf16[1536,1152]{1,0:T(8,128)(2,1)}, bf16[1536,1152]{1,0:T(8,128)(2,1)S(1)}, u32[]{:S(2)}) %copy-start) | copy-done | bytes 3538968
  85.1 32.3 %layer.1 = bf16[1024,384]{1,0:T(8,128)(2,1)} custom-call(s32[5]{0:T(128)} %stack.23.place_ref, bf16[128,3072]{1,0:T(8,128)(2,1)} %copy-done.2, bf16[128,3072]{1,0:T(8,128)(2,1)} %copy-done.4, bf16[128,3072]{1,0:T(8,128)(2,1)} %copy-done.3, bf16[128,3072]{1,0:T(8,128)(2,1)} %collective-permute-done.3.refs_3_, ...), custom_call_target="tpu_custom_call" | custom-call | tf_op jit(solution)/shard_map/layer/pallas_call | solution.py:247
  117.4 17.3 %all_to_all.5 = bf16[8,128,384]{2,1,0:T(8,128)(2,1)S(1)} all-to-all(bf16[8,128,384]{2,1,0:T(8,128)(2,1)} %bitcast.11), channel_id=1, replica_groups=mesh['x'=4,'yh'=2,'yl'=2,'z'=8,'c'=2] {'x','yh'}, dimensions={0} | all-to-all | bytes 1572864 | tf_op jit(solution)/shard_map/all_to_all | solution.py:339
  134.7 0.1 fusion
  134.8 0.9 pad_maximum_fusion.2
  (26 shorter events, 0.2 us)
Async XLA Ops:
  6.5 9.2 %copy-start.5 = (bf16[2,128,3072]{2,1,0:T(8,128)(2,1)S(1)}, bf16[2,128,3072]{2,1,0:T(8,128)(2,1)}, u32[]{:S(2)}) copy-start(bf16[2,128,3072]{2,1,0:T(8,128)(2,1)} %param.8) | copy-start | bytes 4718596
  6.5 63.7 %all-gather.2.cloned.1.call-start = ((), (), s32[]{:S(2)}) async-start(), calls=%async_computation.1 | async-start | bytes 3981312 | tf_op jit(solution)/shard_map/all_gather | solution.py:331
  7.7 7.3 %collective-permute-start.9 = (bf16[96,1152]{1,0:T(8,128)(2,1)S(1)}, bf16[96,1152]{1,0:T(8,128)(2,1)S(1)}, u32[]{:S(2)}, u32[]{:S(2)}) collective-permute-start(bf16[96,1152]{1,0:T(8,128)(2,1)S(1)} %pad_maximum_fusion.4), channel_id=1, source_target_pairs={{0,16},{16,0},{1,17},{17,1},{2,18},{18,2},{3,19},{19,3},{4,20},{20... | collective-permute-start | bytes 663560 | tf_op jit(solution)/shard_map/ppermute | solution.py:330
  15.9 21.0 %copy-start.2 = (bf16[128,3072]{1,0:T(8,128)(2,1)}, bf16[128,3072]{1,0:T(8,128)(2,1)S(1)}, u32[]{:S(2)}) copy-start(bf16[128,3072]{1,0:T(8,128)(2,1)S(1)} %get-tuple-element.16.refs_0_) | copy-start | bytes 2359300
  15.9 20.0 %collective-permute-start = (bf16[128,3072]{1,0:T(8,128)(2,1)S(1)}, bf16[128,3072]{1,0:T(8,128)(2,1)S(1)}, u32[]{:S(2)}, u32[]{:S(2)}) collective-permute-start(bf16[128,3072]{1,0:T(8,128)(2,1)S(1)} %get-tuple-element.15), channel_id=1, source_target_pairs={{0,32},{32,0},{1,33},{33,1},{2,34},{34,2},{3,35},{35,3},{4,36},{36... | collective-permute-start | bytes 2359304 | tf_op jit(solution)/shard_map/ppermute | solution.py:322
  19.2 18.4 %collective-permute-start.2 = (bf16[128,3072]{1,0:T(8,128)(2,1)S(1)}, bf16[128,3072]{1,0:T(8,128)(2,1)S(1)}, u32[]{:S(2)}, u32[]{:S(2)}) collective-permute-start(bf16[128,3072]{1,0:T(8,128)(2,1)S(1)} %get-tuple-element.16.refs_0_), channel_id=1, source_target_pairs={{0,192},{64,0},{128,64},{192,128},{1,193},{65,1},{129,65},{193,129... | collective-permute-start | bytes 2359304 | tf_op jit(solution)/shard_map/ppermute | solution.py:323
  21.9 19.1 %collective-permute-start.1 = (bf16[128,3072]{1,0:T(8,128)(2,1)S(1)}, bf16[128,3072]{1,0:T(8,128)(2,1)S(1)}, u32[]{:S(2)}, u32[]{:S(2)}) collective-permute-start(bf16[128,3072]{1,0:T(8,128)(2,1)S(1)} %get-tuple-element.16.refs_0_), channel_id=1, source_target_pairs={{0,64},{64,128},{128,192},{192,0},{1,65},{65,129},{129,193},{193,1... | collective-permute-start | bytes 2359304 | tf_op jit(solution)/shard_map/ppermute | solution.py:323
  35.9 0.9 copy-start.1
  37.6 4.3 %copy-start.3 = (bf16[128,3072]{1,0:T(8,128)(2,1)}, bf16[128,3072]{1,0:T(8,128)(2,1)S(1)}, u32[]{:S(2)}) copy-start(bf16[128,3072]{1,0:T(8,128)(2,1)S(1)} %collective-permute-done.2.refs_2_) | copy-start | bytes 2359300
  41.0 0.9 copy-start.4
  42.0 30.4 %copy-start.8 = (f32[1536]{0:T(1024)S(1)}, f32[1536]{0:T(1024)}, u32[]{:S(2)}) copy-start(f32[1536]{0:T(1024)} %param.15) | copy-start | bytes 18436
  42.0 27.5 %collective-permute-start.4 = (bf16[128,3072]{1,0:T(8,128)(2,1)S(1)}, bf16[128,3072]{1,0:T(8,128)(2,1)}, u32[]{:S(2)}, u32[]{:S(2)}) collective-permute-start(bf16[128,3072]{1,0:T(8,128)(2,1)S(1)} %pad_maximum_fusion.1), channel_id=1, source_target_pairs={{0,192},{64,0},{128,64},{192,128},{1,193},{65,1},{129,65},{193,129... | collective-permute-start | bytes 2359304 | tf_op jit(solution)/shard_map/ppermute | solution.py:327
  42.7 27.5 %collective-permute-start.3 = (bf16[128,3072]{1,0:T(8,128)(2,1)S(1)}, bf16[128,3072]{1,0:T(8,128)(2,1)}, u32[]{:S(2)}, u32[]{:S(2)}) collective-permute-start(bf16[128,3072]{1,0:T(8,128)(2,1)S(1)} %pad_maximum_fusion), channel_id=1, source_target_pairs={{0,64},{64,128},{128,192},{192,0},{1,65},{65,129},{129,193},{193,1... | collective-permute-start | bytes 2359304 | tf_op jit(solution)/shard_map/ppermute | solution.py:326
  44.3 23.3 %collective-permute-start.6 = (bf16[64,3072]{1,0:T(8,128)(2,1)S(1)}, bf16[64,3072]{1,0:T(8,128)(2,1)S(1)}, u32[]{:S(2)}, u32[]{:S(2)}) collective-permute-start(bf16[64,3072]{1,0:T(8,128)(2,1)S(1)} %get-tuple-element.12), channel_id=1, source_target_pairs={{0,192},{64,0},{128,64},{192,128},{1,193},{65,1},{129,65},{193,129... | collective-permute-start | bytes 1179656 | tf_op jit(solution)/shard_map/ppermute | solution.py:325
  46.1 23.4 %collective-permute-start.5 = (bf16[64,3072]{1,0:T(8,128)(2,1)S(1)}, bf16[64,3072]{1,0:T(8,128)(2,1)S(1)}, u32[]{:S(2)}, u32[]{:S(2)}) collective-permute-start(bf16[64,3072]{1,0:T(8,128)(2,1)S(1)} %get-tuple-element.13), channel_id=1, source_target_pairs={{0,64},{64,128},{128,192},{192,0},{1,65},{65,129},{129,193},{193,1... | collective-permute-start | bytes 1179656 | tf_op jit(solution)/shard_map/ppermute | solution.py:325
  67.6 1.9 %copy-start.6 = (bf16[64,3072]{1,0:T(8,128)(2,1)}, bf16[64,3072]{1,0:T(8,128)(2,1)S(1)}, u32[]{:S(2)}) copy-start(bf16[64,3072]{1,0:T(8,128)(2,1)S(1)} %collective-permute-done.6.refs_7_) | copy-start | bytes 1179652
  69.5 0.8 copy-start.7
  70.2 13.1 %collective-permute-start.10 = (bf16[1536,1152]{1,0:T(8,128)(2,1)}, bf16[1536,1152]{1,0:T(8,128)(2,1)S(1)}, u32[]{:S(2)}, u32[]{:S(2)}) collective-permute-start(bf16[1536,1152]{1,0:T(8,128)(2,1)} %all-gather.2.cloned.1.call-done.refs_10_), channel_id=1, source_target_pairs={{0,1},{1,0},{2,3},{3,2},{4,5},{5,4},{6,7},{7,6},{8,9},{9,8},{10,11... | collective-permute-start | bytes 10616840 | tf_op jit(solution)/shard_map/ppermute | solution.py:333
  70.3 11.9 %collective-permute-start.8 = (bf16[64,3072]{1,0:T(8,128)(2,1)}, bf16[64,3072]{1,0:T(8,128)(2,1)}, u32[]{:S(2)}, u32[]{:S(2)}) collective-permute-start(bf16[64,3072]{1,0:T(8,128)(2,1)} %copy-done.6), channel_id=1, source_target_pairs={{0,192},{64,0},{128,64},{192,128},{1,193},{65,1},{129,65},{193,129... | collective-permute-start | bytes 1179656 | tf_op jit(solution)/shard_map/ppermute | solution.py:328
  70.6 12.7 %collective-permute-start.7 = (bf16[64,3072]{1,0:T(8,128)(2,1)}, bf16[64,3072]{1,0:T(8,128)(2,1)}, u32[]{:S(2)}, u32[]{:S(2)}) collective-permute-start(bf16[64,3072]{1,0:T(8,128)(2,1)} %copy-done.7), channel_id=1, source_target_pairs={{0,64},{64,128},{128,192},{192,0},{1,65},{65,129},{129,193},{193,1... | collective-permute-start | bytes 1179656 | tf_op jit(solution)/shard_map/ppermute | solution.py:328
  83.3 1.8 %copy-start = (bf16[1536,1152]{1,0:T(8,128)(2,1)}, bf16[1536,1152]{1,0:T(8,128)(2,1)S(1)}, u32[]{:S(2)}) copy-start(bf16[1536,1152]{1,0:T(8,128)(2,1)S(1)} %collective-permute-done.10.refs_11_) | copy-start | bytes 10616836
Sparse Core Ops, SparseCore 0:
  15.9 49.9 all-gather.1

commit v5 on v4

--- a/solution.py
+++ b/solution.py
@@ -70,7 +70,8 @@
                     sems.at[len(WEIGHT_PIECES) + i],
                 )
             )
-        for copy in copies:
+        early = len(WEIGHT_PIECES) + 4
+        for copy in copies[:early]:
             copy.start()
         first = x * 6
         for p in range(PAIRS):
@@ -93,6 +94,8 @@
             rate_bias = jnp.where(lane == j, rate_bias_ref[first + j], rate_bias)
         for copy in copies[: len(WEIGHT_PIECES)]:
             copy.wait()
+        for copy in copies[early:]:
+            copy.start()
         for i in range(4):
             for copy in copies[len(WEIGHT_PIECES) + 4 * i : len(WEIGHT_PIECES) + 4 * i + 4]:
                 copy.wait()

time: 143 us -> 143 us (level)
  no operation moved by 1% of the time
where the time goes in v5:
time: 143 us
  waiting for transfers between devices  56.7 us (40%)
  Pallas kernels  32.3 us (23%)
  blocking collectives  17.3 us (12%)
  starting transfers between devices  14 us (10%)
  between operations  13.5 us (9%)
  local copies, waits for them, and re-layouts  6.92 us (5%)
  other arithmetic  1.87 us (1%)
    pallas_call x1, Pallas kernels, layer(): pl.pallas_call(layer_kernel, out_shape=jax.ShapeDtypeStruct((1024, 384),...  32.3 us
    ppermute x2, waiting for transfers between devices, on_device(): a2, b2 = (lax.ppermute(t0, 'x', up), lax.ppermute(t1, 'x', down))  23.2 us
    all_to_all x1, blocking collectives, on_device(): result = lax.all_to_all(result.reshape(8, 128, 384), SEQ, 0, 0, tiled=True)  17.3 us
    ppermute x1, waiting for transfers between devices, on_device(): theirs = lax.ppermute(sent, 'yh', swap)  14 us
    ppermute x2, waiting for transfers between devices, on_device(): a4, b4 = (lax.ppermute(a2, 'x', up), lax.ppermute(b2, 'x', down))  9.77 us
    ppermute x1, waiting for transfers between devices, on_device(): pair = jnp.concatenate([part, lax.ppermute(part, 'yl', swap)])  5.59 us
    unnamed x18, local copies, waits for them, and re-layouts  4.34 us
    ppermute x2, waiting for transfers between devices, on_device(): a1, b1 = (lax.ppermute(mine, 'x', up), lax.ppermute(mine, 'x', down))  4.13 us
  transfers between devices with their start and end apart: 12, of which 8 were waited for; matrix products, arithmetic and copies ran while one was open for 1% of the time, Pallas kernels for 0%

profile of v5, /device:TPU:96, one launch (start us, length us, event | category | flops | bytes accessed | tf_op | source)
XLA Modules:
  0.0 142.6 jit_solution(1667661030534010650)
XLA Ops:
  6.5 1.1 constant_dynamic-slice_fusion.2
  7.7 1.7 %collective-permute-start.9 = (bf16[96,1152]{1,0:T(8,128)(2,1)S(1)}, bf16[96,1152]{1,0:T(8,128)(2,1)S(1)}, u32[]{:S(2)}, u32[]{:S(2)}) collective-permute-start(bf16[96,1152]{1,0:T(8,128)(2,1)S(1)} %pad_maximum_fusion.4), channel_id=1, source_target_pairs={{0,16},{16,0},{1,17},{17,1},{2,18},{18,2},{3,19},{19,3},{4,20},{20... | collective-permute-start | bytes 663560 | tf_op jit(solution)/shard_map/ppermute | solution.py:333
  9.3 5.6 %collective-permute-done.9 = bf16[96,1152]{1,0:T(8,128)(2,1)S(1)} collective-permute-done((bf16[96,1152]{1,0:T(8,128)(2,1)S(1)}, bf16[96,1152]{1,0:T(8,128)(2,1)S(1)}, u32[]{:S(2)}, u32[]{:S(2)}) %collective-permute-start.9) | collective-permute-done | bytes 221216 | tf_op jit(solution)/shard_map/ppermute | solution.py:333
  14.9 0.8 pad_maximum_fusion.3
  15.8 0.1 dynamic-slice_bitcast_fusion
  15.9 3.3 %collective-permute-start = (bf16[128,3072]{1,0:T(8,128)(2,1)S(1)}, bf16[128,3072]{1,0:T(8,128)(2,1)S(1)}, u32[]{:S(2)}, u32[]{:S(2)}) collective-permute-start(bf16[128,3072]{1,0:T(8,128)(2,1)S(1)} %get-tuple-element.15), channel_id=1, source_target_pairs={{0,32},{32,0},{1,33},{33,1},{2,34},{34,2},{3,35},{35,3},{4,36},{36... | collective-permute-start | bytes 2359304 | tf_op jit(solution)/shard_map/ppermute | solution.py:325
  19.2 2.8 %collective-permute-start.2 = (bf16[128,3072]{1,0:T(8,128)(2,1)S(1)}, bf16[128,3072]{1,0:T(8,128)(2,1)S(1)}, u32[]{:S(2)}, u32[]{:S(2)}) collective-permute-start(bf16[128,3072]{1,0:T(8,128)(2,1)S(1)} %get-tuple-element.16.refs_0_), channel_id=1, source_target_pairs={{0,192},{64,0},{128,64},{192,128},{1,193},{65,1},{129,65},{193,129... | collective-permute-start | bytes 2359304 | tf_op jit(solution)/shard_map/ppermute | solution.py:326
  21.9 14.0 %collective-permute-done.refs_5_ = bf16[128,3072]{1,0:T(8,128)(2,1)S(1)} collective-permute-done((bf16[128,3072]{1,0:T(8,128)(2,1)S(1)}, bf16[128,3072]{1,0:T(8,128)(2,1)S(1)}, u32[]{:S(2)}, u32[]{:S(2)}) %collective-permute-start) | collective-permute-done | bytes 786464 | tf_op jit(solution)/shard_map/ppermute | solution.py:325
  35.9 0.9 copy-done.1
  36.8 0.1 fusion.1
  36.9 0.7 collective-permute-done.2.refs_2_
  37.6 3.4 %collective-permute-done.1.refs_1_ = bf16[128,3072]{1,0:T(8,128)(2,1)S(1)} collective-permute-done((bf16[128,3072]{1,0:T(8,128)(2,1)S(1)}, bf16[128,3072]{1,0:T(8,128)(2,1)S(1)}, u32[]{:S(2)}, u32[]{:S(2)}) %collective-permute-start.1) | collective-permute-done | bytes 786464 | tf_op jit(solution)/shard_map/ppermute | solution.py:326
  41.0 0.9 copy-done.4
  42.0 0.1 pad_maximum_fusion.1
  42.0 0.6 collective-permute-start.4
  42.7 1.5 %collective-permute-start.3 = (bf16[128,3072]{1,0:T(8,128)(2,1)S(1)}, bf16[128,3072]{1,0:T(8,128)(2,1)}, u32[]{:S(2)}, u32[]{:S(2)}) collective-permute-start(bf16[128,3072]{1,0:T(8,128)(2,1)S(1)} %pad_maximum_fusion), channel_id=1, source_target_pairs={{0,64},{64,128},{128,192},{192,0},{1,65},{65,129},{129,193},{193,1... | collective-permute-start | bytes 2359304 | tf_op jit(solution)/shard_map/ppermute | solution.py:329
  44.3 1.8 %collective-permute-start.6 = (bf16[64,3072]{1,0:T(8,128)(2,1)S(1)}, bf16[64,3072]{1,0:T(8,128)(2,1)S(1)}, u32[]{:S(2)}, u32[]{:S(2)}) collective-permute-start(bf16[64,3072]{1,0:T(8,128)(2,1)S(1)} %get-tuple-element.12), channel_id=1, source_target_pairs={{0,192},{64,0},{128,64},{192,128},{1,193},{65,1},{129,65},{193,129... | collective-permute-start | bytes 1179656 | tf_op jit(solution)/shard_map/ppermute | solution.py:328
  46.1 0.2 collective-permute-start.5
  46.3 21.3 %collective-permute-done.6.refs_7_ = bf16[64,3072]{1,0:T(8,128)(2,1)S(1)} collective-permute-done((bf16[64,3072]{1,0:T(8,128)(2,1)S(1)}, bf16[64,3072]{1,0:T(8,128)(2,1)S(1)}, u32[]{:S(2)}, u32[]{:S(2)}) %collective-permute-start.6) | collective-permute-done | bytes 393248 | tf_op jit(solution)/shard_map/ppermute | solution.py:328
  67.6 1.9 %collective-permute-done.5.refs_6_ = bf16[64,3072]{1,0:T(8,128)(2,1)S(1)} collective-permute-done((bf16[64,3072]{1,0:T(8,128)(2,1)S(1)}, bf16[64,3072]{1,0:T(8,128)(2,1)S(1)}, u32[]{:S(2)}, u32[]{:S(2)}) %collective-permute-start.5) | collective-permute-done | bytes 393248 | tf_op jit(solution)/shard_map/ppermute | solution.py:328
  69.5 0.7 copy-done.7
  70.3 0.4 collective-permute-start.8
  70.6 1.7 %collective-permute-start.7 = (bf16[64,3072]{1,0:T(8,128)(2,1)}, bf16[64,3072]{1,0:T(8,128)(2,1)}, u32[]{:S(2)}, u32[]{:S(2)}) collective-permute-start(bf16[64,3072]{1,0:T(8,128)(2,1)} %copy-done.7), channel_id=1, source_target_pairs={{0,64},{64,128},{128,192},{192,0},{1,65},{65,129},{129,193},{193,1... | collective-permute-start | bytes 1179656 | tf_op jit(solution)/shard_map/ppermute | solution.py:331
  72.4 0.6 reshape.15.refs_17_
  73.0 0.6 stack.23.place_ref
  73.6 8.6 %collective-permute-done.8.refs_9_ = bf16[64,3072]{1,0:T(8,128)(2,1)} collective-permute-done((bf16[64,3072]{1,0:T(8,128)(2,1)}, bf16[64,3072]{1,0:T(8,128)(2,1)}, u32[]{:S(2)}, u32[]{:S(2)}) %collective-permute-start.8) | collective-permute-done | bytes 393248 | tf_op jit(solution)/shard_map/ppermute | solution.py:331
  82.1 1.2 collective-permute-done.7.refs_8_
  83.3 1.8 %copy-done = bf16[1536,1152]{1,0:T(8,128)(2,1)} copy-done((bf16[1536,1152]{1,0:T(8,128)(2,1)}, bf16[1536,1152]{1,0:T(8,128)(2,1)S(1)}, u32[]{:S(2)}) %copy-start) | copy-done | bytes 3538968
  85.1 32.3 %layer.1 = bf16[1024,384]{1,0:T(8,128)(2,1)} custom-call(s32[5]{0:T(128)} %stack.23.place_ref, bf16[128,3072]{1,0:T(8,128)(2,1)} %copy-done.2, bf16[128,3072]{1,0:T(8,128)(2,1)} %copy-done.4, bf16[128,3072]{1,0:T(8,128)(2,1)} %copy-done.3, bf16[128,3072]{1,0:T(8,128)(2,1)} %collective-permute-done.3.refs_3_, ...), custom_call_target="tpu_custom_call" | custom-call | tf_op jit(solution)/shard_map/layer/pallas_call | solution.py:250
  117.4 17.3 %all_to_all.5 = bf16[8,128,384]{2,1,0:T(8,128)(2,1)S(1)} all-to-all(bf16[8,128,384]{2,1,0:T(8,128)(2,1)} %bitcast.11), channel_id=1, replica_groups=mesh['x'=4,'yh'=2,'yl'=2,'z'=8,'c'=2] {'x','yh'}, dimensions={0} | all-to-all | bytes 1572864 | tf_op jit(solution)/shard_map/all_to_all | solution.py:342
  134.7 0.1 fusion
  134.8 0.9 pad_maximum_fusion.2
  (26 shorter events, 0.2 us)
Async XLA Ops:
  6.5 9.2 %copy-start.5 = (bf16[2,128,3072]{2,1,0:T(8,128)(2,1)S(1)}, bf16[2,128,3072]{2,1,0:T(8,128)(2,1)}, u32[]{:S(2)}) copy-start(bf16[2,128,3072]{2,1,0:T(8,128)(2,1)} %param.8) | copy-start | bytes 4718596
  6.5 63.7 %all-gather.2.cloned.1.call-start = ((), (), s32[]{:S(2)}) async-start(), calls=%async_computation.1 | async-start | bytes 3981312 | tf_op jit(solution)/shard_map/all_gather | solution.py:334
  7.7 7.3 %collective-permute-start.9 = (bf16[96,1152]{1,0:T(8,128)(2,1)S(1)}, bf16[96,1152]{1,0:T(8,128)(2,1)S(1)}, u32[]{:S(2)}, u32[]{:S(2)}) collective-permute-start(bf16[96,1152]{1,0:T(8,128)(2,1)S(1)} %pad_maximum_fusion.4), channel_id=1, source_target_pairs={{0,16},{16,0},{1,17},{17,1},{2,18},{18,2},{3,19},{19,3},{4,20},{20... | collective-permute-start | bytes 663560 | tf_op jit(solution)/shard_map/ppermute | solution.py:333
  15.9 21.0 %copy-start.2 = (bf16[128,3072]{1,0:T(8,128)(2,1)}, bf16[128,3072]{1,0:T(8,128)(2,1)S(1)}, u32[]{:S(2)}) copy-start(bf16[128,3072]{1,0:T(8,128)(2,1)S(1)} %get-tuple-element.16.refs_0_) | copy-start | bytes 2359300
  15.9 20.0 %collective-permute-start = (bf16[128,3072]{1,0:T(8,128)(2,1)S(1)}, bf16[128,3072]{1,0:T(8,128)(2,1)S(1)}, u32[]{:S(2)}, u32[]{:S(2)}) collective-permute-start(bf16[128,3072]{1,0:T(8,128)(2,1)S(1)} %get-tuple-element.15), channel_id=1, source_target_pairs={{0,32},{32,0},{1,33},{33,1},{2,34},{34,2},{3,35},{35,3},{4,36},{36... | collective-permute-start | bytes 2359304 | tf_op jit(solution)/shard_map/ppermute | solution.py:325
  19.2 18.4 %collective-permute-start.2 = (bf16[128,3072]{1,0:T(8,128)(2,1)S(1)}, bf16[128,3072]{1,0:T(8,128)(2,1)S(1)}, u32[]{:S(2)}, u32[]{:S(2)}) collective-permute-start(bf16[128,3072]{1,0:T(8,128)(2,1)S(1)} %get-tuple-element.16.refs_0_), channel_id=1, source_target_pairs={{0,192},{64,0},{128,64},{192,128},{1,193},{65,1},{129,65},{193,129... | collective-permute-start | bytes 2359304 | tf_op jit(solution)/shard_map/ppermute | solution.py:326
  21.9 19.1 %collective-permute-start.1 = (bf16[128,3072]{1,0:T(8,128)(2,1)S(1)}, bf16[128,3072]{1,0:T(8,128)(2,1)S(1)}, u32[]{:S(2)}, u32[]{:S(2)}) collective-permute-start(bf16[128,3072]{1,0:T(8,128)(2,1)S(1)} %get-tuple-element.16.refs_0_), channel_id=1, source_target_pairs={{0,64},{64,128},{128,192},{192,0},{1,65},{65,129},{129,193},{193,1... | collective-permute-start | bytes 2359304 | tf_op jit(solution)/shard_map/ppermute | solution.py:326
  35.9 0.9 copy-start.1
  37.6 4.3 %copy-start.3 = (bf16[128,3072]{1,0:T(8,128)(2,1)}, bf16[128,3072]{1,0:T(8,128)(2,1)S(1)}, u32[]{:S(2)}) copy-start(bf16[128,3072]{1,0:T(8,128)(2,1)S(1)} %collective-permute-done.2.refs_2_) | copy-start | bytes 2359300
  41.0 0.9 copy-start.4
  42.0 30.4 %copy-start.8 = (f32[1536]{0:T(1024)S(1)}, f32[1536]{0:T(1024)}, u32[]{:S(2)}) copy-start(f32[1536]{0:T(1024)} %param.15) | copy-start | bytes 18436
  42.0 27.5 %collective-permute-start.4 = (bf16[128,3072]{1,0:T(8,128)(2,1)S(1)}, bf16[128,3072]{1,0:T(8,128)(2,1)}, u32[]{:S(2)}, u32[]{:S(2)}) collective-permute-start(bf16[128,3072]{1,0:T(8,128)(2,1)S(1)} %pad_maximum_fusion.1), channel_id=1, source_target_pairs={{0,192},{64,0},{128,64},{192,128},{1,193},{65,1},{129,65},{193,129... | collective-permute-start | bytes 2359304 | tf_op jit(solution)/shard_map/ppermute | solution.py:330
  42.7 27.5 %collective-permute-start.3 = (bf16[128,3072]{1,0:T(8,128)(2,1)S(1)}, bf16[128,3072]{1,0:T(8,128)(2,1)}, u32[]{:S(2)}, u32[]{:S(2)}) collective-permute-start(bf16[128,3072]{1,0:T(8,128)(2,1)S(1)} %pad_maximum_fusion), channel_id=1, source_target_pairs={{0,64},{64,128},{128,192},{192,0},{1,65},{65,129},{129,193},{193,1... | collective-permute-start | bytes 2359304 | tf_op jit(solution)/shard_map/ppermute | solution.py:329
  44.3 23.3 %collective-permute-start.6 = (bf16[64,3072]{1,0:T(8,128)(2,1)S(1)}, bf16[64,3072]{1,0:T(8,128)(2,1)S(1)}, u32[]{:S(2)}, u32[]{:S(2)}) collective-permute-start(bf16[64,3072]{1,0:T(8,128)(2,1)S(1)} %get-tuple-element.12), channel_id=1, source_target_pairs={{0,192},{64,0},{128,64},{192,128},{1,193},{65,1},{129,65},{193,129... | collective-permute-start | bytes 1179656 | tf_op jit(solution)/shard_map/ppermute | solution.py:328
  46.1 23.4 %collective-permute-start.5 = (bf16[64,3072]{1,0:T(8,128)(2,1)S(1)}, bf16[64,3072]{1,0:T(8,128)(2,1)S(1)}, u32[]{:S(2)}, u32[]{:S(2)}) collective-permute-start(bf16[64,3072]{1,0:T(8,128)(2,1)S(1)} %get-tuple-element.13), channel_id=1, source_target_pairs={{0,64},{64,128},{128,192},{192,0},{1,65},{65,129},{129,193},{193,1... | collective-permute-start | bytes 1179656 | tf_op jit(solution)/shard_map/ppermute | solution.py:328
  67.6 1.9 %copy-start.6 = (bf16[64,3072]{1,0:T(8,128)(2,1)}, bf16[64,3072]{1,0:T(8,128)(2,1)S(1)}, u32[]{:S(2)}) copy-start(bf16[64,3072]{1,0:T(8,128)(2,1)S(1)} %collective-permute-done.6.refs_7_) | copy-start | bytes 1179652
  69.5 0.8 copy-start.7
  70.2 13.1 %collective-permute-start.10 = (bf16[1536,1152]{1,0:T(8,128)(2,1)}, bf16[1536,1152]{1,0:T(8,128)(2,1)S(1)}, u32[]{:S(2)}, u32[]{:S(2)}) collective-permute-start(bf16[1536,1152]{1,0:T(8,128)(2,1)} %all-gather.2.cloned.1.call-done.refs_10_), channel_id=1, source_target_pairs={{0,1},{1,0},{2,3},{3,2},{4,5},{5,4},{6,7},{7,6},{8,9},{9,8},{10,11... | collective-permute-start | bytes 10616840 | tf_op jit(solution)/shard_map/ppermute | solution.py:336
  70.3 11.9 %collective-permute-start.8 = (bf16[64,3072]{1,0:T(8,128)(2,1)}, bf16[64,3072]{1,0:T(8,128)(2,1)}, u32[]{:S(2)}, u32[]{:S(2)}) collective-permute-start(bf16[64,3072]{1,0:T(8,128)(2,1)} %copy-done.6), channel_id=1, source_target_pairs={{0,192},{64,0},{128,64},{192,128},{1,193},{65,1},{129,65},{193,129... | collective-permute-start | bytes 1179656 | tf_op jit(solution)/shard_map/ppermute | solution.py:331
  70.6 12.7 %collective-permute-start.7 = (bf16[64,3072]{1,0:T(8,128)(2,1)}, bf16[64,3072]{1,0:T(8,128)(2,1)}, u32[]{:S(2)}, u32[]{:S(2)}) collective-permute-start(bf16[64,3072]{1,0:T(8,128)(2,1)} %copy-done.7), channel_id=1, source_target_pairs={{0,64},{64,128},{128,192},{192,0},{1,65},{65,129},{129,193},{193,1... | collective-permute-start | bytes 1179656 | tf_op jit(solution)/shard_map/ppermute | solution.py:331
  83.3 1.8 %copy-start = (bf16[1536,1152]{1,0:T(8,128)(2,1)}, bf16[1536,1152]{1,0:T(8,128)(2,1)S(1)}, u32[]{:S(2)}) copy-start(bf16[1536,1152]{1,0:T(8,128)(2,1)S(1)} %collective-permute-done.10.refs_11_) | copy-start | bytes 10616836
Sparse Core Ops, SparseCore 0:
  15.9 49.9 all-gather.1

commit v6 on v4

--- a/solution.py
+++ b/solution.py
@@ -323,8 +323,9 @@
     a1, b1 = lax.ppermute(mine, "x", up), lax.ppermute(mine, "x", down)
     t0, t1, a1, b1 = lax.optimization_barrier((theirs[:64], theirs[64:], a1, b1))
     a2, b2 = lax.ppermute(t0, "x", up), lax.ppermute(t1, "x", down)
-    a3 = lax.ppermute(jnp.concatenate([a1[:64], t1]), "x", up)
-    b3 = lax.ppermute(jnp.concatenate([b1[64:], t0]), "x", down)
+    a3, b3 = jnp.concatenate([a1[:64], t1]), jnp.concatenate([b1[64:], t0])
+    a3, b3, a2, b2 = lax.optimization_barrier((a3, b3, a2, b2))
+    a3, b3 = lax.ppermute(a3, "x", up), lax.ppermute(b3, "x", down)
     a4, b4 = lax.ppermute(a2, "x", up), lax.ppermute(b2, "x", down)
     tokens = [mine, a1, b1, a3, b3, theirs, a2, b2, a4, b4]
     pair = jnp.concatenate([part, lax.ppermute(part, "yl", swap)])

time: 143 us -> 143 us (level)
  starting transfers between devices: 14 us -> 16.4 us
  waiting for transfers between devices: 56.7 us -> 54.4 us
  blocking collectives: 17.3 us -> 19.3 us
  local copies, waits for them, and re-layouts: 6.92 us -> 5.38 us
    ppermute x2, waiting for transfers between devices: 23.2 us -> 7.94 us  [on_device(): a2, b2 = (lax.ppermute(t0, 'x', up), lax.ppermute(t1, 'x', down))]
    ppermute x2, waiting for transfers between devices: 0.01 us -> 14.3 us  [on_device(): a3, b3 = (lax.ppermute(a3, 'x', up), lax.ppermute(b3, 'x', down))]
    all_to_all x1, blocking collectives: 17.3 us -> 19.3 us  [on_device(): result = lax.all_to_all(result.reshape(8, 128, 384), SEQ, 0, 0, tiled=True)]
    unnamed x18, local copies, waits for them, and re-layouts: 4.34 us -> 2.71 us
where the time goes in v6:
time: 143 us
  waiting for transfers between devices  54.4 us (38%)
  Pallas kernels  32.3 us (23%)
  blocking collectives  19.3 us (13%)
  starting transfers between devices  16.4 us (11%)
  between operations  13.5 us (9%)
  local copies, waits for them, and re-layouts  5.38 us (4%)
  other arithmetic  1.87 us (1%)
    pallas_call x1, Pallas kernels, layer(): pl.pallas_call(layer_kernel, out_shape=jax.ShapeDtypeStruct((1024, 384),...  32.3 us
    all_to_all x1, blocking collectives, on_device(): result = lax.all_to_all(result.reshape(8, 128, 384), SEQ, 0, 0, tiled=True)  19.3 us
    ppermute x2, waiting for transfers between devices, on_device(): a3, b3 = (lax.ppermute(a3, 'x', up), lax.ppermute(b3, 'x', down))  14.3 us
    ppermute x1, waiting for transfers between devices, on_device(): theirs = lax.ppermute(sent, 'yh', swap)  14 us
    ppermute x2, waiting for transfers between devices, on_device(): a4, b4 = (lax.ppermute(a2, 'x', up), lax.ppermute(b2, 'x', down))  8.46 us
    ppermute x2, waiting for transfers between devices, on_device(): a2, b2 = (lax.ppermute(t0, 'x', up), lax.ppermute(t1, 'x', down))  7.94 us
    ppermute x1, waiting for transfers between devices, on_device(): pair = jnp.concatenate([part, lax.ppermute(part, 'yl', swap)])  5.59 us
    ppermute x2, waiting for transfers between devices, on_device(): a1, b1 = (lax.ppermute(mine, 'x', up), lax.ppermute(mine, 'x', down))  4.14 us
  transfers between devices with their start and end apart: 12, of which 8 were waited for; matrix products, arithmetic and copies ran while one was open for 1% of the time, Pallas kernels for 0%

profile of v6, /device:TPU:96, one launch (start us, length us, event | category | flops | bytes accessed | tf_op | source)
XLA Modules:
  0.0 143.2 jit_solution(13475799971631789401)
XLA Ops:
  6.5 1.1 constant_dynamic-slice_fusion.2
  7.7 1.7 %collective-permute-start.9 = (bf16[96,1152]{1,0:T(8,128)(2,1)S(1)}, bf16[96,1152]{1,0:T(8,128)(2,1)S(1)}, u32[]{:S(2)}, u32[]{:S(2)}) collective-permute-start(bf16[96,1152]{1,0:T(8,128)(2,1)S(1)} %pad_maximum_fusion.4), channel_id=1, source_target_pairs={{0,16},{16,0},{1,17},{17,1},{2,18},{18,2},{3,19},{19,3},{4,20},{20... | collective-permute-start | bytes 663560 | tf_op jit(solution)/shard_map/ppermute | solution.py:331
  9.3 5.6 %collective-permute-done.9 = bf16[96,1152]{1,0:T(8,128)(2,1)S(1)} collective-permute-done((bf16[96,1152]{1,0:T(8,128)(2,1)S(1)}, bf16[96,1152]{1,0:T(8,128)(2,1)S(1)}, u32[]{:S(2)}, u32[]{:S(2)}) %collective-permute-start.9) | collective-permute-done | bytes 221216 | tf_op jit(solution)/shard_map/ppermute | solution.py:331
  14.9 0.8 pad_maximum_fusion.3
  15.8 0.1 dynamic-slice_bitcast_fusion
  15.9 3.3 %collective-permute-start = (bf16[128,3072]{1,0:T(8,128)(2,1)S(1)}, bf16[128,3072]{1,0:T(8,128)(2,1)S(1)}, u32[]{:S(2)}, u32[]{:S(2)}) collective-permute-start(bf16[128,3072]{1,0:T(8,128)(2,1)S(1)} %get-tuple-element.23), channel_id=1, source_target_pairs={{0,32},{32,0},{1,33},{33,1},{2,34},{34,2},{3,35},{35,3},{4,36},{36... | collective-permute-start | bytes 2359304 | tf_op jit(solution)/shard_map/ppermute | solution.py:322
  19.2 2.8 %collective-permute-start.2 = (bf16[128,3072]{1,0:T(8,128)(2,1)S(1)}, bf16[128,3072]{1,0:T(8,128)(2,1)S(1)}, u32[]{:S(2)}, u32[]{:S(2)}) collective-permute-start(bf16[128,3072]{1,0:T(8,128)(2,1)S(1)} %get-tuple-element.24.refs_0_), channel_id=1, source_target_pairs={{0,192},{64,0},{128,64},{192,128},{1,193},{65,1},{129,65},{193,129... | collective-permute-start | bytes 2359304 | tf_op jit(solution)/shard_map/ppermute | solution.py:323
  21.9 14.0 %collective-permute-done.refs_5_ = bf16[128,3072]{1,0:T(8,128)(2,1)S(1)} collective-permute-done((bf16[128,3072]{1,0:T(8,128)(2,1)S(1)}, bf16[128,3072]{1,0:T(8,128)(2,1)S(1)}, u32[]{:S(2)}, u32[]{:S(2)}) %collective-permute-start) | collective-permute-done | bytes 786464 | tf_op jit(solution)/shard_map/ppermute | solution.py:322
  35.9 0.9 copy-done.1
  36.8 0.1 fusion.1
  36.9 0.7 collective-permute-done.2.refs_2_
  37.6 3.4 %collective-permute-done.1.refs_1_ = bf16[128,3072]{1,0:T(8,128)(2,1)S(1)} collective-permute-done((bf16[128,3072]{1,0:T(8,128)(2,1)S(1)}, bf16[128,3072]{1,0:T(8,128)(2,1)S(1)}, u32[]{:S(2)}, u32[]{:S(2)}) %collective-permute-start.1) | collective-permute-done | bytes 786464 | tf_op jit(solution)/shard_map/ppermute | solution.py:323
  41.0 0.4 collective-permute-start.4
  41.4 1.7 %collective-permute-start.3 = (bf16[64,3072]{1,0:T(8,128)(2,1)S(1)}, bf16[64,3072]{1,0:T(8,128)(2,1)S(1)}, u32[]{:S(2)}, u32[]{:S(2)}) collective-permute-start(bf16[64,3072]{1,0:T(8,128)(2,1)S(1)} %get-tuple-element.17), channel_id=1, source_target_pairs={{0,64},{64,128},{128,192},{192,0},{1,65},{65,129},{129,193},{193,1... | collective-permute-start | bytes 1179656 | tf_op jit(solution)/shard_map/ppermute | solution.py:325
  43.1 0.1 pad_maximum_fusion
  43.2 6.4 %collective-permute-done.4.refs_7_ = bf16[64,3072]{1,0:T(8,128)(2,1)S(1)} collective-permute-done((bf16[64,3072]{1,0:T(8,128)(2,1)S(1)}, bf16[64,3072]{1,0:T(8,128)(2,1)S(1)}, u32[]{:S(2)}, u32[]{:S(2)}) %collective-permute-start.4) | collective-permute-done | bytes 393248 | tf_op jit(solution)/shard_map/ppermute | solution.py:325
  49.6 1.6 %collective-permute-done.3.refs_6_ = bf16[64,3072]{1,0:T(8,128)(2,1)S(1)} collective-permute-done((bf16[64,3072]{1,0:T(8,128)(2,1)S(1)}, bf16[64,3072]{1,0:T(8,128)(2,1)S(1)}, u32[]{:S(2)}, u32[]{:S(2)}) %collective-permute-start.3) | collective-permute-done | bytes 393248 | tf_op jit(solution)/shard_map/ppermute | solution.py:325
  51.2 0.6 collective-permute-start.5
  51.8 2.6 %collective-permute-start.6 = (bf16[128,3072]{1,0:T(8,128)(2,1)S(1)}, bf16[128,3072]{1,0:T(8,128)(2,1)}, u32[]{:S(2)}, u32[]{:S(2)}) collective-permute-start(bf16[128,3072]{1,0:T(8,128)(2,1)S(1)} %get-tuple-element.19), channel_id=1, source_target_pairs={{0,192},{64,0},{128,64},{192,128},{1,193},{65,1},{129,65},{193,129... | collective-permute-start | bytes 2359304 | tf_op jit(solution)/shard_map/ppermute | solution.py:328
  54.4 14.3 %collective-permute-done.5.refs_3_ = bf16[128,3072]{1,0:T(8,128)(2,1)} collective-permute-done((bf16[128,3072]{1,0:T(8,128)(2,1)S(1)}, bf16[128,3072]{1,0:T(8,128)(2,1)}, u32[]{:S(2)}, u32[]{:S(2)}) %collective-permute-start.5) | collective-permute-done | bytes 786464 | tf_op jit(solution)/shard_map/ppermute | solution.py:328
  68.7 0.0 all-gather.2.cloned.1.call-done.refs_10_
  68.7 0.1 collective-permute-start.10
  68.8 0.1 collective-permute-start.7
  68.9 3.2 %collective-permute-start.8 = (bf16[64,3072]{1,0:T(8,128)(2,1)}, bf16[64,3072]{1,0:T(8,128)(2,1)}, u32[]{:S(2)}, u32[]{:S(2)}) collective-permute-start(bf16[64,3072]{1,0:T(8,128)(2,1)} %copy-done.6), channel_id=1, source_target_pairs={{0,192},{64,0},{128,64},{192,128},{1,193},{65,1},{129,65},{193,129... | collective-permute-start | bytes 1179656 | tf_op jit(solution)/shard_map/ppermute | solution.py:329
  72.2 0.6 reshape.15.refs_17_
  72.8 0.7 stack.23.place_ref
  73.4 8.5 %collective-permute-done.7.refs_8_ = bf16[64,3072]{1,0:T(8,128)(2,1)} collective-permute-done((bf16[64,3072]{1,0:T(8,128)(2,1)}, bf16[64,3072]{1,0:T(8,128)(2,1)}, u32[]{:S(2)}, u32[]{:S(2)}) %collective-permute-start.7) | collective-permute-done | bytes 393248 | tf_op jit(solution)/shard_map/ppermute | solution.py:329
  81.9 1.8 %copy-done = bf16[1536,1152]{1,0:T(8,128)(2,1)} copy-done((bf16[1536,1152]{1,0:T(8,128)(2,1)}, bf16[1536,1152]{1,0:T(8,128)(2,1)S(1)}, u32[]{:S(2)}) %copy-start) | copy-done | bytes 3538968
  83.7 32.3 %layer.1 = bf16[1024,384]{1,0:T(8,128)(2,1)} custom-call(s32[5]{0:T(128)} %stack.23.place_ref, bf16[128,3072]{1,0:T(8,128)(2,1)} %copy-done.2, bf16[128,3072]{1,0:T(8,128)(2,1)} %copy-done.4, bf16[128,3072]{1,0:T(8,128)(2,1)} %copy-done.3, bf16[128,3072]{1,0:T(8,128)(2,1)} %collective-permute-done.5.refs_3_, ...), custom_call_target="tpu_custom_call" | custom-call | tf_op jit(solution)/shard_map/layer/pallas_call | solution.py:247
  116.0 19.3 %all_to_all.5 = bf16[8,128,384]{2,1,0:T(8,128)(2,1)S(1)} all-to-all(bf16[8,128,384]{2,1,0:T(8,128)(2,1)} %bitcast.11), channel_id=1, replica_groups=mesh['x'=4,'yh'=2,'yl'=2,'z'=8,'c'=2] {'x','yh'}, dimensions={0} | all-to-all | bytes 1572864 | tf_op jit(solution)/shard_map/all_to_all | solution.py:340
  135.3 0.1 fusion
  135.4 0.9 pad_maximum_fusion.2
  (25 shorter events, 0.1 us)
Async XLA Ops:
  6.5 9.2 %copy-start.5 = (bf16[2,128,3072]{2,1,0:T(8,128)(2,1)S(1)}, bf16[2,128,3072]{2,1,0:T(8,128)(2,1)}, u32[]{:S(2)}) copy-start(bf16[2,128,3072]{2,1,0:T(8,128)(2,1)} %param.8) | copy-start | bytes 4718596
  6.5 62.2 %all-gather.2.cloned.1.call-start = ((), (), s32[]{:S(2)}) async-start(), calls=%async_computation.1 | async-start | bytes 3981312 | tf_op jit(solution)/shard_map/all_gather | solution.py:332
  7.7 7.3 %collective-permute-start.9 = (bf16[96,1152]{1,0:T(8,128)(2,1)S(1)}, bf16[96,1152]{1,0:T(8,128)(2,1)S(1)}, u32[]{:S(2)}, u32[]{:S(2)}) collective-permute-start(bf16[96,1152]{1,0:T(8,128)(2,1)S(1)} %pad_maximum_fusion.4), channel_id=1, source_target_pairs={{0,16},{16,0},{1,17},{17,1},{2,18},{18,2},{3,19},{19,3},{4,20},{20... | collective-permute-start | bytes 663560 | tf_op jit(solution)/shard_map/ppermute | solution.py:331
  15.9 21.0 %copy-start.2 = (bf16[128,3072]{1,0:T(8,128)(2,1)}, bf16[128,3072]{1,0:T(8,128)(2,1)S(1)}, u32[]{:S(2)}) copy-start(bf16[128,3072]{1,0:T(8,128)(2,1)S(1)} %get-tuple-element.24.refs_0_) | copy-start | bytes 2359300
  15.9 20.0 %collective-permute-start = (bf16[128,3072]{1,0:T(8,128)(2,1)S(1)}, bf16[128,3072]{1,0:T(8,128)(2,1)S(1)}, u32[]{:S(2)}, u32[]{:S(2)}) collective-permute-start(bf16[128,3072]{1,0:T(8,128)(2,1)S(1)} %get-tuple-element.23), channel_id=1, source_target_pairs={{0,32},{32,0},{1,33},{33,1},{2,34},{34,2},{3,35},{35,3},{4,36},{36... | collective-permute-start | bytes 2359304 | tf_op jit(solution)/shard_map/ppermute | solution.py:322
  19.2 18.4 %collective-permute-start.2 = (bf16[128,3072]{1,0:T(8,128)(2,1)S(1)}, bf16[128,3072]{1,0:T(8,128)(2,1)S(1)}, u32[]{:S(2)}, u32[]{:S(2)}) collective-permute-start(bf16[128,3072]{1,0:T(8,128)(2,1)S(1)} %get-tuple-element.24.refs_0_), channel_id=1, source_target_pairs={{0,192},{64,0},{128,64},{192,128},{1,193},{65,1},{129,65},{193,129... | collective-permute-start | bytes 2359304 | tf_op jit(solution)/shard_map/ppermute | solution.py:323
  21.9 19.1 %collective-permute-start.1 = (bf16[128,3072]{1,0:T(8,128)(2,1)S(1)}, bf16[128,3072]{1,0:T(8,128)(2,1)S(1)}, u32[]{:S(2)}, u32[]{:S(2)}) collective-permute-start(bf16[128,3072]{1,0:T(8,128)(2,1)S(1)} %get-tuple-element.24.refs_0_), channel_id=1, source_target_pairs={{0,64},{64,128},{128,192},{192,0},{1,65},{65,129},{129,193},{193,1... | collective-permute-start | bytes 2359304 | tf_op jit(solution)/shard_map/ppermute | solution.py:323
  35.9 0.9 copy-start.1
  37.6 5.5 %copy-start.3 = (bf16[128,3072]{1,0:T(8,128)(2,1)}, bf16[128,3072]{1,0:T(8,128)(2,1)S(1)}, u32[]{:S(2)}) copy-start(bf16[128,3072]{1,0:T(8,128)(2,1)S(1)} %collective-permute-done.2.refs_2_) | copy-start | bytes 2359300
  41.0 2.0 %copy-start.4 = (bf16[128,3072]{1,0:T(8,128)(2,1)}, bf16[128,3072]{1,0:T(8,128)(2,1)S(1)}, u32[]{:S(2)}) copy-start(bf16[128,3072]{1,0:T(8,128)(2,1)S(1)} %collective-permute-done.1.refs_1_) | copy-start | bytes 2359300
  41.0 8.6 %collective-permute-start.4 = (bf16[64,3072]{1,0:T(8,128)(2,1)S(1)}, bf16[64,3072]{1,0:T(8,128)(2,1)S(1)}, u32[]{:S(2)}, u32[]{:S(2)}) collective-permute-start(bf16[64,3072]{1,0:T(8,128)(2,1)S(1)} %get-tuple-element.16), channel_id=1, source_target_pairs={{0,192},{64,0},{128,64},{192,128},{1,193},{65,1},{129,65},{193,129... | collective-permute-start | bytes 1179656 | tf_op jit(solution)/shard_map/ppermute | solution.py:325
  41.4 9.8 %collective-permute-start.3 = (bf16[64,3072]{1,0:T(8,128)(2,1)S(1)}, bf16[64,3072]{1,0:T(8,128)(2,1)S(1)}, u32[]{:S(2)}, u32[]{:S(2)}) collective-permute-start(bf16[64,3072]{1,0:T(8,128)(2,1)S(1)} %get-tuple-element.17), channel_id=1, source_target_pairs={{0,64},{64,128},{128,192},{192,0},{1,65},{65,129},{129,193},{193,1... | collective-permute-start | bytes 1179656 | tf_op jit(solution)/shard_map/ppermute | solution.py:325
  43.1 29.1 %copy-start.8 = (f32[1536]{0:T(1024)S(1)}, f32[1536]{0:T(1024)}, u32[]{:S(2)}) copy-start(f32[1536]{0:T(1024)} %param.15) | copy-start | bytes 18436
  49.6 19.1 %copy-start.6 = (bf16[64,3072]{1,0:T(8,128)(2,1)}, bf16[64,3072]{1,0:T(8,128)(2,1)S(1)}, u32[]{:S(2)}) copy-start(bf16[64,3072]{1,0:T(8,128)(2,1)S(1)} %collective-permute-done.4.refs_7_) | copy-start | bytes 1179652
  51.2 17.5 %copy-start.7 = (bf16[64,3072]{1,0:T(8,128)(2,1)}, bf16[64,3072]{1,0:T(8,128)(2,1)S(1)}, u32[]{:S(2)}) copy-start(bf16[64,3072]{1,0:T(8,128)(2,1)S(1)} %collective-permute-done.3.refs_6_) | copy-start | bytes 1179652
  51.2 17.5 %collective-permute-start.5 = (bf16[128,3072]{1,0:T(8,128)(2,1)S(1)}, bf16[128,3072]{1,0:T(8,128)(2,1)}, u32[]{:S(2)}, u32[]{:S(2)}) collective-permute-start(bf16[128,3072]{1,0:T(8,128)(2,1)S(1)} %get-tuple-element.18), channel_id=1, source_target_pairs={{0,64},{64,128},{128,192},{192,0},{1,65},{65,129},{129,193},{193,1... | collective-permute-start | bytes 2359304 | tf_op jit(solution)/shard_map/ppermute | solution.py:328
  51.8 16.9 %collective-permute-start.6 = (bf16[128,3072]{1,0:T(8,128)(2,1)S(1)}, bf16[128,3072]{1,0:T(8,128)(2,1)}, u32[]{:S(2)}, u32[]{:S(2)}) collective-permute-start(bf16[128,3072]{1,0:T(8,128)(2,1)S(1)} %get-tuple-element.19), channel_id=1, source_target_pairs={{0,192},{64,0},{128,64},{192,128},{1,193},{65,1},{129,65},{193,129... | collective-permute-start | bytes 2359304 | tf_op jit(solution)/shard_map/ppermute | solution.py:328
  68.7 13.2 %collective-permute-start.10 = (bf16[1536,1152]{1,0:T(8,128)(2,1)}, bf16[1536,1152]{1,0:T(8,128)(2,1)S(1)}, u32[]{:S(2)}, u32[]{:S(2)}) collective-permute-start(bf16[1536,1152]{1,0:T(8,128)(2,1)} %all-gather.2.cloned.1.call-done.refs_10_), channel_id=1, source_target_pairs={{0,1},{1,0},{2,3},{3,2},{4,5},{5,4},{6,7},{7,6},{8,9},{9,8},{10,11... | collective-permute-start | bytes 10616840 | tf_op jit(solution)/shard_map/ppermute | solution.py:334
  68.8 13.1 %collective-permute-start.7 = (bf16[64,3072]{1,0:T(8,128)(2,1)}, bf16[64,3072]{1,0:T(8,128)(2,1)}, u32[]{:S(2)}, u32[]{:S(2)}) collective-permute-start(bf16[64,3072]{1,0:T(8,128)(2,1)} %copy-done.7), channel_id=1, source_target_pairs={{0,64},{64,128},{128,192},{192,0},{1,65},{65,129},{129,193},{193,1... | collective-permute-start | bytes 1179656 | tf_op jit(solution)/shard_map/ppermute | solution.py:329
  68.9 13.0 %collective-permute-start.8 = (bf16[64,3072]{1,0:T(8,128)(2,1)}, bf16[64,3072]{1,0:T(8,128)(2,1)}, u32[]{:S(2)}, u32[]{:S(2)}) collective-permute-start(bf16[64,3072]{1,0:T(8,128)(2,1)} %copy-done.6), channel_id=1, source_target_pairs={{0,192},{64,0},{128,64},{192,128},{1,193},{65,1},{129,65},{193,129... | collective-permute-start | bytes 1179656 | tf_op jit(solution)/shard_map/ppermute | solution.py:329
  81.9 1.8 %copy-start = (bf16[1536,1152]{1,0:T(8,128)(2,1)}, bf16[1536,1152]{1,0:T(8,128)(2,1)S(1)}, u32[]{:S(2)}) copy-start(bf16[1536,1152]{1,0:T(8,128)(2,1)S(1)} %collective-permute-done.10.refs_11_) | copy-start | bytes 10616836
Sparse Core Ops, SparseCore 0:
  15.9 49.9 all-gather.1
